TPU v7x, 32 devices: a whole 2x2x4 slice. The times are simulated.
32 devices in a mesh: seq: 4 (over y, x), wt: 8 (over z, core).
Axes of the slice: x: 2, y: 2, z: 4, core: 2. Of those that a mesh axis runs over, the one named last changes fastest.
Arguments:
- tokens: bfloat16 [24576, 768], P(('wt', 'seq')), may hold values from -6 to 6
- output_cotangent: bfloat16 [24576, 768], P(('wt', 'seq')), may hold values from -6 to 6
- attention_weight: bfloat16 [768, 2304], P('wt'), may hold values from -0.21875 to 0.21875
- query_bias: bfloat16 [768], replicated, may hold values from -3 to 3
- value_bias: bfloat16 [768], replicated, may hold values from -3 to 3
- output_weight: bfloat16 [768, 768], P('wt'), may hold values from -6 to 6
- output_bias: bfloat16 [768], replicated, may hold values from -3 to 3
- first_gain: bfloat16 [768], replicated, may hold values from 0.5 to 1.5
- first_shift: bfloat16 [768], replicated, may hold values from -3 to 3
- expand_weight: bfloat16 [768, 3072], P('wt'), may hold values from -0.21875 to 0.21875
- expand_bias: bfloat16 [3072], replicated, may hold values from -3 to 3
- contract_weight: bfloat16 [3072, 768], P('wt'), may hold values from -0.109375 to 0.109375
- contract_bias: bfloat16 [768], replicated, may hold values from -3 to 3
- second_gain: bfloat16 [768], replicated, may hold values from 0.5 to 1.5
- second_shift: bfloat16 [768], replicated, may hold values from -3 to 3
- head_gate: float32 [12], replicated, may hold values from 0.5 to 1.5
- hidden_gate: float32 [768], replicated, may hold values from 0.5 to 1.5
- unit_gate: float32 [3072], replicated, may hold values from 0.5 to 1.5
- head_mask: int32 [12], replicated, may hold values 0 or 1
- hidden_mask: int32 [768], replicated, may hold values 0 or 1
- unit_mask: int32 [3072], replicated, may hold values 0 or 1
- attention_mask: int32 [8], replicated, may hold values 0 or 1
- feedforward_mask: int32 [8], replicated, may hold values 0 or 1
- continuation_lengths: int32 [8, 2], replicated, may hold values from 512 to 1536, as said below
Outputs:
- layer_output: bfloat16 [24576, 768], P(('wt', 'seq'))
- tokens_grad: float32 [24576, 768], P(('wt', 'seq'))
- attention_weight_grad: float32 [768, 2304], P('wt')
- query_bias_grad: float32 [768], P('wt')
- value_bias_grad: float32 [768], P('wt')
- output_weight_grad: float32 [768, 768], P('wt')
- output_bias_grad: float32 [768], P('wt')
- first_gain_grad: float32 [768], P('wt')
- first_shift_grad: float32 [768], P('wt')
- expand_weight_grad: float32 [768, 3072], P('wt')
- expand_bias_grad: float32 [3072], P('wt')
- contract_weight_grad: float32 [3072, 768], P('wt')
- contract_bias_grad: float32 [768], P('wt')
- second_gain_grad: float32 [768], P('wt')
- second_shift_grad: float32 [768], P('wt')
- head_gate_grad: float32 [12], replicated
- hidden_gate_grad: float32 [768], P('wt')
- unit_gate_grad: float32 [3072], P('wt')
Inputs may be any that keep to these rules, and one draw needn't show every extreme that they name: `continuation_lengths`: row g lists the lengths of group g's 2 continuations; in every row one continuation, at a place drawn from the seed, has exactly 1536 tokens, and the others share the remaining 2 * 1024 - 1536 tokens evenly, any remainder on the last of them.
All inputs are finite; a program needn't handle non-finite values.
Results may differ from a plain program's by a relative error of at most 0.018.
Values may be sent and summed in bfloat16 or wider, within the bound.
A program may use at most 192 MiB of HBM per device.

v0:
```python
import jax
import jax.numpy as jnp
from jax import lax
from jax.sharding import PartitionSpec as P

PROMPT = 1024
GRP_WT = 1
GLEN = 3072


epsilon = 1e-06
score_scale = 0.125
root_half = 0.7071067811865476
density_scale = 0.3989422804014327


def segment_ids(lengths_row):
    position = jnp.arange(GLEN, dtype=jnp.int32)
    seg_ends = PROMPT + jnp.cumsum(lengths_row, dtype=jnp.int32)
    counted = jnp.sum((position[:, None] >= seg_ends[None, :-1]).astype(jnp.int32), axis=1)
    return jnp.where(position < PROMPT, 0, 1 + counted)


def norm_parts(summed):
    centre = summed - jnp.mean(summed, axis=-1, keepdims=True)
    inverse = lax.rsqrt(jnp.mean(centre * centre, axis=-1, keepdims=True) + epsilon)
    return (centre * inverse, inverse)


def norm_back(grad_normed, normed, inverse):
    return inverse * (
        grad_normed
        - jnp.mean(grad_normed, axis=-1, keepdims=True)
        - normed * jnp.mean(grad_normed * normed, axis=-1, keepdims=True)
    )


def masked_scores(query_rows, keys_all, query_segments, key_segments):
    scores = (
        jnp.einsum("qd,kd->qk", query_rows, keys_all, preferred_element_type=jnp.float32)
        * score_scale
    )
    allowed = (key_segments[None, :] == query_segments[:, None]) | (key_segments[None, :] == 0)
    return jnp.where(allowed, scores, -jnp.inf)


def head_forward(queries, keys_all, values, segments):
    block_rows = min(512, GLEN)

    def one_block(offset):
        query_rows = lax.dynamic_slice_in_dim(queries, offset, block_rows, 0)
        query_segments = lax.dynamic_slice_in_dim(segments, offset, block_rows, 0)
        scores = masked_scores(query_rows, keys_all, query_segments, segments)
        row_max = jnp.max(scores, axis=-1, keepdims=True)
        weights = jnp.exp(scores - row_max)
        summed = jnp.sum(weights, axis=-1, keepdims=True)
        attn_probs = (weights / summed).astype(jnp.bfloat16)
        mixed_rows = jnp.dot(attn_probs, values, preferred_element_type=jnp.float32)
        return (mixed_rows.astype(jnp.bfloat16), (row_max + jnp.log(summed))[:, 0])

    offsets = jnp.arange(GLEN // block_rows, dtype=jnp.int32) * block_rows
    mixed_rows, log_sums = lax.map(one_block, offsets)
    return (mixed_rows.reshape(GLEN, values.shape[1]), log_sums.reshape(GLEN))


def head_backward(queries, keys_all, values, segments, log_sums, grad_mixed):
    block_rows = min(512, GLEN)

    def one_block(running, offset):
        grad_keys, grad_values = running
        query_rows = lax.dynamic_slice_in_dim(queries, offset, block_rows, 0)
        query_segments = lax.dynamic_slice_in_dim(segments, offset, block_rows, 0)
        log_rows = lax.dynamic_slice_in_dim(log_sums, offset, block_rows, 0)
        grad_rows = lax.dynamic_slice_in_dim(grad_mixed, offset, block_rows, 0)
        scores = masked_scores(query_rows, keys_all, query_segments, segments)
        attn_probs = jnp.exp(scores - log_rows[:, None])
        probs_low = attn_probs.astype(jnp.bfloat16)
        grad_probs = jnp.einsum("qd,kd->qk", grad_rows, values, preferred_element_type=jnp.float32)
        row_inner = jnp.sum(attn_probs * grad_probs, axis=-1, keepdims=True)
        grad_scores = (attn_probs * (grad_probs - row_inner)).astype(jnp.bfloat16)
        grad_query = (
            jnp.dot(grad_scores, keys_all, preferred_element_type=jnp.float32) * score_scale
        )
        grad_keys = (
            grad_keys
            + jnp.einsum("qk,qd->kd", grad_scores, query_rows, preferred_element_type=jnp.float32)
            * score_scale
        )
        grad_values = grad_values + jnp.einsum(
            "qk,qd->kd", probs_low, grad_rows, preferred_element_type=jnp.float32
        )
        return ((grad_keys, grad_values), grad_query)

    offsets = jnp.arange(GLEN // block_rows, dtype=jnp.int32) * block_rows
    zero_rows = jnp.zeros(keys_all.shape, jnp.float32)
    (grad_keys, grad_values), grad_query = lax.scan(one_block, (zero_rows, zero_rows), offsets)
    return (grad_query.reshape(GLEN, keys_all.shape[1]), grad_keys, grad_values)


def local(
    tokens,
    output_cotangent,
    attention_weight,
    query_bias,
    value_bias,
    output_weight,
    output_bias,
    first_gain,
    first_shift,
    expand_weight,
    expand_bias,
    contract_weight,
    contract_bias,
    second_gain,
    second_shift,
    head_gate,
    hidden_gate,
    unit_gate,
    head_mask,
    hidden_mask,
    unit_mask,
    attention_mask,
    feedforward_mask,
    continuation_lengths,
):
    row_count = tokens.shape[0]
    seq_count = lax.axis_size("seq")
    head_count = head_gate.shape[0]
    model_width = hidden_gate.shape[0]
    head_size = model_width // head_count
    local_heads = head_count // seq_count
    seq_index = lax.axis_index("seq")
    wt_index = lax.axis_index("wt")
    full_attention, full_output, full_expand, full_contract = (
        lax.all_gather(attention_weight, "wt", axis=0, tiled=True),
        lax.all_gather(output_weight, "wt", axis=0, tiled=True),
        lax.all_gather(expand_weight, "wt", axis=0, tiled=True),
        lax.all_gather(contract_weight, "wt", axis=0, tiled=True),
    )
    position = seq_index * row_count + jnp.arange(row_count, dtype=jnp.int32)
    group_local = position // GLEN
    own_groups = jnp.arange(GRP_WT, dtype=jnp.int32)
    chosen = group_local[:, None] == own_groups[None, :]
    first_group = wt_index * GRP_WT
    own_attention = lax.dynamic_slice_in_dim(attention_mask, first_group, GRP_WT, 0).astype(
        jnp.float32
    )
    own_feedforward = lax.dynamic_slice_in_dim(feedforward_mask, first_group, GRP_WT, 0).astype(
        jnp.float32
    )
    attention_rows = jnp.sum(jnp.where(chosen, own_attention[None, :], 0.0), axis=1)
    feedforward_rows = jnp.sum(jnp.where(chosen, own_feedforward[None, :], 0.0), axis=1)
    head_scale = head_mask.astype(jnp.float32) * head_gate
    hidden_scale = hidden_mask.astype(jnp.float32) * hidden_gate
    unit_scale = unit_mask.astype(jnp.float32) * unit_gate
    first_gain_f = first_gain.astype(jnp.float32)
    second_gain_f = second_gain.astype(jnp.float32)
    bias_table = jnp.stack(
        [
            query_bias.astype(jnp.float32).reshape(head_count, head_size),
            jnp.zeros((head_count, head_size), jnp.float32),
            value_bias.astype(jnp.float32).reshape(head_count, head_size),
        ],
        axis=1,
    )
    projected = (
        jnp.dot(tokens, full_attention, preferred_element_type=jnp.float32).reshape(
            row_count, head_count, 3, head_size
        )
        + bias_table
    )
    value_scale = head_scale[None, :] * attention_rows[:, None]
    constant_rows = jnp.ones_like(value_scale)
    factor = jnp.stack([constant_rows, constant_rows, value_scale], axis=2)[..., None]
    packed = (
        (projected * factor)
        .astype(jnp.bfloat16)
        .reshape(row_count, seq_count, local_heads, 3 * head_size)
    )
    by_head = lax.all_to_all(packed, "seq", split_axis=1, concat_axis=0, tiled=True)
    grouped = by_head.reshape(GRP_WT, GLEN, local_heads, 3, head_size).transpose(0, 2, 3, 1, 4)
    lengths_own = lax.dynamic_slice_in_dim(continuation_lengths, first_group, GRP_WT, 0)
    segments = jax.vmap(segment_ids)(lengths_own)

    def attend_group(group_item):
        group_packed, group_segments = group_item

        def attend_head(head_packed):
            return head_forward(head_packed[0], head_packed[1], head_packed[2], group_segments)

        return lax.map(attend_head, group_packed)

    mixed_heads, log_sums = lax.map(attend_group, (grouped, segments))
    leaving = mixed_heads.transpose(0, 2, 1, 3).reshape(GRP_WT * GLEN, 1, local_heads * head_size)
    context = lax.all_to_all(leaving, "seq", split_axis=0, concat_axis=1, tiled=True).reshape(
        row_count, model_width
    )
    attn_out = jnp.dot(
        context, full_output, preferred_element_type=jnp.float32
    ) + output_bias.astype(jnp.float32)
    normed_one, inverse_one = norm_parts(tokens.astype(jnp.float32) + attn_out)
    shaped_one = normed_one * first_gain_f + first_shift.astype(jnp.float32)
    first_out = shaped_one * hidden_scale
    first_low = first_out.astype(jnp.bfloat16)
    hidden = jnp.dot(
        first_low, full_expand, preferred_element_type=jnp.float32
    ) + expand_bias.astype(jnp.float32)
    gelu_out = jax.nn.gelu(hidden, approximate=False)
    unit_rows_scale = unit_scale[None, :] * feedforward_rows[:, None]
    activated = (gelu_out * unit_rows_scale).astype(jnp.bfloat16)
    branch = jnp.dot(
        activated, full_contract, preferred_element_type=jnp.float32
    ) + contract_bias.astype(jnp.float32)
    normed_two, inverse_two = norm_parts(first_out + branch)
    shaped_two = normed_two * second_gain_f + second_shift.astype(jnp.float32)
    layer_output = (shaped_two * hidden_scale).astype(jnp.bfloat16)
    back_attention, back_output, back_expand, back_contract = (
        full_attention,
        full_output,
        full_expand,
        full_contract,
    )
    cotangent = output_cotangent.astype(jnp.float32)
    grad_shaped_two = cotangent * hidden_scale
    second_gain_grad = jnp.sum(grad_shaped_two * normed_two, axis=0)
    second_shift_grad = jnp.sum(grad_shaped_two, axis=0)
    grad_total_two = norm_back(grad_shaped_two * second_gain_f, normed_two, inverse_two)
    grad_branch = grad_total_two.astype(jnp.bfloat16)
    contract_bias_grad = jnp.sum(grad_branch.astype(jnp.float32), axis=0)
    contract_weight_grad = jnp.einsum(
        "ti,td->id", activated, grad_branch, preferred_element_type=jnp.float32
    )
    grad_activated = jnp.einsum(
        "td,id->ti", grad_branch, back_contract, preferred_element_type=jnp.float32
    )
    unit_gate_grad = unit_mask.astype(jnp.float32) * jnp.sum(
        grad_activated * gelu_out * feedforward_rows[:, None], axis=0
    )
    cumulative = 0.5 * (1.0 + lax.erf(hidden * root_half))
    gelu_slope = cumulative + hidden * jnp.exp(-0.5 * hidden * hidden) * density_scale
    grad_hidden = (grad_activated * unit_rows_scale * gelu_slope).astype(jnp.bfloat16)
    expand_bias_grad = jnp.sum(grad_hidden.astype(jnp.float32), axis=0)
    expand_weight_grad = jnp.einsum(
        "td,tf->df", first_low, grad_hidden, preferred_element_type=jnp.float32
    )
    grad_first = grad_total_two + jnp.einsum(
        "tf,df->td", grad_hidden, back_expand, preferred_element_type=jnp.float32
    )
    grad_shaped_one = grad_first * hidden_scale
    first_gain_grad = jnp.sum(grad_shaped_one * normed_one, axis=0)
    first_shift_grad = jnp.sum(grad_shaped_one, axis=0)
    hidden_gate_grad = hidden_mask.astype(jnp.float32) * jnp.sum(
        cotangent * shaped_two + grad_first * shaped_one, axis=0
    )
    grad_total_one = norm_back(grad_shaped_one * first_gain_f, normed_one, inverse_one)
    grad_attn = grad_total_one.astype(jnp.bfloat16)
    output_bias_grad = jnp.sum(grad_attn.astype(jnp.float32), axis=0)
    output_weight_grad = jnp.einsum(
        "ti,td->id", context, grad_attn, preferred_element_type=jnp.float32
    )
    grad_context = jnp.einsum(
        "td,id->ti", grad_attn, back_output, preferred_element_type=jnp.float32
    ).astype(jnp.bfloat16)
    arriving = lax.all_to_all(
        grad_context.reshape(row_count, seq_count, local_heads * head_size),
        "seq",
        split_axis=1,
        concat_axis=0,
        tiled=True,
    )
    grad_heads = arriving.reshape(GRP_WT, GLEN, local_heads, head_size).transpose(0, 2, 1, 3)

    def back_group(group_item):
        group_packed, group_segments, group_sums, group_grad = group_item

        def back_head(head_item):
            head_packed, head_sums, head_grad = head_item
            return head_backward(
                head_packed[0], head_packed[1], head_packed[2], group_segments, head_sums, head_grad
            )

        return lax.map(back_head, (group_packed, group_sums, group_grad))

    grad_query, grad_keys, grad_values = lax.map(
        back_group, (grouped, segments, log_sums, grad_heads)
    )
    grad_stack = jnp.stack([grad_query, grad_keys, grad_values], axis=2).astype(jnp.bfloat16)
    returning = grad_stack.transpose(0, 3, 1, 2, 4).reshape(
        GRP_WT * GLEN, 1, local_heads, 3 * head_size
    )
    grad_packed = lax.all_to_all(returning, "seq", split_axis=0, concat_axis=1, tiled=True).reshape(
        row_count, head_count, 3, head_size
    )
    head_partial = head_mask.astype(jnp.float32) * jnp.sum(
        grad_packed[:, :, 2, :].astype(jnp.float32)
        * projected[:, :, 2, :]
        * attention_rows[:, None, None],
        axis=(0, 2),
    )
    grad_projected = (grad_packed.astype(jnp.float32) * factor).astype(jnp.bfloat16)
    query_bias_grad = jnp.sum(grad_projected[:, :, 0, :].astype(jnp.float32), axis=0).reshape(
        model_width
    )
    value_bias_grad = jnp.sum(grad_projected[:, :, 2, :].astype(jnp.float32), axis=0).reshape(
        model_width
    )
    grad_flat = grad_projected.reshape(row_count, 3 * model_width)
    attention_weight_grad = jnp.einsum(
        "td,tc->dc", tokens, grad_flat, preferred_element_type=jnp.float32
    )
    tokens_grad = grad_total_one + jnp.einsum(
        "tc,dc->td", grad_flat, back_attention, preferred_element_type=jnp.float32
    )
    head_gate_grad = lax.psum(head_partial, ("seq", "wt"))
    width_vectors = jnp.stack(
        [
            query_bias_grad,
            value_bias_grad,
            output_bias_grad,
            first_gain_grad,
            first_shift_grad,
            contract_bias_grad,
            second_gain_grad,
            second_shift_grad,
            hidden_gate_grad,
        ],
        axis=1,
    )
    unit_vectors = jnp.stack([expand_bias_grad, unit_gate_grad], axis=1)
    pieces = (
        lax.psum_scatter(attention_weight_grad, "wt", scatter_dimension=0, tiled=True),
        lax.psum_scatter(output_weight_grad, "wt", scatter_dimension=0, tiled=True),
        lax.psum_scatter(expand_weight_grad, "wt", scatter_dimension=0, tiled=True),
        lax.psum_scatter(contract_weight_grad, "wt", scatter_dimension=0, tiled=True),
        lax.psum_scatter(width_vectors, "wt", scatter_dimension=0, tiled=True),
        lax.psum_scatter(unit_vectors, "wt", scatter_dimension=0, tiled=True),
    )
    shards = (
        lax.psum(pieces[0].astype(jnp.bfloat16), "seq").astype(jnp.float32),
        lax.psum(pieces[1].astype(jnp.bfloat16), "seq").astype(jnp.float32),
        lax.psum(pieces[2].astype(jnp.bfloat16), "seq").astype(jnp.float32),
        lax.psum(pieces[3].astype(jnp.bfloat16), "seq").astype(jnp.float32),
        lax.psum(pieces[4].astype(jnp.bfloat16), "seq").astype(jnp.float32),
        lax.psum(pieces[5].astype(jnp.bfloat16), "seq").astype(jnp.float32),
    )
    width_shard = shards[4]
    unit_shard = shards[5]
    return (
        layer_output,
        tokens_grad,
        shards[0],
        width_shard[:, 0],
        width_shard[:, 1],
        shards[1],
        width_shard[:, 2],
        width_shard[:, 3],
        width_shard[:, 4],
        shards[2],
        unit_shard[:, 0],
        shards[3],
        width_shard[:, 5],
        width_shard[:, 6],
        width_shard[:, 7],
        head_gate_grad,
        width_shard[:, 8],
        unit_shard[:, 1],
    )


def solution(mesh):
    return jax.shard_map(
        local,
        mesh=mesh,
        in_specs=(
            P(("wt", "seq"), None),
            P(("wt", "seq"), None),
            P("wt", None),
            P(),
            P(),
            P("wt", None),
            P(),
            P(),
            P(),
            P("wt", None),
            P(),
            P("wt", None),
            P(),
            P(),
            P(),
            P(),
            P(),
            P(),
            P(),
            P(),
            P(),
            P(),
            P(),
            P(),
        ),
        out_specs=(
            P(("wt", "seq"), None),
            P(("wt", "seq"), None),
            P("wt", None),
            P("wt"),
            P("wt"),
            P("wt", None),
            P("wt"),
            P("wt"),
            P("wt"),
            P("wt", None),
            P("wt"),
            P("wt", None),
            P("wt"),
            P("wt"),
            P("wt"),
            P(),
            P("wt"),
            P("wt"),
        ),
        check_vma=False,
    )
```

profile of v0, /device:TPU:0, one launch (start us, length us, event | category | flops | bytes accessed | tf_op | source)
XLA Modules:
  0.0 1243.2 jit_solution(8047395525472370364)
XLA Ops:
  14.0 40.0 %all-gather.5.cloned.1.call-done = bf16[768,2304]{1,0:T(8,128)(2,1)} async-done(((bf16[96,2304]{1,0:T(8,128)(2,1)}), bf16[768,2304]{1,0:T(8,128)(2,1)}) %all-gather.5.cloned.1.call-update) | async-done | bytes 3538960 | tf_op jit(solution)/shard_map/all_gather | solution.py:135
  53.9 5.3 fusion.75
  64.3 3.7 all-to-all-start
  69.3 39.7 %all-to-all-done = bf16[768,4,3,192]{0,3,2,1:T(8,128)(2,1)S(1)} async-done(((bf16[768,4,3,192]{0,3,2,1:T(8,128)(2,1)}), bf16[768,4,3,192]{0,3,2,1:T(8,128)(2,1)S(1)}, u32[]{:S(2)}, u32[]{:S(2)}) %all-to-all-start) | async-done | bytes 3538976 | tf_op jit(solution)/shard_map/all_to_all | solution.py:180
  109.1 4.5 copy.111
  113.6 6.0 reshape.358
  119.6 5.6 copy.112
  125.2 140.0 %while.78 = (s32[]{:T(128)}, bf16[3,3072,64]{1,2,0:T(8,128)(2,1)}, f32[3,3072]{1,0:T(4,128)}, bf16[3,3,3072,64]{3,2,1,0:T(8,128)(2,1)}, s32[]{:T(128)}, /*index=...) while((s32[]{:T(128)}, bf16[3,3072,64]{1,2,0:T(8,128)(2,1)}, ...), condition=%wide.region_6.7_spmd.clone, body=%wide.region_1.6_spmd.clone.sunk | while | flops 418432512 | bytes 25481688 | solution.py:191
  127.7 41.2 %while.81 = (s32[]{:T(128)}, bf16[6,512,64]{1,2,0:T(8,128)(2,1)S(1)}, f32[6,512]{1,0:T(8,128)S(1)}, s32[3072]{0:T(1024)S(1)}, s32[6]{0:T(128)S(1)}, /*index=5*/b...) while((s32[]{:T(128)}, ...), condition=%wide.region_5.5_spmd, body=%wide.region_2.4_spmd.sunk | while | flops 418417152 | bytes 20701364 | solution.py:62
  174.3 41.2 %while.81 = (s32[]{:T(128)}, bf16[6,512,64]{1,2,0:T(8,128)(2,1)S(1)}, f32[6,512]{1,0:T(8,128)S(1)}, s32[3072]{0:T(1024)S(1)}, s32[6]{0:T(128)S(1)}, /*index=5*/b...) while((s32[]{:T(128)}, ...), condition=%wide.region_5.5_spmd, body=%wide.region_2.4_spmd.sunk | while | flops 418417152 | bytes 20701364 | solution.py:62
  221.0 41.2 %while.81 = (s32[]{:T(128)}, bf16[6,512,64]{1,2,0:T(8,128)(2,1)S(1)}, f32[6,512]{1,0:T(8,128)S(1)}, s32[3072]{0:T(1024)S(1)}, s32[6]{0:T(128)S(1)}, /*index=5*/b...) while((s32[]{:T(128)}, ...), condition=%wide.region_5.5_spmd, body=%wide.region_2.4_spmd.sunk | while | flops 418417152 | bytes 20701364 | solution.py:62
  272.1 4.8 all-to-all-start.1
  284.8 7.2 all-to-all-done.1
  295.5 6.0 copy.115
  308.5 29.7 %fusion.28 = (f32[768,3072]{1,0:T(8,128)}, f32[768,3072]{1,0:T(8,128)}) fusion(f32[3072]{0:T(1024)} %convert_element_type.183, bf16[768,3072]{1,0:T(8,128)(2,1)} %all-gather.9.cloned.1.call-done, f32[768]{0:T(1024)S(1)} %get-tuple-element.558, f32[768]{0:T(1024)} %convert_element_type.180, f32[768]{0:T(1024)S(1)} %convert_element_type.179, ...), kind=kOutput, calls=%fused_computation.62 | convolution fusion | flops 3780771840 | bytes 25979904 | tf_op jit(solution)/shard_map/dot_general | solution.py:205
  338.2 10.1 fusion.74
  352.6 16.4 %convert_reduce_fusion = (f32[3072]{0:T(1024)}, bf16[768,3072]{1,0:T(8,128)(2,1)}, f32[3072]{0:T(1024)}) fusion(f32[768,3072]{1,0:T(8,128)} %get-tuple-element.554, f32[3072]{0:T(1024)S(1)} %copy-done.30, f32[768]{0:T(1024)S(1)} %copy-done.36, f32[3072]{0:T(1024)S(1)} %copy-done.32, f32[768,3072]{1,0:T(8,128)} %get-tuple-element.553, ...), kind=kOutput, calls=%fused_computation.68 | convolution fusion | flops 3666929664 | bytes 30723072 | tf_op jit(solution)/shard_map/td,id->ti/dot_general | solution.py:233
  369.1 9.5 fusion.52
  387.4 4.2 fusion.59
  391.7 10.1 all-to-all-done.2
  404.9 301.5 %while.80 = (s32[]{:T(128)}, bf16[3,3072,64]{1,2,0:T(8,128)(2,1)}, bf16[3,3072,64]{1,2,0:T(8,128)(2,1)}, bf16[3,3072,64]{1,2,0:T(8,128)(2,1)}, bf16[3,3,3072,64]...) while((s32[]{:T(128)}, bf16[3,3072,64]{1,2,0:T(8,128)(2,1)}, ...), condition=%wide.region_19.20_spmd.clone, body=%wide.region_15.19_spmd.clone.sunk | while | flops 1024968192 | bytes 62081840 | solution.py:282
  411.8 91.2 %while.82 = (s32[]{:T(128)}, f32[3072,64]{0,1:T(8,128)S(1)}, f32[3072,64]{0,1:T(8,128)S(1)}, bf16[6,512,64]{1,2,0:T(8,128)(2,1)S(1)}, s32[3072]{0:T(1024)S(1)}, ...) while((s32[]{:T(128)}, f32[3072,64]{0,1:T(8,128)S(1)}, ...), condition=%wide.region_18.18_spmd.clone, body=%wide.region_16.17_spmd.clone.sunk | while | flops 1024952832 | bytes 52607444 | solution.py:96
  417.1 3.6 multiply_reduce_fusion.9
  432.3 3.6 multiply_reduce_fusion.9
  447.5 3.6 multiply_reduce_fusion.9
  462.7 3.6 multiply_reduce_fusion.9
  512.3 91.2 %while.82 = (s32[]{:T(128)}, f32[3072,64]{0,1:T(8,128)S(1)}, f32[3072,64]{0,1:T(8,128)S(1)}, bf16[6,512,64]{1,2,0:T(8,128)(2,1)S(1)}, s32[3072]{0:T(1024)S(1)}, ...) while((s32[]{:T(128)}, f32[3072,64]{0,1:T(8,128)S(1)}, ...), condition=%wide.region_18.18_spmd.clone, body=%wide.region_16.17_spmd.clone.sunk | while | flops 1024952832 | bytes 52607444 | solution.py:96
  578.4 3.6 multiply_reduce_fusion.9
  593.6 3.6 multiply_reduce_fusion.9
  612.8 91.2 %while.82 = (s32[]{:T(128)}, f32[3072,64]{0,1:T(8,128)S(1)}, f32[3072,64]{0,1:T(8,128)S(1)}, bf16[6,512,64]{1,2,0:T(8,128)(2,1)S(1)}, s32[3072]{0:T(1024)S(1)}, ...) while((s32[]{:T(128)}, f32[3072,64]{0,1:T(8,128)S(1)}, ...), condition=%wide.region_18.18_spmd.clone, body=%wide.region_16.17_spmd.clone.sunk | while | flops 1024952832 | bytes 52607444 | solution.py:96
  618.1 3.6 multiply_reduce_fusion.9
  678.9 3.6 multiply_reduce_fusion.9
  694.0 3.6 multiply_reduce_fusion.9
  708.6 6.9 copy.126
  715.5 76.7 %all_to_all.60 = bf16[3072,1,3,192]{3,2,1,0:T(4,128)(2,1)} all-to-all(bf16[3072,1,3,192]{3,2,1,0:T(4,128)(2,1)} %copy.126), channel_id=1, replica_groups=mesh['seq'=4,'wt'=8] {'seq'}, dimensions={0} | all-to-all | bytes 7077888 | tf_op jit(solution)/shard_map/all_to_all | solution.py:291
  792.2 8.2 copy.128
  804.1 4.9 convolution_bitcast_fusion
  809.0 8.0 copy.140
  817.7 12.8 %fusion.62 = f32[3072,768]{1,0:T(8,128)} fusion(f32[768,768]{0,1:T(8,128)} %copy-done.7, f32[768,3072]{1,0:T(8,128)} %get-tuple-element.553, f32[768]{0:T(1024)S(1)} %copy-done.37, f32[3072]{0:T(1024)S(1)} %copy-done.33), kind=kOutput, calls=%fused_computation.175 | convolution fusion | flops 3631546368 | bytes 21249024 | tf_op jit(solution)/shard_map/ti,td->id/dot_general | solution.py:230
  831.2 10.8 fusion.68
  866.0 26.0 %reduce-scatter.19.cloned.1.call-done = f32[96,2304]{1,0:T(8,128)} async-done(((f32[768,2304]{1,0:T(8,128)}), f32[96,2304]{1,0:T(8,128)}) %reduce-scatter.19.cloned.1.call-update) | async-done | bytes 884752
  894.3 97.9 %reduce-scatter.17.cloned.1.call-done = f32[384,768]{1,0:T(8,128)} async-done(((f32[3072,768]{1,0:T(8,128)}), f32[384,768]{1,0:T(8,128)}) %reduce-scatter.17.cloned.1.call-update) | async-done | bytes 1179664 | tf_op jit(solution)/shard_map/reduce_scatter | solution.py:334
  994.4 98.0 %reduce-scatter.15.cloned.1.call-done = f32[96,3072]{1,0:T(8,128)} async-done(((f32[768,3072]{1,0:T(8,128)}), f32[96,3072]{1,0:T(8,128)}) %reduce-scatter.15.cloned.1.call-update) | async-done | bytes 1179664 | tf_op jit(solution)/shard_map/reduce_scatter | solution.py:333
  1100.1 27.1 %reduce-scatter.23.cloned.1.call-done = f32[384,2]{1,0:T(8,128)} async-done(((f32[3072,2]{1,0:T(8,128)}), f32[384,2]{1,0:T(8,128)}) %reduce-scatter.23.cloned.1.call-update) | async-done | bytes 3088
  1128.2 38.2 %psum.55 = f32[12]{0:T(128)} all-reduce(f32[12]{0:T(128)S(1)} %convert_multiply_fusion.7), channel_id=1, replica_groups=mesh['seq'=4,'wt'=8] {'seq','wt'}, use_global_device_ids=true, to_apply=%region_44.45 | all-reduce | flops 12 | bytes 96 | tf_op jit(solution)/shard_map/psum | solution.py:314
  1166.4 7.2 convolution_add_fusion.1
  1176.4 10.2 all-reduce.1
  1187.8 41.5 %all-reduce.5.cloned.1.call-done = (bf16[96,2304]{0,1:T(8,128)(2,1)}, bf16[96,768]{1,0:T(8,128)(2,1)}, bf16[96,3072]{1,0:T(8,128)(2,1)}, bf16[384,768]{1,0:T(8,128)(2,1)}) async-done(((bf16[96,2304]{0,1:T(8,128)(2,1)}, bf16[96,768]{1,0:T(8,128)(2,1)}, bf16[96,3072]{1,0:T(8,128)(2,1)}, bf16[384,768]{1,0:T(8,128)(2,1)}), (bf16[96,2304]{0,1:T(8,128)(2,1)}, bf16[96,768]{1,0:T(8,128)(2,1)}, ...) | async-done | bytes 1769488 | tf_op jit(solution)/shard_map/psum | solution.py:339
  (684 shorter events, 445.1 us)
Async XLA Ops:
  7.2 61.5 %copy-start = (s32[8,2]{0,1:T(2,128)S(1)}, s32[8,2]{0,1:T(2,128)}, u32[]{:S(2)}) copy-start(s32[8,2]{0,1:T(2,128)} %param.55) | copy-start | bytes 196
  7.2 46.7 %all-gather.5.cloned.1.call-start = ((), (), s32[]{:S(2)}) async-start(), calls=%async_computation.10 | async-start | bytes 3981312 | tf_op jit(solution)/shard_map/all_gather | solution.py:135
  7.9 296.5 %all-gather.7.cloned.1.call-start = ((), (), s32[]{:S(2)}) async-start(), calls=%async_computation.11 | async-start | bytes 1327104 | tf_op jit(solution)/shard_map/all_gather | solution.py:136
  8.7 299.8 %all-gather.9.cloned.1.call-start = ((), (), s32[]{:S(2)}) async-start(), calls=%async_computation.12 | async-start | bytes 5308416 | tf_op jit(solution)/shard_map/all_gather | solution.py:137
  13.9 45.3 %copy-start.8 = (f32[768,12,3]{0,2,1:T(4,128)}, f32[768,12,3]{0,2,1:T(4,128)S(1)}, u32[]{:S(2)}) copy-start(f32[768,12,3]{0,2,1:T(4,128)S(1)} %stack.54) | copy-start | bytes 331780
  64.3 44.7 %all-to-all-start = ((bf16[768,4,3,192]{0,3,2,1:T(8,128)(2,1)}), bf16[768,4,3,192]{0,3,2,1:T(8,128)(2,1)S(1)}, u32[]{:S(2)}, u32[]{:S(2)}) async-start(bf16[768,4,3,192]{0,3,2,1:T(8,128)(2,1)} %multiply_convert_fusion.2), calls=%async_computation | async-start | bytes 7077888 | tf_op jit(solution)/shard_map/all_to_all | solution.py:180
  68.1 270.1 %all-gather.11.cloned.1.call-start = ((), (), s32[]{:S(2)}) async-start(), calls=%async_computation.13 | async-start | bytes 5308416 | tf_op jit(solution)/shard_map/all_gather | solution.py:138
  269.1 9.3 copy-start.48
  269.1 10.5 copy-start.40
  269.2 10.5 copy-start.41
  269.2 11.1 copy-start.42
  269.2 11.1 copy-start.43
  269.2 11.1 copy-start.44
  269.2 11.7 copy-start.45
  269.2 12.3 copy-start.34
  269.2 12.9 %copy-start.9 = (bf16[768,768]{1,0:T(8,128)(2,1)S(1)}, bf16[768,768]{1,0:T(8,128)(2,1)}, u32[]{:S(2)}) copy-start(bf16[768,768]{1,0:T(8,128)(2,1)} %param.33) | copy-start | bytes 3538948
  272.1 4.8 copy-start.10
  272.1 11.5 copy-start.27
  272.1 11.5 copy-start.35
  272.1 12.1 copy-start.16
  272.1 12.1 copy-start.31
  272.1 19.9 %all-to-all-start.1 = ((bf16[4,2,73728]{2,1,0:T(2,128)(2,1)}), bf16[4,2,73728]{2,1,0:T(2,128)(2,1)}, u32[]{:S(2)}, u32[]{:S(2)}) async-start(bf16[4,2,73728]{2,1,0:T(2,128)(2,1)} %reshape.378), calls=%async_computation.1 | async-start | bytes 2359296 | tf_op jit(solution)/shard_map/all_to_all | solution.py:195
  279.7 98.9 %copy-start.23 = (f32[768]{0:T(1024)}, f32[768]{0:T(1024)S(1)}, u32[]{:S(2)}) copy-start(f32[768]{0:T(1024)S(1)} %convert_element_type.179) | copy-start | bytes 9220
  284.2 94.4 %copy-start.14 = (f32[768]{0:T(1024)}, f32[768]{0:T(1024)S(1)}, u32[]{:S(2)}) copy-start(f32[768]{0:T(1024)S(1)} %get-tuple-element.558) | copy-start | bytes 9220
  307.3 71.2 %copy-start.4 = (f32[768,768]{0,1:T(8,128)}, f32[768,768]{0,1:T(8,128)S(1)}, u32[]{:S(2)}) copy-start(f32[768,768]{0,1:T(8,128)S(1)} %get-tuple-element.552) | copy-start | bytes 7077892
  307.3 71.2 %copy-start.18 = (f32[768]{0:T(1024)}, f32[768]{0:T(1024)S(1)}, u32[]{:S(2)}) copy-start(f32[768]{0:T(1024)S(1)} %broadcast_multiply_fusion.6) | copy-start | bytes 9220
  350.3 18.8 %slice-start = ((s8[4718592]{0:T(1024)(128)(4,1)}), s8[4194304]{0:T(1024)(128)(4,1)S(1)}, s32[]{:S(2)}) async-start(s8[4718592]{0:T(1024)(128)(4,1)} %bitcast.211), calls=%async_computation.21 | async-start | bytes 8388608
  352.1 17.0 %copy-start.7 = (f32[768,768]{0,1:T(8,128)}, f32[768,768]{0,1:T(8,128)S(1)}, u32[]{:S(2)}) copy-start(f32[768,768]{0,1:T(8,128)S(1)} %get-tuple-element.525) | copy-start | bytes 7077892
  352.6 16.5 %copy-start.25 = (f32[768]{0:T(1024)S(1)}, f32[768]{0:T(1024)}, u32[]{:S(2)}) copy-start(f32[768]{0:T(1024)} %add_rsqrt_fusion.1) | copy-start | bytes 9220
  352.6 16.5 %copy-start.38 = (f32[768]{0:T(1024)S(1)}, f32[768]{0:T(1024)}, u32[]{:S(2)}) copy-start(f32[768]{0:T(1024)} %convert_element_type.180) | copy-start | bytes 9220
  352.6 16.5 %copy-start.39 = (f32[768]{0:T(1024)S(1)}, f32[768]{0:T(1024)}, u32[]{:S(2)}) copy-start(f32[768]{0:T(1024)} %convert_element_type.189) | copy-start | bytes 9220
  352.6 16.5 %slice-start.1 = ((s8[4718592]{0:T(1024)(128)(4,1)}), s8[524288]{0:T(1024)(128)(4,1)S(1)}, s32[]{:S(2)}) async-start(s8[4718592]{0:T(1024)(128)(4,1)} %bitcast.211), calls=%async_computation.22 | async-start | bytes 1048576
  383.8 18.0 %all-to-all-start.2 = ((bf16[768,4,192]{0,2,1:T(8,128)(2,1)}), bf16[768,4,192]{0,2,1:T(8,128)(2,1)S(1)}, u32[]{:S(2)}, u32[]{:S(2)}) async-start(bf16[768,4,192]{0,2,1:T(8,128)(2,1)} %bitcast.18), calls=%async_computation.2 | async-start | bytes 2359296 | tf_op jit(solution)/shard_map/all_to_all | solution.py:264
  387.3 477.0 %reduce-scatter.13.cloned.1.call-start = ((), (), s32[]{:S(2)}) async-start(), calls=%async_computation.14 | async-start | bytes 2654208 | tf_op jit(solution)/shard_map/reduce_scatter | solution.py:332
  391.7 500.4 %reduce-scatter.19.cloned.1.call-start = ((), (), s32[]{:S(2)}) async-start(), calls=%async_computation.17 | async-start | bytes 7962624
  800.4 3.7 copy-start.11
  817.0 175.2 %reduce-scatter.17.cloned.1.call-start = ((), (), s32[]{:S(2)}) async-start(), calls=%async_computation.16 | async-start | bytes 10616832 | tf_op jit(solution)/shard_map/reduce_scatter | solution.py:334
  830.6 261.9 %reduce-scatter.15.cloned.1.call-start = ((), (), s32[]{:S(2)}) async-start(), calls=%async_computation.15 | async-start | bytes 10616832 | tf_op jit(solution)/shard_map/reduce_scatter | solution.py:333
  842.1 8.9 copy-start.17
  842.1 285.1 %reduce-scatter.23.cloned.1.call-start = ((), (), s32[]{:S(2)}) async-start(), calls=%async_computation.19 | async-start | bytes 1769472
  855.4 320.1 %reduce-scatter.21.cloned.1.call-start = ((), (), s32[]{:S(2)}) async-start(), calls=%async_computation.18 | async-start | bytes 442368
  855.5 4.8 copy-start.28
  855.5 4.8 copy-start.29
  864.1 365.2 %all-reduce.5.cloned.1.call-start = ((), (), s32[]{:S(2)}) async-start(), calls=%async_computation.20 | async-start | bytes 3833856 | tf_op jit(solution)/shard_map/psum | solution.py:339
  994.4 103.4 %copy-start.21 = (f32[768]{0:T(1024)S(1)}, f32[768]{0:T(1024)}, u32[]{:S(2)}) copy-start(f32[768]{0:T(1024)} %copy-done.20) | copy-start | bytes 9220
  1094.6 5.5 copy-start.49
  1173.6 62.9 %copy-start.1 = (s32[8,2]{0,1:T(2,128)S(1)}, s32[8,2]{0,1:T(2,128)}, u32[]{:S(2)}) copy-start(s32[8,2]{0,1:T(2,128)} %param.55) | copy-start | bytes 196
  1229.3 6.1 copy-start.12
  (54 other events, 115.6 us)
Sparse Core Ops, SparseCore 0:
  9.7 44.2 all-gather.4
  55.6 21.5 all-gather.6
  78.8 51.4 all-gather.8
  131.8 50.5 all-gather.10
  391.8 35.7 reduce-scatter.12
  817.2 74.8 reduce-scatter.18
  894.3 97.8 reduce-scatter.16
  994.5 97.8 reduce-scatter.14
  1094.7 32.4 reduce-scatter.22
  1129.3 28.9 reduce-scatter.20
  1163.4 65.8 all-reduce.4
where the time goes:
time: 1250 us; the launch traced here: 1240 us
  waiting for transfers between devices  390 us (31%)
  matrix products  353 us (28%)
  local copies, waits for them, and re-layouts  183 us (15%)
  blocking collectives  125 us (10%)
  other arithmetic  91.3 us (7%)
  loops' own time  72.2 us (6%)
  between operations  16.1 us (1%)
  starting transfers between devices  12.9 us (1%)
    reduce_scatter x1, waiting for transfers between devices, local(): lax.psum_scatter(expand_weight_grad, 'wt', scatter_dimension=0, tiled=True)  98 us
    reduce_scatter x1, waiting for transfers between devices, local(): lax.psum_scatter(contract_weight_grad, 'wt', scatter_dimension=0, tiled=T...  97.9 us
    dot_general x36, matrix products, masked_scores(): jnp.einsum('qd,kd->qk', query_rows, keys_all, preferred_element_type=jnp....  96.3 us
    all_to_all x1, blocking collectives, local(): lax.all_to_all(returning, 'seq', split_axis=0, concat_axis=1, tiled=True)  76.7 us
    unnamed x14, waiting for transfers between devices  55.6 us
    unnamed x119, local copies, waits for them, and re-layouts  47.3 us
    psum x1, waiting for transfers between devices, local(): lax.psum(pieces[0].astype(jnp.bfloat16), 'seq').astype(jnp.float32)  41.5 us
    all_gather x1, waiting for transfers between devices, local(): lax.all_gather(attention_weight, 'wt', axis=0, tiled=True)  40 us
  transfers between devices with their start and end apart: 14, of which 9 were waited for; matrix products, arithmetic and copies ran while one was open for 45% of the time, Pallas kernels for 0%

commit v1 on v0

v1 whole, which is shorter than its diff:
```python
import functools

import jax
import jax.numpy as jnp
from jax import lax
from jax.experimental import pallas as pl
from jax.experimental.pallas import tpu as pltpu
from jax.sharding import PartitionSpec as P

PROMPT = 1024
GRP_WT = 1
GLEN = 3072
SHORT = 512
LONG = 1536
HD = 64
TQ = 512
KC = 512

epsilon = 1e-06
score_scale = 0.125
exp2_scale = 0.125 * 1.4426950408889634
root_half = 0.7071067811865476
density_scale = 0.3989422804014327
bf16 = jnp.bfloat16
f32 = jnp.float32

NT = (((1,), (1,)), ((), ()))
NN = (((1,), (0,)), ((), ()))


def mm(a, b, dims=NN):
    return lax.dot_general(a, b, dims, preferred_element_type=f32)


def query_tiles(short_first, tile):
    short_at = pl.multiple_of(jnp.where(short_first, PROMPT, PROMPT + LONG), SHORT)
    long_at = pl.multiple_of(jnp.where(short_first, PROMPT + SHORT, PROMPT), SHORT)
    for base, own_at, own_len, rows in (
        (0, 0, 0, PROMPT),
        (short_at, short_at, SHORT, SHORT),
        (long_at, long_at, LONG, LONG),
    ):

        def step(i, carry, base=base, own_at=own_at, own_len=own_len):
            tile(pl.multiple_of(base + i * TQ, TQ), own_at, own_len)
            return carry

        lax.fori_loop(0, rows // TQ, step, 0)


def attend_kernel(
    heads, lens_ref, tok_ref, w_ref, vec_ref, packed_ref, ctx_ref, lse_ref, q_sc, k_sc, vt_sc, ot_sc
):
    def project(i, carry):
        rows = pl.ds(pl.multiple_of(i * TQ, TQ), TQ)
        x = mm(tok_ref[rows, :], w_ref[...]) + vec_ref[0:1, :]
        x = (x * vec_ref[1:2, :]).astype(bf16)
        packed_ref[rows, :] = x
        for h in range(heads):
            at = 3 * HD * h
            q_sc[h, rows, :] = x[:, at : at + HD]
            k_sc[h, rows, :] = x[:, at + HD : at + 2 * HD]
            vt_sc[h, 0:HD, rows] = x[:, at + 2 * HD : at + 3 * HD].T
        return carry

    lax.fori_loop(0, GLEN // TQ, project, 0)
    for h in range(heads):
        vt_sc[h, HD : HD + 16, :] = jnp.ones((16, GLEN), bf16)

    def one_head(h, carry):
        def tile(q_at, own_at, own_len):
            rows = pl.ds(q_at, TQ)
            q = q_sc[h, rows, :]
            s1 = mm(k_sc[h, 0:PROMPT, :], q, NT)
            top = jnp.max(s1, axis=0, keepdims=True)
            if own_len:
                own = pl.ds(own_at, own_len)
                s2 = mm(k_sc[h, own, :], q, NT)
                top = jnp.maximum(top, jnp.max(s2, axis=0, keepdims=True))
            top = top * exp2_scale
            p1 = jnp.exp2(s1 * exp2_scale - top)
            o = mm(vt_sc[h, :, 0:PROMPT], p1.astype(bf16))
            total = jnp.sum(p1, axis=0, keepdims=True)
            if own_len:
                p2 = jnp.exp2(s2 * exp2_scale - top)
                o = o + mm(vt_sc[h, :, own], p2.astype(bf16))
                total = total + jnp.sum(p2, axis=0, keepdims=True)
            ot_sc[h, :, rows] = o[0:HD, :] / total
            lse_ref[h, :, rows] = top + jnp.log2(total)

        query_tiles(lens_ref[0] == SHORT, tile)
        return carry

    lax.fori_loop(0, heads, one_head, 0)

    def place(i, carry):
        rows = pl.ds(pl.multiple_of(i * TQ, TQ), TQ)
        for h in range(heads):
            ctx_ref[rows, HD * h : HD * (h + 1)] = ot_sc[h, :, rows].T.astype(bf16)
        return carry

    lax.fori_loop(0, GLEN // TQ, place, 0)


def attend(lens, tokens_all, weight, vec, heads):
    width = 3 * HD * heads
    whole = pl.BlockSpec(memory_space=pltpu.VMEM)
    return pl.pallas_call(
        functools.partial(attend_kernel, heads),
        out_shape=(
            jax.ShapeDtypeStruct((GLEN, width), bf16),
            jax.ShapeDtypeStruct((GLEN, HD * heads), bf16),
            jax.ShapeDtypeStruct((heads, 1, GLEN), f32),
        ),
        in_specs=[pl.BlockSpec(memory_space=pltpu.SMEM), whole, whole, whole],
        out_specs=(whole, whole, whole),
        scratch_shapes=[
            pltpu.VMEM((heads, GLEN, HD), bf16),
            pltpu.VMEM((heads, GLEN, HD), bf16),
            pltpu.VMEM((heads, HD + 16, GLEN), bf16),
            pltpu.VMEM((heads, HD, GLEN), f32),
        ],
        compiler_params=pltpu.CompilerParams(vmem_limit_bytes=56 * 2**20),
        cost_estimate=pl.CostEstimate(
            flops=2 * GLEN * 768 * width + heads * 4 * 256 * 5767168,
            bytes_accessed=2 * GLEN * (768 + width),
            transcendentals=heads * 5767168,
        ),
        name="attend",
    )(lens, tokens_all, weight, vec)


def attend_back_kernel(
    heads, lens_ref, packed_ref, ctx_ref, gctx_ref, lse_ref, scale_ref,
    out_ref, sums_ref, gate_ref,
    q_sc, k_sc, v_sc, kt_sc, g_sc, delta_sc, dqt_sc, dk_sc, dv_sc,
):
    def split(i, carry):
        rows = pl.ds(pl.multiple_of(i * TQ, TQ), TQ)
        x = packed_ref[rows, :]
        g = gctx_ref[rows, :]
        inner = (g.astype(f32) * ctx_ref[rows, :].astype(f32)).T
        for h in range(heads):
            at = 3 * HD * h
            q_sc[h, rows, :] = x[:, at : at + HD]
            k = x[:, at + HD : at + 2 * HD]
            k_sc[h, rows, :] = k
            kt_sc[h, :, rows] = k.T
            v_sc[h, rows, :] = x[:, at + 2 * HD : at + 3 * HD]
            g_sc[h, rows, :] = g[:, HD * h : HD * (h + 1)]
            delta_sc[h, :, rows] = jnp.sum(inner[HD * h : HD * (h + 1), :], axis=0, keepdims=True)
        return carry

    lax.fori_loop(0, GLEN // TQ, split, 0)
    dk_sc[...] = jnp.zeros_like(dk_sc)
    dv_sc[...] = jnp.zeros_like(dv_sc)

    def one_head(h, carry):
        def tile(q_at, own_at, own_len):
            rows = pl.ds(q_at, TQ)
            q = q_sc[h, rows, :]
            g = g_sc[h, rows, :]
            lse = lse_ref[h, :, rows]
            delta = delta_sc[h, :, rows]
            dq = jnp.zeros((HD, TQ), f32)
            pieces = [(j * KC, PROMPT // KC) for j in range(PROMPT // KC)]
            pieces = [c for c, _ in pieces] + [own_at + j * KC for j in range(own_len // KC)]
            for start in pieces:
                keys = pl.ds(start, KC)
                s = mm(k_sc[h, keys, :], q, NT)
                p = jnp.exp2(s * exp2_scale - lse)
                dp = mm(v_sc[h, keys, :], g, NT)
                ds = (p * (dp - delta)).astype(bf16)
                dv_sc[h, keys, :] += mm(p.astype(bf16), g)
                dk_sc[h, keys, :] += mm(ds, q)
                dq = dq + mm(kt_sc[h, :, keys], ds)
            dqt_sc[h, :, rows] = dq * score_scale

        query_tiles(lens_ref[0] == SHORT, tile)
        return carry

    lax.fori_loop(0, heads, one_head, 0)
    sums_ref[...] = jnp.zeros_like(sums_ref)
    gate_ref[...] = jnp.zeros_like(gate_ref)

    def place(i, carry):
        rows = pl.ds(pl.multiple_of(i * TQ, TQ), TQ)
        for h in range(heads):
            at = 3 * HD * h
            dq = dqt_sc[h, :, rows].T.astype(bf16)
            dk = (dk_sc[h, rows, :] * score_scale).astype(bf16)
            dv = dv_sc[h, rows, :].astype(bf16).astype(f32)
            gate_ref[0:1, HD * h : HD * (h + 1)] += jnp.sum(
                dv * v_sc[h, rows, :].astype(f32), axis=0, keepdims=True
            )
            dv = (dv * scale_ref[:, at + 2 * HD : at + 3 * HD]).astype(bf16)
            out_ref[rows, at : at + HD] = dq
            out_ref[rows, at + HD : at + 2 * HD] = dk
            out_ref[rows, at + 2 * HD : at + 3 * HD] = dv
            sums_ref[0:1, at : at + HD] += jnp.sum(dq.astype(f32), axis=0, keepdims=True)
            sums_ref[0:1, at + 2 * HD : at + 3 * HD] += jnp.sum(
                dv.astype(f32), axis=0, keepdims=True
            )
        return carry

    lax.fori_loop(0, GLEN // TQ, place, 0)


def attend_back(lens, packed, ctx, gctx, lse, scale, heads):
    width = 3 * HD * heads
    whole = pl.BlockSpec(memory_space=pltpu.VMEM)
    rows64 = pltpu.VMEM((heads, GLEN, HD), bf16)
    rows64f = pltpu.VMEM((heads, GLEN, HD), f32)
    return pl.pallas_call(
        functools.partial(attend_back_kernel, heads),
        out_shape=(
            jax.ShapeDtypeStruct((GLEN, width), bf16),
            jax.ShapeDtypeStruct((8, width), f32),
            jax.ShapeDtypeStruct((8, HD * heads), f32),
        ),
        in_specs=[pl.BlockSpec(memory_space=pltpu.SMEM)] + [whole] * 5,
        out_specs=(whole, whole, whole),
        scratch_shapes=[
            rows64,
            rows64,
            rows64,
            pltpu.VMEM((heads, HD, GLEN), bf16),
            rows64,
            pltpu.VMEM((heads, 1, GLEN), f32),
            pltpu.VMEM((heads, HD, GLEN), f32),
            rows64f,
            rows64f,
        ],
        compiler_params=pltpu.CompilerParams(vmem_limit_bytes=56 * 2**20),
        cost_estimate=pl.CostEstimate(
            flops=heads * 10 * 256 * 5767168,
            bytes_accessed=2 * GLEN * (3 * width),
            transcendentals=heads * 5767168,
        ),
        name="attend_back",
    )(lens, packed, ctx, gctx, lse, scale)


def norm_parts(summed):
    centre = summed - jnp.mean(summed, axis=-1, keepdims=True)
    inverse = lax.rsqrt(jnp.mean(centre * centre, axis=-1, keepdims=True) + epsilon)
    return (centre * inverse, inverse)


def norm_back(grad_normed, normed, inverse):
    return inverse * (
        grad_normed
        - jnp.mean(grad_normed, axis=-1, keepdims=True)
        - normed * jnp.mean(grad_normed * normed, axis=-1, keepdims=True)
    )


def local(
    tokens,
    output_cotangent,
    attention_weight,
    query_bias,
    value_bias,
    output_weight,
    output_bias,
    first_gain,
    first_shift,
    expand_weight,
    expand_bias,
    contract_weight,
    contract_bias,
    second_gain,
    second_shift,
    head_gate,
    hidden_gate,
    unit_gate,
    head_mask,
    hidden_mask,
    unit_mask,
    attention_mask,
    feedforward_mask,
    continuation_lengths,
):
    row_count = tokens.shape[0]
    seq_count = lax.axis_size("seq")
    head_count = head_gate.shape[0]
    model_width = hidden_gate.shape[0]
    head_size = model_width // head_count
    local_heads = head_count // seq_count
    seq_index = lax.axis_index("seq")
    wt_index = lax.axis_index("wt")
    local_width = 3 * head_size * local_heads
    tokens_all = lax.all_gather(tokens, "seq", axis=0, tiled=True)
    own_columns = lax.dynamic_slice_in_dim(attention_weight, seq_index * local_width, local_width, 1)
    own_weight = lax.all_gather(own_columns, "wt", axis=0, tiled=True)
    full_output, full_expand, full_contract, full_attention = (
        lax.all_gather(output_weight, "wt", axis=0, tiled=True),
        lax.all_gather(expand_weight, "wt", axis=0, tiled=True),
        lax.all_gather(contract_weight, "wt", axis=0, tiled=True),
        lax.all_gather(attention_weight, "wt", axis=0, tiled=True),
    )
    position = seq_index * row_count + jnp.arange(row_count, dtype=jnp.int32)
    group_local = position // GLEN
    own_groups = jnp.arange(GRP_WT, dtype=jnp.int32)
    chosen = group_local[:, None] == own_groups[None, :]
    first_group = wt_index * GRP_WT
    own_attention = lax.dynamic_slice_in_dim(attention_mask, first_group, GRP_WT, 0).astype(
        jnp.float32
    )
    own_feedforward = lax.dynamic_slice_in_dim(feedforward_mask, first_group, GRP_WT, 0).astype(
        jnp.float32
    )
    attention_rows = jnp.sum(jnp.where(chosen, own_attention[None, :], 0.0), axis=1)
    feedforward_rows = jnp.sum(jnp.where(chosen, own_feedforward[None, :], 0.0), axis=1)
    head_scale = head_mask.astype(jnp.float32) * head_gate
    hidden_scale = hidden_mask.astype(jnp.float32) * hidden_gate
    unit_scale = unit_mask.astype(jnp.float32) * unit_gate
    first_gain_f = first_gain.astype(jnp.float32)
    second_gain_f = second_gain.astype(jnp.float32)
    bias_table = jnp.stack(
        [
            query_bias.astype(jnp.float32).reshape(head_count, head_size),
            jnp.zeros((head_count, head_size), jnp.float32),
            value_bias.astype(jnp.float32).reshape(head_count, head_size),
        ],
        axis=1,
    )
    own_scale = lax.dynamic_slice_in_dim(head_scale, seq_index * local_heads, local_heads, 0)
    own_scale = own_scale * own_attention[0]
    own_mask = lax.dynamic_slice_in_dim(head_mask, seq_index * local_heads, local_heads, 0)
    own_gate = lax.dynamic_slice_in_dim(head_gate, seq_index * local_heads, local_heads, 0)
    own_bias = lax.dynamic_slice_in_dim(bias_table, seq_index * local_heads, local_heads, 0)
    constant = jnp.ones((local_heads, head_size), jnp.float32)
    factor = jnp.stack([constant, constant, constant * own_scale[:, None]], axis=1)
    vec = jnp.stack([own_bias.reshape(local_width), factor.reshape(local_width)], axis=0)
    lens = lax.dynamic_slice_in_dim(continuation_lengths, first_group, GRP_WT, 0)[0]
    packed, mixed_heads, log_sums = attend(lens, tokens_all, own_weight, vec, local_heads)
    context = lax.all_to_all(
        mixed_heads.reshape(GLEN, 1, local_heads * head_size), "seq", split_axis=0, concat_axis=1, tiled=True
    ).reshape(row_count, model_width)
    attn_out = jnp.dot(
        context, full_output, preferred_element_type=jnp.float32
    ) + output_bias.astype(jnp.float32)
    normed_one, inverse_one = norm_parts(tokens.astype(jnp.float32) + attn_out)
    shaped_one = normed_one * first_gain_f + first_shift.astype(jnp.float32)
    first_out = shaped_one * hidden_scale
    first_low = first_out.astype(jnp.bfloat16)
    hidden = jnp.dot(
        first_low, full_expand, preferred_element_type=jnp.float32
    ) + expand_bias.astype(jnp.float32)
    gelu_out = jax.nn.gelu(hidden, approximate=False)
    unit_rows_scale = unit_scale[None, :] * feedforward_rows[:, None]
    activated = (gelu_out * unit_rows_scale).astype(jnp.bfloat16)
    branch = jnp.dot(
        activated, full_contract, preferred_element_type=jnp.float32
    ) + contract_bias.astype(jnp.float32)
    normed_two, inverse_two = norm_parts(first_out + branch)
    shaped_two = normed_two * second_gain_f + second_shift.astype(jnp.float32)
    layer_output = (shaped_two * hidden_scale).astype(jnp.bfloat16)
    back_attention, back_output, back_expand, back_contract = (
        full_attention,
        full_output,
        full_expand,
        full_contract,
    )
    cotangent = output_cotangent.astype(jnp.float32)
    grad_shaped_two = cotangent * hidden_scale
    second_gain_grad = jnp.sum(grad_shaped_two * normed_two, axis=0)
    second_shift_grad = jnp.sum(grad_shaped_two, axis=0)
    grad_total_two = norm_back(grad_shaped_two * second_gain_f, normed_two, inverse_two)
    grad_branch = grad_total_two.astype(jnp.bfloat16)
    contract_bias_grad = jnp.sum(grad_branch.astype(jnp.float32), axis=0)
    contract_weight_grad = jnp.einsum(
        "ti,td->id", activated, grad_branch, preferred_element_type=jnp.float32
    )
    grad_activated = jnp.einsum(
        "td,id->ti", grad_branch, back_contract, preferred_element_type=jnp.float32
    )
    unit_gate_grad = unit_mask.astype(jnp.float32) * jnp.sum(
        grad_activated * gelu_out * feedforward_rows[:, None], axis=0
    )
    cumulative = 0.5 * (1.0 + lax.erf(hidden * root_half))
    gelu_slope = cumulative + hidden * jnp.exp(-0.5 * hidden * hidden) * density_scale
    grad_hidden = (grad_activated * unit_rows_scale * gelu_slope).astype(jnp.bfloat16)
    expand_bias_grad = jnp.sum(grad_hidden.astype(jnp.float32), axis=0)
    expand_weight_grad = jnp.einsum(
        "td,tf->df", first_low, grad_hidden, preferred_element_type=jnp.float32
    )
    grad_first = grad_total_two + jnp.einsum(
        "tf,df->td", grad_hidden, back_expand, preferred_element_type=jnp.float32
    )
    grad_shaped_one = grad_first * hidden_scale
    first_gain_grad = jnp.sum(grad_shaped_one * normed_one, axis=0)
    first_shift_grad = jnp.sum(grad_shaped_one, axis=0)
    hidden_gate_grad = hidden_mask.astype(jnp.float32) * jnp.sum(
        cotangent * shaped_two + grad_first * shaped_one, axis=0
    )
    grad_total_one = norm_back(grad_shaped_one * first_gain_f, normed_one, inverse_one)
    grad_attn = grad_total_one.astype(jnp.bfloat16)
    output_bias_grad = jnp.sum(grad_attn.astype(jnp.float32), axis=0)
    output_weight_grad = jnp.einsum(
        "ti,td->id", context, grad_attn, preferred_element_type=jnp.float32
    )
    grad_context = jnp.einsum(
        "td,id->ti", grad_attn, back_output, preferred_element_type=jnp.float32
    ).astype(jnp.bfloat16)
    arriving = lax.all_to_all(
        grad_context.reshape(row_count, seq_count, local_heads * head_size),
        "seq",
        split_axis=1,
        concat_axis=0,
        tiled=True,
    )
    grad_packed, sums, gate_sums = attend_back(
        lens,
        packed,
        mixed_heads,
        arriving.reshape(GLEN, local_heads * head_size),
        log_sums,
        vec[1:2],
        local_heads,
    )
    head_own = own_mask.astype(jnp.float32) * own_attention[0] / own_gate
    head_own = head_own * jnp.sum(gate_sums[0].reshape(local_heads, head_size), axis=1)
    head_partial = lax.dynamic_update_slice_in_dim(
        jnp.zeros((head_count,), jnp.float32), head_own, seq_index * local_heads, 0
    )
    sums = sums[0].reshape(local_heads, 3, head_size)
    zeros_wide = jnp.zeros((model_width,), jnp.float32)
    at_own = seq_index * local_heads * head_size
    query_bias_grad = lax.dynamic_update_slice_in_dim(zeros_wide, sums[:, 0].reshape(-1), at_own, 0)
    value_bias_grad = lax.dynamic_update_slice_in_dim(zeros_wide, sums[:, 2].reshape(-1), at_own, 0)
    grad_flat = lax.all_to_all(
        grad_packed.reshape(GLEN, 1, local_width), "seq", split_axis=0, concat_axis=1, tiled=True
    ).reshape(row_count, 3 * model_width)
    attention_weight_grad = jnp.einsum(
        "td,tc->dc", tokens_all, grad_packed, preferred_element_type=jnp.float32
    )
    tokens_grad = grad_total_one + jnp.einsum(
        "tc,dc->td", grad_flat, back_attention, preferred_element_type=jnp.float32
    )
    head_gate_grad = lax.psum(head_partial, ("seq", "wt"))
    width_vectors = jnp.stack(
        [
            query_bias_grad,
            value_bias_grad,
            output_bias_grad,
            first_gain_grad,
            first_shift_grad,
            contract_bias_grad,
            second_gain_grad,
            second_shift_grad,
            hidden_gate_grad,
        ],
        axis=1,
    )
    unit_vectors = jnp.stack([expand_bias_grad, unit_gate_grad], axis=1)
    pieces = (
        lax.psum_scatter(attention_weight_grad.astype(bf16), "wt", scatter_dimension=0, tiled=True),
        lax.psum_scatter(output_weight_grad.astype(bf16), "wt", scatter_dimension=0, tiled=True),
        lax.psum_scatter(expand_weight_grad.astype(bf16), "wt", scatter_dimension=0, tiled=True),
        lax.psum_scatter(contract_weight_grad.astype(bf16), "wt", scatter_dimension=0, tiled=True),
        lax.psum_scatter(width_vectors, "wt", scatter_dimension=0, tiled=True),
        lax.psum_scatter(unit_vectors, "wt", scatter_dimension=0, tiled=True),
    )
    shards = (
        lax.all_gather(pieces[0], "seq", axis=1, tiled=True).astype(jnp.float32),
        lax.psum(pieces[1], "seq").astype(jnp.float32),
        lax.psum(pieces[2], "seq").astype(jnp.float32),
        lax.psum(pieces[3], "seq").astype(jnp.float32),
        lax.psum(pieces[4], "seq"),
        lax.psum(pieces[5], "seq"),
    )
    width_shard = shards[4]
    unit_shard = shards[5]
    return (
        layer_output,
        tokens_grad,
        shards[0],
        width_shard[:, 0],
        width_shard[:, 1],
        shards[1],
        width_shard[:, 2],
        width_shard[:, 3],
        width_shard[:, 4],
        shards[2],
        unit_shard[:, 0],
        shards[3],
        width_shard[:, 5],
        width_shard[:, 6],
        width_shard[:, 7],
        head_gate_grad,
        width_shard[:, 8],
        unit_shard[:, 1],
    )


def solution(mesh):
    return jax.shard_map(
        local,
        mesh=mesh,
        in_specs=(
            P(("wt", "seq"), None),
            P(("wt", "seq"), None),
            P("wt", None),
            P(),
            P(),
            P("wt", None),
            P(),
            P(),
            P(),
            P("wt", None),
            P(),
            P("wt", None),
            P(),
            P(),
            P(),
            P(),
            P(),
            P(),
            P(),
            P(),
            P(),
            P(),
            P(),
            P(),
        ),
        out_specs=(
            P(("wt", "seq"), None),
            P(("wt", "seq"), None),
            P("wt", None),
            P("wt"),
            P("wt"),
            P("wt", None),
            P("wt"),
            P("wt"),
            P("wt"),
            P("wt", None),
            P("wt"),
            P("wt", None),
            P("wt"),
            P("wt"),
            P("wt"),
            P(),
            P("wt"),
            P("wt"),
        ),
        check_vma=False,
    )
```

time: 1250 us -> 610 us (0.49)
  matrix products: 353 us -> 105 us
  waiting for transfers between devices: 390 us -> 169 us
  Pallas kernels: 0 us -> 104 us
  local copies, waits for them, and re-layouts: 183 us -> 82.8 us
  loops' own time: 72.2 us -> 0 us
  other arithmetic: 91.3 us -> 26.5 us
  blocking collectives: 125 us -> 83.9 us
    dot_general x128 -> x1, matrix products: 247 us -> 6.59 us  [local(): jnp.einsum('td,tc->dc', tokens_all, grad_packed, preferred_element_type=j...]
    reduce_scatter x3, waiting for transfers between devices: 196 us -> 3.96 us  [the longest x1 3.93 us: local(): lax.psum_scatter(contract_weight_grad.astype(bf16), 'wt', scatter_dimensi...]
    pallas_call x0 -> x2, Pallas kernels: none -> 104 us  [the longest x1 61.2 us: attend_back(): pl.pallas_call(functools.partial(attend_back_kernel, heads), out_shape=(j...]
    all_to_all x1 -> x0, blocking collectives: 76.7 us -> none  [local(): lax.all_to_all(returning, 'seq', split_axis=0, concat_axis=1, tiled=True)]
    another operation x8 -> x0, loops' own time: 72.2 us -> none  [the longest x3 36.2 us: head_backward(): lax.scan(one_block, (zero_rows, zero_rows), offsets)]
    dynamic_slice x100 -> x2, local copies, waits for them, and re-layouts: 48.6 us -> 1.71 us  [the longest x1 1.01 us: local(): lax.dynamic_slice_in_dim(attention_weight, seq_index * local_width, local...]
    convert_element_type x29 -> x3, other arithmetic: 48.1 us -> 5.1 us  [the longest x1 2.21 us: local(): lax.psum(pieces[2], 'seq').astype(jnp.float32)]
    all_to_all x2, waiting for transfers between devices: 46.9 us -> 5.69 us  [the longest x1 5.69 us: local(): lax.all_to_all(mixed_heads.reshape(GLEN, 1, local_heads * head_size), 'se...]
  transfers between devices with their start and end apart: 14 -> 15, of which waited for: 9 -> 9; matrix products, arithmetic and copies ran while one was open for 45% -> 26% of each run, Pallas kernels for 0% -> 17%
where the time goes in v1:
time: 610 us; the launch traced here: 600 us
  waiting for transfers between devices  169 us (28%)
  matrix products  105 us (17%)
  Pallas kernels  104 us (17%)
  blocking collectives  83.9 us (14%)
  local copies, waits for them, and re-layouts  82.8 us (14%)
  other arithmetic  26.5 us (4%)
  between operations  16.9 us (3%)
  starting transfers between devices  12.3 us (2%)
    pallas_call x1, Pallas kernels, attend_back(): pl.pallas_call(functools.partial(attend_back_kernel, heads), out_shape=(j...  61.2 us
    psum x1, waiting for transfers between devices, local(): lax.psum(pieces[1], 'seq').astype(jnp.float32)  51 us
    unnamed x130, local copies, waits for them, and re-layouts  50.9 us
    unnamed x15, waiting for transfers between devices  43.4 us
    pallas_call x1, Pallas kernels, attend(): pl.pallas_call(functools.partial(attend_kernel, heads), out_shape=(jax.Sh...  42.3 us
    psum x1, blocking collectives, local(): head_gate_grad = lax.psum(head_partial, ('seq', 'wt'))  37.9 us
    all_gather x1, waiting for transfers between devices, local(): tokens_all = lax.all_gather(tokens, 'seq', axis=0, tiled=True)  36.5 us
    dot_general x1, matrix products, local(): jnp.dot(first_low, full_expand, preferred_element_type=jnp.float32)  30.7 us
  transfers between devices with their start and end apart: 15, of which 9 were waited for; matrix products, arithmetic and copies ran while one was open for 26% of the time, Pallas kernels for 17%

profile of v1, /device:TPU:0, one launch (start us, length us, event | category | flops | bytes accessed | tf_op | source)
XLA Modules:
  0.0 599.9 jit_solution(7534870663527069977)
XLA Ops:
  13.0 18.9 %all_gather.22.w_ref = bf16[768,576]{1,0:T(8,128)(2,1)} all-gather(bf16[96,576]{1,0:T(8,128)(2,1)S(1)} %constant_dynamic-slice_fusion), channel_id=1, replica_groups=mesh['seq'=4,'wt'=8] {'wt'}, dimensions={0}, use_global_device_ids=true | all-gather | bytes 995328 | tf_op jit(solution)/shard_map/all_gather | solution.py:295
  33.2 36.5 %all-gather.7.cloned.1.call-done.tok_ref = bf16[3072,768]{1,0:T(8,128)(2,1)} async-done(((bf16[768,768]{1,0:T(8,128)(2,1)}), bf16[3072,768]{1,0:T(8,128)(2,1)}) %all-gather.7.cloned.1.call-update) | async-done | bytes 4718608 | tf_op jit(solution)/shard_map/all_gather | solution.py:293
  69.7 42.3 %attend.1 = (bf16[3072,576]{1,0:T(8,128)(2,1)}, bf16[3072,192]{1,0:T(8,128)(2,1)}, f32[3,1,3072]{2,1,0:T(1,128)}) custom-call(s32[2]{0:T(128)} %dynamic-slice_reduce_fusion.lens_ref, bf16[3072,768]{1,0:T(8,128)(2,1)} %all-gather.7.cloned.1.call-done.tok_ref, bf16[768,576]{1,0:T(8,128)(2,1)} %all_gather.22.w_ref, f32[2,576]{1,0:T(2,128)} %pad_maximum_fusion.1.vec_ref), custom_call_target="tpu_custom_call" | custom-call | flops 20434649088 | bytes 8257536 | tf_op jit(solution)/shard_map/attend/pallas_call | solution.py:108
  112.6 3.1 reduce.16
  115.7 2.9 reshape.167
  118.6 4.4 all-to-all-start
  132.7 5.7 all-to-all-done
  138.4 3.5 reshape.168
  141.9 6.0 %copy.75 = bf16[3072,1,192]{0,2,1:T(8,128)(2,1)} copy(bf16[3072,1,192]{2,1,0:T(2,128)(2,1)S(1)} %reshape.168) | data formatting | bytes 2359296 | tf_op jit(solution)/shard_map/all_to_all | solution.py:338
  148.0 2.7 all_to_all.34
  150.8 2.9 fusion.44
  155.2 30.7 %fusion.4 = (f32[768,3072]{1,0:T(8,128)}, f32[768,3072]{1,0:T(8,128)}) fusion(f32[3072]{0:T(1024)} %convert_element_type.114, bf16[768,3072]{1,0:T(8,128)(2,1)} %all-gather.11.cloned.1.call-done, f32[768]{0:T(1024)S(1)} %convert_multiply_fusion.5, f32[768]{0:T(1024)} %convert_element_type.111, f32[768]{0:T(1024)} %convert_element_type.110, ...), kind=kOutput, calls=%fused_computation.8 | convolution fusion | flops 3780771840 | bytes 25979904 | tf_op jit(solution)/shard_map/dot_general | solution.py:348
  185.9 13.4 %all-gather.13.cloned.1.call-done = bf16[3072,768]{1,0:T(8,128)(2,1)} async-done(((bf16[384,768]{1,0:T(8,128)(2,1)}), bf16[3072,768]{1,0:T(8,128)(2,1)}) %all-gather.13.cloned.1.call-update) | async-done | bytes 4718608 | tf_op jit(solution)/shard_map/all_gather | solution.py:299
  199.3 10.0 %fusion.45 = (f32[768]{0:T(1024)S(1)}, f32[768,768]{0,1:T(8,128)S(1)}) fusion(f32[768]{0:T(1024)} %convert_element_type.118, bf16[3072,768]{1,0:T(8,128)(2,1)} %all-gather.13.cloned.1.call-done, f32[768,3072]{1,0:T(8,128)} %get-tuple-element.139, f32[768]{0:T(1024)} %fusion.32, f32[3072]{0:T(1024)} %convert_multiply_fusion.3, ...), kind=kOutput, calls=%fused_computation.121 | convolution fusion | flops 3635674368 | bytes 18911232 | tf_op jit(solution)/shard_map/dot_general | solution.py:354
  211.3 1.8 convert_reduce_fusion.1
  213.2 16.1 %convert_reduce_fusion = (f32[3072]{0:T(1024)}, bf16[768,3072]{1,0:T(8,128)(2,1)}, f32[3072]{0:T(1024)}) fusion(f32[768,3072]{1,0:T(8,128)} %get-tuple-element.140, f32[3072]{0:T(1024)S(1)} %copy-done.20, f32[768]{0:T(1024)S(1)} %copy-done.30, f32[3072]{0:T(1024)S(1)} %copy-done.22, f32[768,3072]{1,0:T(8,128)} %get-tuple-element.139, ...), kind=kOutput, calls=%fused_computation.14 | convolution fusion | flops 3666929664 | bytes 30723072 | tf_op jit(solution)/shard_map/td,id->ti/dot_general | solution.py:376
  229.4 9.4 %fusion.27 = (f32[768]{0:T(1024)}, f32[768]{0:T(1024)S(1)}, f32[768]{0:T(1024)}, f32[768]{0:T(1024)}, f32[768]{0:T(1024)S(1)}, /*index=5*/f32[768]{0:T(1024)}, f...) fusion(bf16[768,768]{0,1:T(8,128)(2,1)S(1)} %copy-done.2, f32[768,768]{0,1:T(8,128)S(1)} %get-tuple-element.142, ...), kind=kOutput, calls=%fused_computation.45 | convolution fusion | flops 3640388352 | bytes 21282816 | tf_op jit(solution)/shard_map/tf,df->td/dot_general | solution.py:389
  241.9 2.2 convolution_convert_fusion.3
  244.1 8.5 %convolution_convert_fusion.1 = bf16[768,3072]{1,0:T(8,128)(2,1)} fusion(bf16[768,3072]{1,0:T(8,128)(2,1)} %get-tuple-element.121, f32[768]{0:T(1024)S(1)} %convert_multiply_fusion.5, f32[768]{0:T(1024)} %convert_element_type.111, f32[768]{0:T(1024)} %convert_element_type.110, f32[768]{0:T(1024)} %add_rsqrt_fusion.1, ...), kind=kOutput, calls=%fused_computation.31 | convolution fusion | flops 3629776896 | bytes 11811840 | tf_op jit(solution)/shard_map/td,tf->df/dot_general | solution.py:386
  254.3 10.2 %convolution_convert_fusion = bf16[3072,768]{1,0:T(8,128)(2,1)} fusion(f32[768,768]{0,1:T(8,128)S(1)} %copy-done.5, f32[768,3072]{1,0:T(8,128)} %get-tuple-element.139, f32[768]{0:T(1024)S(1)} %copy-done.31, f32[3072]{0:T(1024)S(1)} %copy-done.23), kind=kOutput, calls=%fused_computation.30 | convolution fusion | flops 3633905664 | bytes 16530432 | tf_op jit(solution)/shard_map/ti,td->id/dot_general | solution.py:373
  266.4 2.1 convolution_convert_fusion.2
  268.6 3.7 all-to-all-start.1
  272.3 1.8 copy.97
  274.3 13.6 %all-to-all-done.1 = bf16[768,4,192]{0,2,1:T(8,128)(2,1)S(1)} async-done(((bf16[768,4,192]{0,2,1:T(8,128)(2,1)}), bf16[768,4,192]{0,2,1:T(8,128)(2,1)S(1)}, u32[]{:S(2)}, u32[]{:S(2)}) %all-to-all-start.1) | async-done | bytes 1179680 | tf_op jit(solution)/shard_map/all_to_all | solution.py:407
  287.9 1.7 copy.80
  289.6 61.2 %attend_back.1 = (bf16[3072,576]{1,0:T(8,128)(2,1)}, f32[8,576]{1,0:T(8,128)}, f32[8,192]{1,0:T(8,128)}) custom-call(s32[2]{0:T(128)} %dynamic-slice_reduce_fusion.lens_ref, bf16[3072,576]{1,0:T(8,128)(2,1)} %get-tuple-element.25.packed_ref, bf16[3072,192]{1,0:T(8,128)(2,1)} %get-tuple-element.24.ctx_ref, bf16[3072,192]{1,0:T(8,128)(2,1)} %bitcast.69, ...), custom_call_target="tpu_custom_call" | custom-call | flops 44291850240 | bytes 10616832 | tf_op jit(solution)/shard_map/attend_back/pallas_call | solution.py:214
  353.2 6.6 %fusion.28 = bf16[768,576]{0,1:T(8,128)(2,1)S(1)} fusion(bf16[3072,576]{1,0:T(8,128)(2,1)} %get-tuple-element.27, bf16[3072,768]{1,0:T(8,128)(2,1)} %all-gather.7.cloned.1.call-done.tok_ref), kind=kOutput, calls=%fused_computation.68 | convolution fusion | flops 2718351360 | bytes 9142272 | tf_op jit(solution)/shard_map/td,tc->dc/dot_general | solution.py:436
  362.1 6.5 %reduce.17 = bf16[3072,576]{1,0:T(8,128)(2,1)} reduce(bf16[3072,1,576]{2,0,1:T(8,128)(2,1)} %bitcast.66, bf16[]{:T(256)} %broadcast.178), dimensions={1}, to_apply=%copy.81.reduce_sub_computation | reduce | bytes 7077890 | tf_op jit(solution)/shard_map/reshape | solution.py:434
  368.6 7.1 %reshape.169 = bf16[4,2,221184]{2,1,0:T(2,128)(2,1)} reshape(bf16[3072,576]{1,0:T(8,128)(2,1)} %reduce.17) | data formatting | bytes 7077888
  375.8 3.7 all-to-all-start.2
  379.6 2.4 copy.87
  382.9 3.9 reduce-scatter.17.cloned.1.call-done
  387.6 34.1 %reduce-scatter.23.cloned.1.call-done = f32[384,2]{1,0:T(8,128)} async-done(((f32[3072,2]{1,0:T(8,128)}), f32[384,2]{1,0:T(8,128)}) %reduce-scatter.23.cloned.1.call-update) | async-done | bytes 3088
  422.7 37.9 %psum.47 = f32[12]{0:T(128)} all-reduce(f32[12]{0:T(128)} %copy-done.54), channel_id=1, replica_groups=mesh['seq'=4,'wt'=8] {'seq','wt'}, use_global_device_ids=true, to_apply=%region_29.30 | all-reduce | flops 12 | bytes 96 | tf_op jit(solution)/shard_map/psum | solution.py:442
  461.4 16.7 %all-reduce.1 = (f32[96,9]{0,1:T(8,128)}, f32[384,2]{0,1:T(2,128)S(1)}) all-reduce(f32[96,9]{0,1:T(8,128)S(1)} %copy.96, f32[384,2]{0,1:T(2,128)S(1)} %copy.98), channel_id=1, replica_groups=mesh['seq'=4,'wt'=8] {'seq'}, use_global_device_ids=true, to_apply=%region_17.18 | all-reduce | flops 1632 | bytes 13056 | tf_op jit(solution)/shard_map/psum | solution.py:471
  480.2 6.0 reduce-scatter.19.cloned.1.call-done
  487.8 1.7 copy.85
  489.5 10.4 %all-gather = bf16[4,576,96]{1,2,0:T(8,128)(2,1)S(1)} all-gather(bf16[1,576,96]{1,2,0:T(8,128)(2,1)} %copy.85), channel_id=1, replica_groups=mesh['seq'=4,'wt'=8] {'seq'}, dimensions={0}, use_global_device_ids=true | all-gather | bytes 552960 | tf_op jit(solution)/shard_map/all_gather | solution.py:467
  501.2 2.7 reshape.145
  503.9 7.5 %reshape.170 = bf16[3072,1,576]{2,1,0:T(2,128)(2,1)} reshape(bf16[4,2,221184]{2,1,0:T(2,128)(2,1)S(1)} %all-to-all-done.2) | data formatting | bytes 7077888
  511.4 5.9 copy.99
  517.4 7.0 %copy.92 = bf16[4,768,1,576]{1,0,3,2:T(4,128)(2,1)S(1)} copy(bf16[4,768,1,576]{3,1,0,2:T(8,128)(2,1)} %bitcast.62) | data formatting | bytes 7077888 | tf_op jit(solution)/shard_map/all_to_all | solution.py:433
  524.4 2.2 copy.83
  527.8 6.7 %convolution_add_fusion = f32[768,768]{0,1:T(8,128)S(1)} fusion(f32[768,768]{0,1:T(8,128)} %copy-done.6, bf16[768,2304]{1,0:T(8,128)(2,1)} %all-gather.15.cloned.1.call-done, bf16[768,2304]{0,1:T(8,128)(2,1)} %bitcast.67), kind=kOutput, calls=%fused_computation.63 | convolution fusion | flops 2718498816 | bytes 11796480 | tf_op jit(solution)/shard_map/tc,dc->td/dot_general | solution.py:439
  534.5 2.0 copy.88
  536.4 51.0 %all-reduce.5.cloned.1.call-done = (bf16[96,768]{1,0:T(8,128)(2,1)}, bf16[96,3072]{1,0:T(8,128)(2,1)}, bf16[384,768]{1,0:T(8,128)(2,1)}) async-done(((bf16[96,768]{1,0:T(8,128)(2,1)}, bf16[96,3072]{1,0:T(8,128)(2,1)}, bf16[384,768]{1,0:T(8,128)(2,1)}), (bf16[96,768]{1,0:T(8,128)(2,1)}, bf16[96,3072]{1,0:T(8,128)(2,1)}, bf16[384,768]{1,0:T(8,128)(2,1)})) %all-reduce.5.cloned.1.call-update) | async-done | bytes 1327120 | tf_op jit(solution)/shard_map/psum | solution.py:468
  587.4 2.2 convert_element_type.135
  589.6 2.2 convert_element_type.138
  (220 shorter events, 41.5 us)
Async XLA Ops:
  7.2 24.7 %copy-start = (s32[8,2]{0,1:T(2,128)S(1)}, s32[8,2]{0,1:T(2,128)}, u32[]{:S(2)}) copy-start(s32[8,2]{0,1:T(2,128)} %param.47) | copy-start | bytes 196
  7.3 62.5 %all-gather.7.cloned.1.call-start = ((), (), s32[]{:S(2)}) async-start(), calls=%async_computation.9 | async-start | bytes 5898240 | tf_op jit(solution)/shard_map/all_gather | solution.py:293
  8.0 142.8 %all-gather.9.cloned.1.call-start = ((), (), s32[]{:S(2)}) async-start(), calls=%async_computation.10 | async-start | bytes 1327104 | tf_op jit(solution)/shard_map/all_gather | solution.py:297
  8.7 146.5 %all-gather.11.cloned.1.call-start = ((), (), s32[]{:S(2)}) async-start(), calls=%async_computation.11 | async-start | bytes 5308416 | tf_op jit(solution)/shard_map/all_gather | solution.py:298
  9.5 189.8 %all-gather.13.cloned.1.call-start = ((), (), s32[]{:S(2)}) async-start(), calls=%async_computation.12 | async-start | bytes 5308416 | tf_op jit(solution)/shard_map/all_gather | solution.py:299
  11.6 100.4 %copy-start.26 = (f32[1,576]{1,0:T(1,128)}, f32[1,576]{1,0:T(1,128)S(1)}, u32[]{:S(2)}) copy-start(f32[1,576]{1,0:T(1,128)S(1)} %stack_reshape.23.scale_ref) | copy-start | bytes 6916
  115.6 7.5 %copy-start.3 = (bf16[768,768]{1,0:T(8,128)(2,1)S(1)}, bf16[768,768]{1,0:T(8,128)(2,1)}, u32[]{:S(2)}) copy-start(bf16[768,768]{1,0:T(8,128)(2,1)} %param.24) | copy-start | bytes 3538948
  118.5 6.1 %copy-start.38 = (bf16[768]{0:T(1024)(128)(2,1)S(1)}, bf16[768]{0:T(1024)(128)(2,1)}, u32[]{:S(2)}) copy-start(bf16[768]{0:T(1024)(128)(2,1)} %param.30) | copy-start | bytes 4612
  118.5 6.7 %copy-start.39 = (bf16[768]{0:T(1024)(128)(2,1)S(1)}, bf16[768]{0:T(1024)(128)(2,1)}, u32[]{:S(2)}) copy-start(bf16[768]{0:T(1024)(128)(2,1)} %param.31) | copy-start | bytes 4612
  118.5 7.3 %copy-start.40 = (bf16[768]{0:T(1024)(128)(2,1)S(1)}, bf16[768]{0:T(1024)(128)(2,1)}, u32[]{:S(2)}) copy-start(bf16[768]{0:T(1024)(128)(2,1)} %param.32) | copy-start | bytes 4612
  118.5 7.9 %copy-start.27 = (bf16[3072]{0:T(1024)(128)(2,1)S(1)}, bf16[3072]{0:T(1024)(128)(2,1)}, u32[]{:S(2)}) copy-start(bf16[3072]{0:T(1024)(128)(2,1)} %param.34) | copy-start | bytes 18436
  118.5 8.5 %copy-start.53 = (s32[8]{0:T(128)S(1)}, s32[8]{0:T(128)}, u32[]{:S(2)}) copy-start(s32[8]{0:T(128)} %param.46) | copy-start | bytes 100
  118.5 9.7 %copy-start.41 = (bf16[768]{0:T(1024)(128)(2,1)S(1)}, bf16[768]{0:T(1024)(128)(2,1)}, u32[]{:S(2)}) copy-start(bf16[768]{0:T(1024)(128)(2,1)} %param.36) | copy-start | bytes 4612
  118.6 10.3 %copy-start.8 = (bf16[768,768]{1,0:T(8,128)(2,1)S(1)}, bf16[768,768]{1,0:T(8,128)(2,1)}, u32[]{:S(2)}) copy-start(bf16[768,768]{1,0:T(8,128)(2,1)} %param.25) | copy-start | bytes 3538948
  118.6 19.8 %all-to-all-start = ((bf16[4,2,73728]{2,1,0:T(2,128)(2,1)}), bf16[4,2,73728]{2,1,0:T(2,128)(2,1)}, u32[]{:S(2)}, u32[]{:S(2)}) async-start(bf16[4,2,73728]{2,1,0:T(2,128)(2,1)} %reshape.167), calls=%async_computation | async-start | bytes 2359296 | tf_op jit(solution)/shard_map/all_to_all | solution.py:338
  123.0 7.3 %copy-start.42 = (bf16[768]{0:T(1024)(128)(2,1)S(1)}, bf16[768]{0:T(1024)(128)(2,1)}, u32[]{:S(2)}) copy-start(bf16[768]{0:T(1024)(128)(2,1)} %param.37) | copy-start | bytes 4612
  123.0 7.9 %copy-start.43 = (bf16[768]{0:T(1024)(128)(2,1)S(1)}, bf16[768]{0:T(1024)(128)(2,1)}, u32[]{:S(2)}) copy-start(bf16[768]{0:T(1024)(128)(2,1)} %param.38) | copy-start | bytes 4612
  123.0 9.0 %copy-start.18 = (s32[768]{0:T(1024)S(1)}, s32[768]{0:T(1024)}, u32[]{:S(2)}) copy-start(s32[768]{0:T(1024)} %param.43) | copy-start | bytes 9220
  123.1 9.0 %copy-start.28 = (f32[768]{0:T(1024)S(1)}, f32[768]{0:T(1024)}, u32[]{:S(2)}) copy-start(f32[768]{0:T(1024)} %param.40) | copy-start | bytes 9220
  123.1 9.0 %copy-start.10 = (s32[3072]{0:T(1024)S(1)}, s32[3072]{0:T(1024)}, u32[]{:S(2)}) copy-start(s32[3072]{0:T(1024)} %param.44) | copy-start | bytes 36868
  123.1 9.0 %copy-start.21 = (f32[3072]{0:T(1024)S(1)}, f32[3072]{0:T(1024)}, u32[]{:S(2)}) copy-start(f32[3072]{0:T(1024)} %param.41) | copy-start | bytes 36868
  123.1 259.8 %reduce-scatter.13.cloned.1.call-start = ((), (), s32[]{:S(2)}) async-start(), calls=%async_computation.14 | async-start | bytes 1327104 | tf_op jit(solution)/shard_map/reduce_scatter | solution.py:460
  211.3 18.0 %slice-start = ((s8[4718592]{0:T(1024)(128)(4,1)}), s8[4194304]{0:T(1024)(128)(4,1)S(1)}, s32[]{:S(2)}) async-start(s8[4718592]{0:T(1024)(128)(4,1)} %bitcast.76), calls=%async_computation.21 | async-start | bytes 8388608
  213.1 16.2 %copy-start.4 = (f32[768,768]{0,1:T(8,128)}, f32[768,768]{0,1:T(8,128)S(1)}, u32[]{:S(2)}) copy-start(f32[768,768]{0,1:T(8,128)S(1)} %get-tuple-element.123) | copy-start | bytes 7077892
  213.2 16.2 %copy-start.12 = (f32[768]{0:T(1024)S(1)}, f32[768]{0:T(1024)}, u32[]{:S(2)}) copy-start(f32[768]{0:T(1024)} %copy-done.11) | copy-start | bytes 9220
  213.2 16.2 %copy-start.16 = (f32[768]{0:T(1024)S(1)}, f32[768]{0:T(1024)}, u32[]{:S(2)}) copy-start(f32[768]{0:T(1024)} %convert_element_type.110) | copy-start | bytes 9220
  213.2 16.2 %copy-start.17 = (f32[768]{0:T(1024)S(1)}, f32[768]{0:T(1024)}, u32[]{:S(2)}) copy-start(f32[768]{0:T(1024)} %add_rsqrt_fusion.1) | copy-start | bytes 9220
  213.2 16.2 %copy-start.36 = (f32[768]{0:T(1024)S(1)}, f32[768]{0:T(1024)}, u32[]{:S(2)}) copy-start(f32[768]{0:T(1024)} %convert_element_type.111) | copy-start | bytes 9220
  213.2 16.2 %copy-start.37 = (f32[768]{0:T(1024)S(1)}, f32[768]{0:T(1024)}, u32[]{:S(2)}) copy-start(f32[768]{0:T(1024)} %convert_element_type.120) | copy-start | bytes 9220
  213.2 16.2 %slice-start.1 = ((s8[4718592]{0:T(1024)(128)(4,1)}), s8[524288]{0:T(1024)(128)(4,1)S(1)}, s32[]{:S(2)}) async-start(s8[4718592]{0:T(1024)(128)(4,1)} %bitcast.76), calls=%async_computation.22 | async-start | bytes 1048576
  244.1 138.8 %reduce-scatter.15.cloned.1.call-start = ((), (), s32[]{:S(2)}) async-start(), calls=%async_computation.15 | async-start | bytes 5308416 | tf_op jit(solution)/shard_map/reduce_scatter | solution.py:461
  252.6 134.2 %reduce-scatter.17.cloned.1.call-start = ((), (), s32[]{:S(2)}) async-start(), calls=%async_computation.16 | async-start | bytes 5308416 | tf_op jit(solution)/shard_map/reduce_scatter | solution.py:462
  268.5 5.6 copy-start.29
  268.5 5.6 copy-start.35
  268.5 5.6 copy-start.34
  268.5 5.6 copy-start.33
  268.6 5.6 copy-start.32
  268.6 5.6 copy-start.14
  268.6 19.3 %all-to-all-start.1 = ((bf16[768,4,192]{0,2,1:T(8,128)(2,1)}), bf16[768,4,192]{0,2,1:T(8,128)(2,1)S(1)}, u32[]{:S(2)}, u32[]{:S(2)}) async-start(bf16[768,4,192]{0,2,1:T(8,128)(2,1)} %bitcast.5), calls=%async_computation.1 | async-start | bytes 2359296 | tf_op jit(solution)/shard_map/all_to_all | solution.py:407
  272.2 149.4 %reduce-scatter.23.cloned.1.call-start = ((), (), s32[]{:S(2)}) async-start(), calls=%async_computation.19 | async-start | bytes 1769472
  274.2 186.3 %reduce-scatter.21.cloned.1.call-start = ((), (), s32[]{:S(2)}) async-start(), calls=%async_computation.18 | async-start | bytes 442368
  353.1 133.0 %reduce-scatter.19.cloned.1.call-start = ((), (), s32[]{:S(2)}) async-start(), calls=%async_computation.17 | async-start | bytes 1105920
  361.4 166.4 %all-gather.15.cloned.1.call-start = ((), (), s32[]{:S(2)}) async-start(), calls=%async_computation.13 | async-start | bytes 3981312 | tf_op jit(solution)/shard_map/all_gather | solution.py:300
  375.8 128.1 %all-to-all-start.2 = ((bf16[4,2,221184]{2,1,0:T(2,128)(2,1)}), bf16[4,2,221184]{2,1,0:T(2,128)(2,1)S(1)}, u32[]{:S(2)}, u32[]{:S(2)}) async-start(bf16[4,2,221184]{2,1,0:T(2,128)(2,1)} %reshape.169), calls=%async_computation.2 | async-start | bytes 7077888 | tf_op jit(solution)/shard_map/all_to_all | solution.py:433
  379.5 7.4 %copy-start.47 = (f32[12]{0:T(128)S(1)}, f32[12]{0:T(128)}, u32[]{:S(2)}) copy-start(f32[12]{0:T(128)} %param.39) | copy-start | bytes 148
  379.5 7.4 %copy-start.49 = (s32[12]{0:T(128)S(1)}, s32[12]{0:T(128)}, u32[]{:S(2)}) copy-start(s32[12]{0:T(128)} %param.42) | copy-start | bytes 148
  379.5 207.9 %all-reduce.5.cloned.1.call-start = ((), (), s32[]{:S(2)}) async-start(), calls=%async_computation.20 | async-start | bytes 2654208 | tf_op jit(solution)/shard_map/psum | solution.py:468
  534.4 58.1 %copy-start.1 = (s32[8,2]{0,1:T(2,128)S(1)}, s32[8,2]{0,1:T(2,128)}, u32[]{:S(2)}) copy-start(s32[8,2]{0,1:T(2,128)} %param.47) | copy-start | bytes 196
  (24 other events, 64.5 us)
Sparse Core Ops, SparseCore 0:
  9.9 59.7 all-gather.6
  71.4 22.6 all-gather.8
  95.7 51.4 all-gather.10
  148.7 50.5 all-gather.12
  244.2 31.5 reduce-scatter.12
  278.0 53.1 reduce-scatter.14
  333.5 53.3 reduce-scatter.16
  389.1 32.4 reduce-scatter.22
  424.5 28.7 reduce-scatter.20
  456.1 30.0 reduce-scatter.18
  487.8 39.9 all-gather.14
  531.0 56.3 all-reduce.4

commit v2 on v1

--- a/solution.py
+++ b/solution.py
@@ -49,7 +49,7 @@
 
 
 def attend_kernel(
-    heads, lens_ref, tok_ref, w_ref, vec_ref, packed_ref, ctx_ref, lse_ref, q_sc, k_sc, vt_sc, ot_sc
+    heads, lens_ref, tok_ref, w_ref, vec_ref, packed_ref, ctx_ref, lse_ref, q_sc, k_sc, vt_sc
 ):
     def project(i, carry):
         rows = pl.ds(pl.multiple_of(i * TQ, TQ), TQ)
@@ -85,21 +85,13 @@
                 p2 = jnp.exp2(s2 * exp2_scale - top)
                 o = o + mm(vt_sc[h, :, own], p2.astype(bf16))
                 total = total + jnp.sum(p2, axis=0, keepdims=True)
-            ot_sc[h, :, rows] = o[0:HD, :] / total
+            ctx_ref[pl.ds(pl.multiple_of(HD * h, HD), HD), rows] = (o[0:HD, :] / total).astype(bf16)
             lse_ref[h, :, rows] = top + jnp.log2(total)
 
         query_tiles(lens_ref[0] == SHORT, tile)
         return carry
 
     lax.fori_loop(0, heads, one_head, 0)
-
-    def place(i, carry):
-        rows = pl.ds(pl.multiple_of(i * TQ, TQ), TQ)
-        for h in range(heads):
-            ctx_ref[rows, HD * h : HD * (h + 1)] = ot_sc[h, :, rows].T.astype(bf16)
-        return carry
-
-    lax.fori_loop(0, GLEN // TQ, place, 0)
 
 
 def attend(lens, tokens_all, weight, vec, heads):
@@ -109,7 +101,7 @@
         functools.partial(attend_kernel, heads),
         out_shape=(
             jax.ShapeDtypeStruct((GLEN, width), bf16),
-            jax.ShapeDtypeStruct((GLEN, HD * heads), bf16),
+            jax.ShapeDtypeStruct((HD * heads, GLEN), bf16),
             jax.ShapeDtypeStruct((heads, 1, GLEN), f32),
         ),
         in_specs=[pl.BlockSpec(memory_space=pltpu.SMEM), whole, whole, whole],
@@ -118,7 +110,6 @@
             pltpu.VMEM((heads, GLEN, HD), bf16),
             pltpu.VMEM((heads, GLEN, HD), bf16),
             pltpu.VMEM((heads, HD + 16, GLEN), bf16),
-            pltpu.VMEM((heads, HD, GLEN), f32),
         ],
         compiler_params=pltpu.CompilerParams(vmem_limit_bytes=56 * 2**20),
         cost_estimate=pl.CostEstimate(
@@ -138,8 +129,7 @@
     def split(i, carry):
         rows = pl.ds(pl.multiple_of(i * TQ, TQ), TQ)
         x = packed_ref[rows, :]
-        g = gctx_ref[rows, :]
-        inner = (g.astype(f32) * ctx_ref[rows, :].astype(f32)).T
+        inner = gctx_ref[:, rows].astype(f32) * ctx_ref[:, rows].astype(f32)
         for h in range(heads):
             at = 3 * HD * h
             q_sc[h, rows, :] = x[:, at : at + HD]
@@ -147,7 +137,7 @@
             k_sc[h, rows, :] = k
             kt_sc[h, :, rows] = k.T
             v_sc[h, rows, :] = x[:, at + 2 * HD : at + 3 * HD]
-            g_sc[h, rows, :] = g[:, HD * h : HD * (h + 1)]
+            g_sc[h, :, rows] = gctx_ref[HD * h : HD * (h + 1), rows]
             delta_sc[h, :, rows] = jnp.sum(inner[HD * h : HD * (h + 1), :], axis=0, keepdims=True)
         return carry
 
@@ -159,7 +149,7 @@
         def tile(q_at, own_at, own_len):
             rows = pl.ds(q_at, TQ)
             q = q_sc[h, rows, :]
-            g = g_sc[h, rows, :]
+            g = g_sc[h, :, rows]
             lse = lse_ref[h, :, rows]
             delta = delta_sc[h, :, rows]
             dq = jnp.zeros((HD, TQ), f32)
@@ -169,9 +159,9 @@
                 keys = pl.ds(start, KC)
                 s = mm(k_sc[h, keys, :], q, NT)
                 p = jnp.exp2(s * exp2_scale - lse)
-                dp = mm(v_sc[h, keys, :], g, NT)
+                dp = mm(v_sc[h, keys, :], g)
                 ds = (p * (dp - delta)).astype(bf16)
-                dv_sc[h, keys, :] += mm(p.astype(bf16), g)
+                dv_sc[h, keys, :] += mm(p.astype(bf16), g, NT)
                 dk_sc[h, keys, :] += mm(ds, q)
                 dq = dq + mm(kt_sc[h, :, keys], ds)
             dqt_sc[h, :, rows] = dq * score_scale
@@ -225,7 +215,7 @@
             rows64,
             rows64,
             pltpu.VMEM((heads, HD, GLEN), bf16),
-            rows64,
+            pltpu.VMEM((heads, HD, GLEN), bf16),
             pltpu.VMEM((heads, 1, GLEN), f32),
             pltpu.VMEM((heads, HD, GLEN), f32),
             rows64f,
@@ -239,6 +229,327 @@
         ),
         name="attend_back",
     )(lens, packed, ctx, gctx, lse, scale)
+
+
+def send(src, dst, sems, k, peer):
+    copy = pltpu.make_async_remote_copy(
+        src_ref=src,
+        dst_ref=dst,
+        send_sem=sems[0].at[k],
+        recv_sem=sems[1].at[k],
+        device_id=peer,
+        device_id_type=pl.DeviceIdType.MESH,
+    )
+    copy.start()
+    return copy
+
+
+def meet(peers):
+    barrier = pltpu.get_barrier_semaphore()
+    for peer in peers:
+        pl.semaphore_signal(barrier, inc=1, device_id=peer, device_id_type=pl.DeviceIdType.MESH)
+    pl.semaphore_wait(barrier, len(peers))
+
+
+def flip(index, bits):
+    for bit in (1, 2):
+        if bits & bit:
+            index = index + bit - 2 * bit * ((index // bit) % 2)
+    return index
+
+
+def remote_params(number):
+    return pltpu.CompilerParams(
+        collective_id=number, has_side_effects=True, vmem_limit_bytes=56 * 2**20
+    )
+
+
+ANYWHERE = pl.BlockSpec(memory_space=pl.ANY)
+IN_VMEM = pl.BlockSpec(memory_space=pltpu.VMEM)
+
+
+def dma_sems(count):
+    return [pltpu.SemaphoreType.DMA((count,)), pltpu.SemaphoreType.DMA((count,))]
+
+
+def gather_kernel(
+    n, tok_ref, cols_ref, out_ref, tok_all, cols_all, out_all,
+    tok_buf, cols_buf, out_buf, local_sem, s_tok, r_tok, s_w, r_w, s_f, r_f,
+):
+    s, w = lax.axis_index("seq"), lax.axis_index("wt")
+    rows = tok_ref.shape[0]
+    half = rows // 2
+    by_x, by_y, mate = (flip(s, 1), w), (flip(s, 2), w), (s, flip(w, 1))
+    far = [(s, lax.rem(w + 2 * j, n)) for j in range(1, n // 2)]
+    meet([by_x, by_y, mate] + far)
+
+    def part(owner, k):
+        return pl.ds(pl.multiple_of(owner * rows + k * half, half), half)
+
+    tok = (s_tok, r_tok)
+    first = [pl.ds(0, half), pl.ds(half, half)]
+    x0 = send(tok_ref.at[first[0]], tok_all.at[part(s, 0)], tok, 0, by_x)
+    y1 = send(tok_ref.at[first[1]], tok_all.at[part(s, 1)], tok, 1, by_y)
+    x1 = send(tok_ref.at[first[1]], tok_all.at[part(s, 1)], tok, 2, by_x)
+    y0 = send(tok_ref.at[first[0]], tok_all.at[part(s, 0)], tok, 3, by_y)
+    held = []
+    for k, peer in enumerate(far + [mate]):
+        for i, (src, dst) in enumerate(((cols_ref, cols_all), (out_ref, out_all))):
+            held.append(send(src, dst.at[w], (s_w, r_w), 2 * k + i, peer))
+    own = []
+    for i, (src, buf) in enumerate(((tok_ref, tok_buf), (cols_ref, cols_buf), (out_ref, out_buf))):
+        own.append(pltpu.make_async_copy(src, buf, local_sem.at[i]))
+        own[-1].start()
+    for copy in own:
+        copy.wait()
+    targets = (
+        (tok_buf, tok_all.at[pl.ds(pl.multiple_of(s * rows, rows), rows)]),
+        (cols_buf, cols_all.at[w]),
+        (out_buf, out_all.at[w]),
+    )
+    own = []
+    for i, (buf, dst) in enumerate(targets):
+        own.append(pltpu.make_async_copy(buf, dst, local_sem.at[3 + i]))
+        own[-1].start()
+    passed = []
+    x0.wait_recv()
+    there = tok_all.at[part(flip(s, 1), 0)]
+    passed.append(send(there, there, tok, 4, by_y))
+    y1.wait_recv()
+    there = tok_all.at[part(flip(s, 2), 1)]
+    passed.append(send(there, there, tok, 5, by_x))
+    for j in range(1, n // 2):
+        origin = lax.rem(w + n - 2 * j, n)
+        for i, dst in enumerate((cols_all, out_all)):
+            k = 2 * (j - 1) + i
+            held[k].wait_recv()
+            passed.append(send(dst.at[origin], dst.at[origin], (s_f, r_f), k, mate))
+    for copy in own:
+        copy.wait()
+    x1.wait_recv()
+    y0.wait_recv()
+    for copy in held[n - 2 :]:
+        copy.wait_recv()
+    for copy in passed:
+        copy.wait_recv()
+    for copy in [x0, x1, y0, y1] + held + passed:
+        copy.wait_send()
+
+
+def gather_in(n, tokens, own_columns, output_weight):
+    rows, d = tokens.shape
+    return pl.pallas_call(
+        functools.partial(gather_kernel, n),
+        out_shape=(
+            jax.ShapeDtypeStruct((4 * rows, d), bf16),
+            jax.ShapeDtypeStruct((n,) + own_columns.shape, bf16),
+            jax.ShapeDtypeStruct((n,) + output_weight.shape, bf16),
+        ),
+        in_specs=[ANYWHERE] * 3,
+        out_specs=(ANYWHERE,) * 3,
+        scratch_shapes=[
+            pltpu.VMEM(tokens.shape, bf16),
+            pltpu.VMEM(own_columns.shape, bf16),
+            pltpu.VMEM(output_weight.shape, bf16),
+            pltpu.SemaphoreType.DMA((6,)),
+        ]
+        + dma_sems(6)
+        + dma_sems(n)
+        + dma_sems(n - 2),
+        compiler_params=remote_params(0),
+        name="gather_in",
+    )(tokens, own_columns, output_weight)
+
+
+def exchange_kernel(src_of, dst_of, x_ref, o_ref, buf, local_sem, s_sem, r_sem):
+    s, w = lax.axis_index("seq"), lax.axis_index("wt")
+    others = [flip(s, k) for k in (1, 2, 3)]
+    meet([(p, w) for p in others])
+    copies = [
+        send(src_of(x_ref, p), dst_of(o_ref, s), (s_sem, r_sem), k, (p, w))
+        for k, p in enumerate(others)
+    ]
+    come = pltpu.make_async_copy(src_of(x_ref, s), buf, local_sem.at[0])
+    come.start()
+    come.wait()
+    go = pltpu.make_async_copy(buf, dst_of(o_ref, s), local_sem.at[1])
+    go.start()
+    go.wait()
+    for copy in copies:
+        copy.wait()
+
+
+def exchange(x, out_shape, part_shape, src_of, dst_of, number, name):
+    return pl.pallas_call(
+        functools.partial(exchange_kernel, src_of, dst_of),
+        out_shape=jax.ShapeDtypeStruct(out_shape, x.dtype),
+        in_specs=[ANYWHERE],
+        out_specs=ANYWHERE,
+        scratch_shapes=[pltpu.VMEM(part_shape, x.dtype), pltpu.SemaphoreType.DMA((2,))] + dma_sems(3),
+        compiler_params=remote_params(number),
+        name=name,
+    )(x)
+
+
+def reduce_kernel(
+    n, con_ref, exp_ref, out_ref, att_ref, vec_ref, con_o, exp_o, out_o, att_o, vec_o,
+    r_con, r_exp, r_out, h_att, m_att, r_att, r_vec, r_vec2, m_vec, m_ce, g_ce, m_row, g_att,
+    s_a, r_a, s_b, r_b, s_c, r_c, s_d, r_d, s_e, r_e, s_f, r_f, s_g, r_g, s_h, r_h, s_i, r_i,
+):
+    s, w = lax.axis_index("seq"), lax.axis_index("wt")
+    z, c = w // 2, lax.rem(w, 2)
+    others = [flip(s, k) for k in (1, 2, 3)]
+    seq_peers = [(p, w) for p in others]
+    mate = (s, flip(w, 1))
+    wt_peers = [(s, lax.rem(w + j, n)) for j in range(1, n)]
+    meet(seq_peers + wt_peers)
+    wide = exp_ref.shape[1] // 4
+
+    def lanes(p):
+        return pl.ds(pl.multiple_of(p * wide, 128), wide)
+
+    pair = [
+        send(att_ref.at[2 * k + 1 - c], h_att.at[k], (s_a, r_a), k, mate) for k in range(n // 2)
+    ]
+    vecs = [
+        send(vec_ref.at[lax.rem(w + j, n)], r_vec.at[w], (s_b, r_b), j - 1, wt_peers[j - 1])
+        for j in range(1, n)
+    ]
+    cons = [
+        send(con_ref.at[p], r_con.at[s], (s_c, r_c), k, (p, w)) for k, p in enumerate(others)
+    ]
+    exps = [
+        send(exp_ref.at[:, lanes(p)], r_exp.at[s], (s_d, r_d), k, (p, w))
+        for k, p in enumerate(others)
+    ]
+    outs = [send(out_ref, r_out.at[s], (s_e, r_e), k, (p, w)) for k, p in enumerate(others)]
+    r_con[s] = con_ref[s]
+    r_exp[s] = exp_ref[:, lanes(s)]
+    r_out[s] = out_ref[...]
+    r_vec[w] = vec_ref[w]
+    for copy in pair:
+        copy.wait_recv()
+    for k in range(n // 2):
+        m_att[k] = (att_ref[2 * k + c].astype(f32) + h_att[k].astype(f32)).astype(bf16)
+    zs = [lax.rem(z + j, n // 2) for j in range(1, n // 2)]
+    atts = [
+        send(m_att.at[k], r_att.at[z], (s_f, r_f), j, (s, 2 * k + c)) for j, k in enumerate(zs)
+    ]
+    r_att[z] = m_att[z]
+    for copy in vecs:
+        copy.wait_recv()
+    total = r_vec[0]
+    for k in range(1, n):
+        total = total + r_vec[k]
+    m_vec[...] = total
+    vecs2 = [send(m_vec, r_vec2.at[s], (s_g, r_g), k, p) for k, p in enumerate(seq_peers)]
+    r_vec2[s] = total
+
+    def add4(ref):
+        t = [ref[k].astype(f32) for k in range(4)]
+        return (t[0] + t[1]) + (t[2] + t[3])
+
+    for copy in cons:
+        copy.wait_recv()
+    m_ce[0] = add4(r_con).astype(bf16)
+    for copy in exps:
+        copy.wait_recv()
+    m_ce[1] = add4(r_exp).astype(bf16)
+    g_ce[s] = m_ce[...]
+    ces = [send(m_ce, g_ce.at[s], (s_h, r_h), k, p) for k, p in enumerate(seq_peers)]
+    for copy in atts:
+        copy.wait_recv()
+    row = r_att[0].astype(f32)
+    for k in range(1, n // 2):
+        row = row + r_att[k].astype(f32)
+    m_row[...] = row.astype(bf16)
+    g_att[s] = m_row[...]
+    rows = [send(m_row, g_att.at[s], (s_i, r_i), k, p) for k, p in enumerate(seq_peers)]
+    for copy in outs:
+        copy.wait_recv()
+    out_o[...] = add4(r_out)
+    for copy in vecs2:
+        copy.wait_recv()
+    vec_o[...] = (r_vec2[0] + r_vec2[1]) + (r_vec2[2] + r_vec2[3])
+    for copy in ces:
+        copy.wait_recv()
+    for k in range(4):
+        con_o[k] = g_ce[k, 0].astype(f32)
+        exp_o[:, k * wide : (k + 1) * wide] = g_ce[k, 1].astype(f32)
+    for copy in rows:
+        copy.wait_recv()
+    cols = g_att.shape[2]
+    for k in range(4):
+        att_o[:, k * cols : (k + 1) * cols] = g_att[k].astype(f32)
+    for copy in pair + vecs + cons + exps + outs + atts + vecs2 + ces + rows:
+        copy.wait_send()
+
+
+def reduce_out(n, con, expand, out, att, vec):
+    r, d = out.shape
+    cols = att.shape[2]
+    vshape = vec.shape[1:]
+    counts = (n // 2, n - 1, 3, 3, 3, n // 2 - 1, 3, 3, 3)
+    return pl.pallas_call(
+        functools.partial(reduce_kernel, n),
+        out_shape=(
+            jax.ShapeDtypeStruct(con.shape, f32),
+            jax.ShapeDtypeStruct(expand.shape, f32),
+            jax.ShapeDtypeStruct(out.shape, f32),
+            jax.ShapeDtypeStruct((r, 4 * cols), f32),
+            jax.ShapeDtypeStruct(vshape, f32),
+        ),
+        in_specs=[IN_VMEM] * 5,
+        out_specs=(IN_VMEM,) * 5,
+        scratch_shapes=[
+            pltpu.VMEM((4, r, d), bf16),
+            pltpu.VMEM((4, r, d), bf16),
+            pltpu.VMEM((4, r, d), bf16),
+            pltpu.VMEM((n // 2, r, cols), bf16),
+            pltpu.VMEM((n // 2, r, cols), bf16),
+            pltpu.VMEM((n // 2, r, cols), bf16),
+            pltpu.VMEM((n,) + vshape, f32),
+            pltpu.VMEM((4,) + vshape, f32),
+            pltpu.VMEM(vshape, f32),
+            pltpu.VMEM((2, r, d), bf16),
+            pltpu.VMEM((4, 2, r, d), bf16),
+            pltpu.VMEM((r, cols), bf16),
+            pltpu.VMEM((4, r, cols), bf16),
+        ]
+        + [sem for count in counts for sem in dma_sems(count)],
+        compiler_params=remote_params(4),
+        name="reduce_out",
+    )(con, expand, out, att, vec)
+
+
+def tokens_grad_kernel(base_ref, g_ref, w_ref, o_ref):
+    cols = g_ref.shape[2]
+    total = base_ref[...]
+    for k in range(4):
+        total = total + mm(g_ref[k], w_ref[:, k * cols : (k + 1) * cols], NT)
+    o_ref[...] = total
+
+
+def tokens_back(base, g, weight):
+    rows, d = base.shape
+    cols = g.shape[2]
+    block = rows // 3
+    return pl.pallas_call(
+        tokens_grad_kernel,
+        out_shape=jax.ShapeDtypeStruct((rows, d), f32),
+        grid=(3,),
+        in_specs=[
+            pl.BlockSpec((block, d), lambda i: (i, 0)),
+            pl.BlockSpec((4, block, cols), lambda i: (0, i, 0)),
+            pl.BlockSpec(weight.shape, lambda i: (0, 0)),
+        ],
+        out_specs=pl.BlockSpec((block, d), lambda i: (i, 0)),
+        compiler_params=pltpu.CompilerParams(vmem_limit_bytes=48 * 2**20),
+        cost_estimate=pl.CostEstimate(
+            flops=8 * rows * d * cols, bytes_accessed=8 * rows * d + 8 * d * cols, transcendentals=0
+        ),
+        name="tokens_back",
+    )(base, g, weight)
 
 
 def norm_parts(summed):
@@ -290,15 +601,14 @@
     seq_index = lax.axis_index("seq")
     wt_index = lax.axis_index("wt")
     local_width = 3 * head_size * local_heads
-    tokens_all = lax.all_gather(tokens, "seq", axis=0, tiled=True)
+    wt_count = lax.axis_size("wt")
     own_columns = lax.dynamic_slice_in_dim(attention_weight, seq_index * local_width, local_width, 1)
-    own_weight = lax.all_gather(own_columns, "wt", axis=0, tiled=True)
-    full_output, full_expand, full_contract, full_attention = (
-        lax.all_gather(output_weight, "wt", axis=0, tiled=True),
-        lax.all_gather(expand_weight, "wt", axis=0, tiled=True),
-        lax.all_gather(contract_weight, "wt", axis=0, tiled=True),
-        lax.all_gather(attention_weight, "wt", axis=0, tiled=True),
-    )
+    tokens_all, own_weight, full_output = gather_in(wt_count, tokens, own_columns, output_weight)
+    own_weight = own_weight.reshape(model_width, local_width)
+    full_output = full_output.reshape(model_width, model_width)
+    full_expand = lax.all_gather(expand_weight, "wt", axis=0, tiled=True)
+    full_contract = lax.all_gather(contract_weight, "wt", axis=0, tiled=True)
+    full_attention = lax.all_gather(attention_weight, "wt", axis=0, tiled=True)
     position = seq_index * row_count + jnp.arange(row_count, dtype=jnp.int32)
     group_local = position // GLEN
     own_groups = jnp.arange(GRP_WT, dtype=jnp.int32)
@@ -335,11 +645,18 @@
     vec = jnp.stack([own_bias.reshape(local_width), factor.reshape(local_width)], axis=0)
     lens = lax.dynamic_slice_in_dim(continuation_lengths, first_group, GRP_WT, 0)[0]
     packed, mixed_heads, log_sums = attend(lens, tokens_all, own_weight, vec, local_heads)
-    context = lax.all_to_all(
-        mixed_heads.reshape(GLEN, 1, local_heads * head_size), "seq", split_axis=0, concat_axis=1, tiled=True
-    ).reshape(row_count, model_width)
-    attn_out = jnp.dot(
-        context, full_output, preferred_element_type=jnp.float32
+    local_ctx = local_heads * head_size
+    context_t = exchange(
+        mixed_heads,
+        (model_width, row_count),
+        (local_ctx, row_count),
+        lambda ref, p: ref.at[:, pl.ds(pl.multiple_of(p * row_count, 128), row_count)],
+        lambda ref, p: ref.at[pl.ds(pl.multiple_of(p * local_ctx, 16), local_ctx), :],
+        1,
+        "context_out",
+    )
+    attn_out = jnp.einsum(
+        "it,id->td", context_t, full_output, preferred_element_type=jnp.float32
     ) + output_bias.astype(jnp.float32)
     normed_one, inverse_one = norm_parts(tokens.astype(jnp.float32) + attn_out)
     shaped_one = normed_one * first_gain_f + first_shift.astype(jnp.float32)
@@ -399,23 +716,25 @@
     grad_attn = grad_total_one.astype(jnp.bfloat16)
     output_bias_grad = jnp.sum(grad_attn.astype(jnp.float32), axis=0)
     output_weight_grad = jnp.einsum(
-        "ti,td->id", context, grad_attn, preferred_element_type=jnp.float32
-    )
-    grad_context = jnp.einsum(
-        "td,id->ti", grad_attn, back_output, preferred_element_type=jnp.float32
+        "it,td->id", context_t, grad_attn, preferred_element_type=jnp.float32
+    )
+    grad_context_t = jnp.einsum(
+        "td,id->it", grad_attn, back_output, preferred_element_type=jnp.float32
     ).astype(jnp.bfloat16)
-    arriving = lax.all_to_all(
-        grad_context.reshape(row_count, seq_count, local_heads * head_size),
-        "seq",
-        split_axis=1,
-        concat_axis=0,
-        tiled=True,
+    arriving = exchange(
+        grad_context_t,
+        (local_ctx, GLEN),
+        (local_ctx, row_count),
+        lambda ref, p: ref.at[pl.ds(pl.multiple_of(p * local_ctx, 16), local_ctx), :],
+        lambda ref, p: ref.at[:, pl.ds(pl.multiple_of(p * row_count, 128), row_count)],
+        2,
+        "context_grad_in",
     )
     grad_packed, sums, gate_sums = attend_back(
         lens,
         packed,
         mixed_heads,
-        arriving.reshape(GLEN, local_heads * head_size),
+        arriving,
         log_sums,
         vec[1:2],
         local_heads,
@@ -430,17 +749,20 @@
     at_own = seq_index * local_heads * head_size
     query_bias_grad = lax.dynamic_update_slice_in_dim(zeros_wide, sums[:, 0].reshape(-1), at_own, 0)
     value_bias_grad = lax.dynamic_update_slice_in_dim(zeros_wide, sums[:, 2].reshape(-1), at_own, 0)
-    grad_flat = lax.all_to_all(
-        grad_packed.reshape(GLEN, 1, local_width), "seq", split_axis=0, concat_axis=1, tiled=True
-    ).reshape(row_count, 3 * model_width)
+    grad_pieces = exchange(
+        grad_packed.reshape(seq_count, row_count, local_width),
+        (seq_count, row_count, local_width),
+        (row_count, local_width),
+        lambda ref, p: ref.at[p],
+        lambda ref, p: ref.at[p],
+        3,
+        "packed_grad_out",
+    )
     attention_weight_grad = jnp.einsum(
         "td,tc->dc", tokens_all, grad_packed, preferred_element_type=jnp.float32
     )
-    tokens_grad = grad_total_one + jnp.einsum(
-        "tc,dc->td", grad_flat, back_attention, preferred_element_type=jnp.float32
-    )
-    head_gate_grad = lax.psum(head_partial, ("seq", "wt"))
-    width_vectors = jnp.stack(
+    tokens_grad = tokens_back(grad_total_one, grad_pieces, back_attention)
+    width_rows = jnp.stack(
         [
             query_bias_grad,
             value_bias_grad,
@@ -452,46 +774,61 @@
             second_shift_grad,
             hidden_gate_grad,
         ],
+        axis=0,
+    )
+    unit_rows = jnp.stack([expand_bias_grad, unit_gate_grad], axis=0)
+    own_wide, own_units = model_width // wt_count, unit_gate.shape[0] // wt_count
+    by_shard = jnp.concatenate(
+        [
+            width_rows.reshape(9, wt_count, own_wide).transpose(1, 0, 2).reshape(wt_count, -1),
+            unit_rows.reshape(2, wt_count, own_units).transpose(1, 0, 2).reshape(wt_count, -1),
+            jnp.broadcast_to(head_partial[None, :], (wt_count, head_count)),
+        ],
         axis=1,
     )
-    unit_vectors = jnp.stack([expand_bias_grad, unit_gate_grad], axis=1)
-    pieces = (
-        lax.psum_scatter(attention_weight_grad.astype(bf16), "wt", scatter_dimension=0, tiled=True),
-        lax.psum_scatter(output_weight_grad.astype(bf16), "wt", scatter_dimension=0, tiled=True),
-        lax.psum_scatter(expand_weight_grad.astype(bf16), "wt", scatter_dimension=0, tiled=True),
-        lax.psum_scatter(contract_weight_grad.astype(bf16), "wt", scatter_dimension=0, tiled=True),
-        lax.psum_scatter(width_vectors, "wt", scatter_dimension=0, tiled=True),
-        lax.psum_scatter(unit_vectors, "wt", scatter_dimension=0, tiled=True),
-    )
-    shards = (
-        lax.all_gather(pieces[0], "seq", axis=1, tiled=True).astype(jnp.float32),
-        lax.psum(pieces[1], "seq").astype(jnp.float32),
-        lax.psum(pieces[2], "seq").astype(jnp.float32),
-        lax.psum(pieces[3], "seq").astype(jnp.float32),
-        lax.psum(pieces[4], "seq"),
-        lax.psum(pieces[5], "seq"),
-    )
-    width_shard = shards[4]
-    unit_shard = shards[5]
+    used = by_shard.shape[1]
+    by_shard = jnp.pad(by_shard, ((0, 0), (0, -used % 1024))).reshape(wt_count, -1, 128)
+    con_piece = lax.psum_scatter(
+        contract_weight_grad.astype(bf16), "wt", scatter_dimension=0, tiled=True
+    )
+    exp_piece = lax.psum_scatter(
+        expand_weight_grad.astype(bf16), "wt", scatter_dimension=0, tiled=True
+    )
+    out_piece = lax.psum_scatter(
+        output_weight_grad.astype(bf16), "wt", scatter_dimension=0, tiled=True
+    )
+    con_sum, exp_sum, out_sum, att_sum, vec_sum = reduce_out(
+        wt_count,
+        con_piece.reshape(seq_count, own_wide, model_width),
+        exp_piece,
+        out_piece,
+        attention_weight_grad.astype(bf16).reshape(wt_count, own_wide, local_width),
+        by_shard,
+    )
+    vec_sum = vec_sum.reshape(-1)
+    wide = [vec_sum[k * own_wide : (k + 1) * own_wide] for k in range(9)]
+    base = 9 * own_wide
+    units = [vec_sum[base + k * own_units : base + (k + 1) * own_units] for k in range(2)]
+    head_gate_grad = vec_sum[base + 2 * own_units : used]
     return (
         layer_output,
         tokens_grad,
-        shards[0],
-        width_shard[:, 0],
-        width_shard[:, 1],
-        shards[1],
-        width_shard[:, 2],
-        width_shard[:, 3],
-        width_shard[:, 4],
-        shards[2],
-        unit_shard[:, 0],
-        shards[3],
-        width_shard[:, 5],
-        width_shard[:, 6],
-        width_shard[:, 7],
+        att_sum,
+        wide[0],
+        wide[1],
+        out_sum,
+        wide[2],
+        wide[3],
+        wide[4],
+        exp_sum,
+        units[0],
+        con_sum.reshape(seq_count * own_wide, model_width),
+        wide[5],
+        wide[6],
+        wide[7],
         head_gate_grad,
-        width_shard[:, 8],
-        unit_shard[:, 1],
+        wide[8],
+        units[1],
     )
 
 

time: 610 us -> 445 us (0.73)
  Pallas kernels: 104 us -> 293 us
  waiting for transfers between devices: 169 us -> 2.16 us
  blocking collectives: 83.9 us -> 0 us
  local copies, waits for them, and re-layouts: 82.8 us -> 24.8 us
  other arithmetic: 26.5 us -> 7.13 us
  starting transfers between devices: 12.3 us -> 0.24 us
  matrix products: 105 us -> 94.4 us
    pallas_call x0 -> x6, Pallas kernels: none -> 193 us  [the longest x3 73.4 us: exchange(): pl.pallas_call(functools.partial(exchange_kernel, src_of, dst_of), out_sh...]
    psum x2 -> x0, blocking collectives: 54.5 us -> none  [the longest x1 37.9 us: local(): head_gate_grad = lax.psum(head_partial, ('seq', 'wt'))]
    all_gather x5 -> x3, waiting for transfers between devices: 51.1 us -> 0.04 us  [the longest x1 0.02 us: local(): full_expand = lax.all_gather(expand_weight, 'wt', axis=0, tiled=True)]
    psum x1 -> x0, waiting for transfers between devices: 51 us -> none  [local(): lax.psum(pieces[1], 'seq').astype(jnp.float32)]
    unnamed x15 -> x6, waiting for transfers between devices: 43.4 us -> 2.11 us
    unnamed x130 -> x66, local copies, waits for them, and re-layouts: 50.9 us -> 10 us
    all_gather x2 -> x0, blocking collectives: 29.3 us -> none  [the longest x1 18.9 us: local(): own_weight = lax.all_gather(own_columns, 'wt', axis=0, tiled=True)]
    all_to_all x6 -> x0, local copies, waits for them, and re-layouts: 19.8 us -> none  [the longest x2 9.18 us: local(): lax.all_to_all(grad_packed.reshape(GLEN, 1, local_width), 'seq', split_ax...]
  transfers between devices with their start and end apart: 15 -> 6, of which waited for: 9 -> 0; matrix products, arithmetic and copies ran while one was open for 26% -> 26% of each run, Pallas kernels for 17% -> 52%
where the time goes in v2:
time: 445 us; the launch traced here: 438 us
  Pallas kernels  293 us (66%)
  matrix products  94.4 us (21%)
  local copies, waits for them, and re-layouts  24.8 us (6%)
  between operations  16.4 us (4%)
  other arithmetic  7.13 us (2%)
    pallas_call x3, Pallas kernels, exchange(): pl.pallas_call(functools.partial(exchange_kernel, src_of, dst_of), out_sh...  73.4 us
    pallas_call x1, Pallas kernels, reduce_out(): pl.pallas_call(functools.partial(reduce_kernel, n), out_shape=(jax.ShapeD...  66.8 us
    pallas_call x1, Pallas kernels, attend_back(): pl.pallas_call(functools.partial(attend_back_kernel, heads), out_shape=(j...  59.8 us
    pallas_call x1, Pallas kernels, gather_in(): pl.pallas_call(functools.partial(gather_kernel, n), out_shape=(jax.ShapeD...  45.7 us
    pallas_call x1, Pallas kernels, attend(): pl.pallas_call(functools.partial(attend_kernel, heads), out_shape=(jax.Sh...  40.8 us
    dot_general x1, matrix products, local(): jnp.dot(first_low, full_expand, preferred_element_type=jnp.float32)  27.6 us
    dot_general x1, matrix products, local(): jnp.einsum('td,id->ti', grad_branch, back_contract, preferred_element_typ...  14.5 us
    dot_general x1, matrix products, local(): jnp.einsum('ti,td->id', activated, grad_branch, preferred_element_type=jn...  10.5 us
  transfers between devices with their start and end apart: 6, of which 0 were waited for; matrix products, arithmetic and copies ran while one was open for 26% of the time, Pallas kernels for 52%

profile of v2, /device:TPU:0, one launch (start us, length us, event | category | flops | bytes accessed | tf_op | source)
XLA Modules:
  0.0 438.4 jit_solution(5975066747388378487)
XLA Ops:
  7.3 0.7 all-gather.4.cloned.1.call-update
  8.0 0.7 all-gather.6.cloned.1.call-update
  8.7 0.7 all-gather.8.cloned.1.call-update
  9.5 1.2 dynamic_slice.28
  11.4 0.7 convert_multiply_fusion.6
  12.3 0.8 reshape.181
  13.1 0.8 reshape.182
  14.1 1.7 constant_dynamic-slice_fusion.cols_ref
  15.7 0.7 dynamic-slice_reduce_fusion.lens_ref
  16.4 0.6 pad_maximum_fusion.1.vec_ref
  17.0 45.7 %gather_in.1 = (bf16[3072,768]{1,0:T(8,128)(2,1)}, bf16[8,96,576]{2,1,0:T(8,128)(2,1)}, bf16[8,96,768]{2,1,0:T(8,128)(2,1)}) custom-call(bf16[768,768]{1,0:T(8,128)(2,1)} %tok_ref.1, bf16[96,576]{1,0:T(8,128)(2,1)} %constant_dynamic-slice_fusion.cols_ref, bf16[96,768]{1,0:T(8,128)(2,1)} %out_ref.1), custom_call_target="tpu_custom_call" | custom-call | tf_op jit(solution)/shard_map/gather_in/pallas_call | solution.py:341
  62.7 40.8 %attend.1 = (bf16[3072,576]{1,0:T(8,128)(2,1)}, bf16[192,3072]{1,0:T(8,128)(2,1)}, f32[3,1,3072]{2,1,0:T(1,128)}) custom-call(s32[2]{0:T(128)} %dynamic-slice_reduce_fusion.lens_ref, bf16[3072,768]{1,0:T(8,128)(2,1)} %get-tuple-element.32.tok_ref, bf16[768,576]{1,0:T(8,128)(2,1)} %bitcast.45, f32[2,576]{1,0:T(2,128)} %pad_maximum_fusion.1.vec_ref), custom_call_target="tpu_custom_call" | custom-call | flops 20434649088 | bytes 8257536 | tf_op jit(solution)/shard_map/attend/pallas_call | solution.py:100
  103.5 15.5 %context_out.1 = bf16[768,768]{1,0:T(8,128)(2,1)} custom-call(bf16[192,3072]{1,0:T(8,128)(2,1)} %get-tuple-element.34.x_ref.ctx_ref), custom_call_target="tpu_custom_call" | custom-call | tf_op jit(solution)/shard_map/context_out/pallas_call | solution.py:383
  119.1 2.6 fusion.45
  121.9 0.7 dynamic_slice.29
  123.4 0.4 multiply_reduce_fusion.4
  123.9 27.6 %fusion.4 = (f32[768,3072]{1,0:T(8,128)}, f32[768,3072]{1,0:T(8,128)}) fusion(f32[3072]{0:T(1024)S(1)} %convert_element_type.101, bf16[768,3072]{1,0:T(8,128)(2,1)} %all-gather.4.cloned.1.call-done, f32[768]{0:T(1024)S(1)} %get-tuple-element.83, f32[768]{0:T(1024)S(1)} %convert_element_type.98, f32[768]{0:T(1024)S(1)} %convert_element_type.97, ...), kind=kOutput, calls=%fused_computation.8 | convolution fusion | flops 3780771840 | bytes 25979904 | tf_op jit(solution)/shard_map/dot_general | solution.py:665
  151.5 8.5 %fusion.46 = (f32[768]{0:T(1024)S(1)}, f32[768,768]{1,0:T(8,128)S(1)}) fusion(f32[768]{0:T(1024)S(1)} %convert_element_type.105, bf16[3072,768]{1,0:T(8,128)(2,1)} %all-gather.6.cloned.1.call-done, f32[768,3072]{1,0:T(8,128)} %get-tuple-element.78, f32[768]{0:T(1024)S(1)} %fusion.32, f32[3072]{0:T(1024)S(1)} %convert_multiply_fusion.3, ...), kind=kOutput, calls=%fused_computation.112 | convolution fusion | flops 3635674368 | bytes 18911232 | tf_op jit(solution)/shard_map/dot_general | solution.py:671
  160.1 0.4 multiply_reduce_fusion.3
  160.5 0.8 copy-done.4
  161.4 0.9 fusion.21
  162.3 1.0 convert_reduce_fusion.1
  163.3 0.4 copy-done.25
  163.7 14.5 %convert_reduce_fusion = (f32[3072]{0:T(1024)S(1)}, bf16[768,3072]{1,0:T(8,128)(2,1)}, f32[3072]{0:T(1024)S(1)}) fusion(f32[768,3072]{1,0:T(8,128)} %get-tuple-element.79, f32[3072]{0:T(1024)S(1)} %convert_element_type.101, f32[768]{0:T(1024)S(1)} %fusion.32, f32[3072]{0:T(1024)S(1)} %convert_multiply_fusion.3, f32[768,3072]{1,0:T(8,128)} %get-tuple-element.78, ...), kind=kOutput, calls=%fused_computation.14 | convolution fusion | flops 3666929664 | bytes 30723072 | tf_op jit(solution)/shard_map/td,id->ti/dot_general | solution.py:693
  178.3 9.1 %fusion.27 = (f32[768]{0:T(1024)S(1)}, f32[768]{0:T(1024)S(1)}, f32[768]{0:T(1024)S(1)}, f32[768]{0:T(1024)S(1)}, f32[768]{0:T(1024)S(1)}, /*index=5*/f32[768]{0...) fusion(bf16[768,768]{1,0:T(8,128)(2,1)S(1)} %copy-done.4, ...), kind=kOutput, calls=%fused_computation.45 | convolution fusion | flops 3640388352 | bytes 21282816 | tf_op jit(solution)/shard_map/tf,df->td/dot_general | solution.py:706
  187.4 2.3 convert_reduce_fusion.2
  189.7 2.1 convolution_convert_fusion.2
  191.9 9.4 %convolution_convert_fusion = bf16[768,3072]{1,0:T(8,128)(2,1)} fusion(bf16[768,3072]{1,0:T(8,128)(2,1)} %get-tuple-element.58, f32[768]{0:T(1024)S(1)} %get-tuple-element.83, f32[768]{0:T(1024)S(1)} %convert_element_type.98, f32[768]{0:T(1024)S(1)} %convert_element_type.97, f32[768,768]{1,0:T(8,128)} %copy-done.3, f32[768]{0:T(1024)S(1)} %get-tuple-element.84, ...), kind=kOutput, calls=%fused_computation.30 | convolution fusion | flops 3629776896 | bytes 11811840 | tf_op jit(solution)/shard_map/td,tf->df/dot_general | solution.py:703
  201.4 10.5 %convolution_convert_fusion.1 = bf16[3072,768]{1,0:T(8,128)(2,1)} fusion(f32[768,768]{1,0:T(8,128)} %copy-done.5, f32[768,3072]{1,0:T(8,128)} %get-tuple-element.78, f32[768]{0:T(1024)S(1)} %fusion.32, f32[3072]{0:T(1024)S(1)} %convert_multiply_fusion.3), kind=kOutput, calls=%fused_computation.31 | convolution fusion | flops 3633905664 | bytes 16530432 | tf_op jit(solution)/shard_map/ti,td->id/dot_general | solution.py:690
  212.0 3.4 convolution_convert_fusion.3.x_ref
  215.4 14.6 %context_grad_in.1.gctx_ref = bf16[192,3072]{1,0:T(8,128)(2,1)} custom-call(bf16[768,768]{1,0:T(8,128)(2,1)} %convolution_convert_fusion.3.x_ref), custom_call_target="tpu_custom_call" | custom-call | tf_op jit(solution)/shard_map/context_grad_in/pallas_call | solution.py:383
  230.0 59.8 %attend_back.1 = (bf16[3072,576]{1,0:T(8,128)(2,1)}, f32[8,576]{1,0:T(8,128)}, f32[8,192]{1,0:T(8,128)}) custom-call(s32[2]{0:T(128)} %dynamic-slice_reduce_fusion.lens_ref, bf16[3072,576]{1,0:T(8,128)(2,1)} %get-tuple-element.36.packed_ref, bf16[192,3072]{1,0:T(8,128)(2,1)} %get-tuple-element.34.x_ref.ctx_ref, bf16[192,3072]{1,0:T(8,128)(2,1)} %context_grad_in.1.gctx_ref, ...), custom_call_target="tpu_custom_call" | custom-call | flops 44291850240 | bytes 10616832 | tf_op jit(solution)/shard_map/attend_back/pallas_call | solution.py:204
  289.8 0.7 slice_reduce_fusion
  292.0 0.7 slice_reduce_fusion.3
  293.4 0.6 copy.49
  294.0 6.6 %convolution_convert_fusion.4 = bf16[768,576]{0,1:T(8,128)(2,1)S(1)} fusion(bf16[3072,768]{1,0:T(8,128)(2,1)} %get-tuple-element.32.tok_ref, bf16[3072,576]{1,0:T(8,128)(2,1)} %get-tuple-element.38), kind=kOutput, calls=%fused_computation.66 | convolution fusion | flops 2718351360 | bytes 9142272 | tf_op jit(solution)/shard_map/td,tc->dc/dot_general | solution.py:761
  300.6 1.3 copy.45
  302.0 43.4 %packed_grad_out.1.g_ref = bf16[4,768,576]{2,1,0:T(8,128)(2,1)} custom-call(bf16[4,768,576]{2,1,0:T(8,128)(2,1)} %bitcast.32), custom_call_target="tpu_custom_call" | custom-call | tf_op jit(solution)/shard_map/packed_grad_out/pallas_call | solution.py:383
  345.4 2.0 copy-done.2
  347.4 6.8 %tokens_back.1 = f32[768,768]{1,0:T(8,128)} custom-call(f32[768,768]{1,0:T(8,128)S(1)} %get-tuple-element.62.base_ref, bf16[4,768,576]{2,1,0:T(8,128)(2,1)} %packed_grad_out.1.g_ref, bf16[768,2304]{1,0:T(8,128)(2,1)S(1)} %copy-done.2), custom_call_target="tpu_custom_call" | custom-call | flops 2717908992 | bytes 8257536 | tf_op jit(solution)/shard_map/tokens_back/pallas_call | solution.py:537
  354.2 66.8 %reduce_out.1 = (f32[4,96,768]{2,1,0:T(8,128)}, f32[96,3072]{1,0:T(8,128)}, f32[96,768]{1,0:T(8,128)}, f32[96,2304]{1,0:T(8,128)}, f32[16,128]{1,0:T(8,128)}) custom-call(bf16[4,96,768]{2,1,0:T(8,128)(2,1)} %bitcast.34, bf16[96,3072]{1,0:T(8,128)(2,1)} %reduce-scatter.6.cloned.1.call-done.exp_ref, bf16[96,768]{1,0:T(8,128)(2,1)} %reduce-scatter.8.cloned.1.call-done.out_ref, ...), custom_call_target="tpu_custom_call" | custom-call | tf_op jit(solution)/shard_map/reduce_out/pallas_call | solution.py:493
  421.0 1.6 fusion.44
  422.7 1.4 fusion.43
  424.1 1.3 slice.75
  425.3 2.2 copy.59
  427.6 1.7 copy.60
  429.3 1.0 copy.61
  430.3 1.0 copy.62
  (130 shorter events, 3.1 us)
Async XLA Ops:
  7.2 8.5 %copy-start = (s32[8,2]{0,1:T(2,128)S(1)}, s32[8,2]{0,1:T(2,128)}, u32[]{:S(2)}) copy-start(s32[8,2]{0,1:T(2,128)} %param.47) | copy-start | bytes 196
  7.2 116.7 %all-gather.4.cloned.1.call-start = ((), (), s32[]{:S(2)}) async-start(), calls=%async_computation.3 | async-start | bytes 5308416 | tf_op jit(solution)/shard_map/all_gather | solution.py:609
  7.9 143.6 %all-gather.6.cloned.1.call-start = ((), (), s32[]{:S(2)}) async-start(), calls=%async_computation.4 | async-start | bytes 5308416 | tf_op jit(solution)/shard_map/all_gather | solution.py:610
  8.7 336.7 %all-gather.8.cloned.1.call-start = ((), (), s32[]{:S(2)}) async-start(), calls=%async_computation.5 | async-start | bytes 3981312 | tf_op jit(solution)/shard_map/all_gather | solution.py:611
  9.4 344.7 %reduce-scatter.8.cloned.1.call-start = ((), (), s32[]{:S(2)}) async-start(), calls=%async_computation.8 | async-start | bytes 1327104 | tf_op jit(solution)/shard_map/reduce_scatter | solution.py:797
  12.3 91.2 %copy-start.14 = (f32[1,576]{1,0:T(1,128)}, f32[1,576]{1,0:T(1,128)S(1)}, u32[]{:S(2)}) copy-start(f32[1,576]{1,0:T(1,128)S(1)} %stack_reshape.23.scale_ref) | copy-start | bytes 6916
  103.5 15.5 %copy-start.17 = (bf16[768]{0:T(1024)(128)(2,1)S(1)}, bf16[768]{0:T(1024)(128)(2,1)}, u32[]{:S(2)}) copy-start(bf16[768]{0:T(1024)(128)(2,1)} %param.30) | copy-start | bytes 4612
  103.5 15.5 %copy-start.6 = (bf16[768,768]{1,0:T(8,128)(2,1)S(1)}, bf16[768,768]{1,0:T(8,128)(2,1)}, u32[]{:S(2)}) copy-start(bf16[768,768]{1,0:T(8,128)(2,1)} %tok_ref.1) | copy-start | bytes 3538948
  103.5 15.6 %copy-start.26 = (bf16[8,96,768]{2,1,0:T(8,128)(2,1)S(1)}, bf16[8,96,768]{2,1,0:T(8,128)(2,1)}, u32[]{:S(2)}) copy-start(bf16[8,96,768]{2,1,0:T(8,128)(2,1)} %get-tuple-element.35) | copy-start | bytes 3538948
  119.1 2.8 copy-start.18
  119.1 2.8 copy-start.19
  119.1 2.8 copy-start.15
  119.1 2.8 copy-start.27
  119.1 4.2 copy-start.20
  119.1 4.2 copy-start.21
  119.1 4.2 copy-start.22
  121.8 56.5 %copy-start.3 = (f32[768,768]{1,0:T(8,128)}, f32[768,768]{1,0:T(8,128)S(1)}, u32[]{:S(2)}) copy-start(f32[768,768]{1,0:T(8,128)S(1)} %get-tuple-element.77) | copy-start | bytes 7077892
  121.8 2.1 copy-start.10
  121.8 2.1 copy-start.13
  121.8 2.1 copy-start.11
  121.8 2.1 copy-start.16
  160.1 1.3 copy-start.4
  161.4 2.4 copy-start.25
  162.3 16.0 %slice-start = ((s8[4718592]{0:T(1024)(128)(4,1)}), s8[4194304]{0:T(1024)(128)(4,1)S(1)}, s32[]{:S(2)}) async-start(s8[4718592]{0:T(1024)(128)(4,1)} %bitcast.41), calls=%async_computation.9 | async-start | bytes 8388608
  163.3 15.0 %copy-start.5 = (f32[768,768]{1,0:T(8,128)}, f32[768,768]{1,0:T(8,128)S(1)}, u32[]{:S(2)}) copy-start(f32[768,768]{1,0:T(8,128)S(1)} %get-tuple-element.60) | copy-start | bytes 7077892
  163.7 14.6 %slice-start.1 = ((s8[4718592]{0:T(1024)(128)(4,1)}), s8[524288]{0:T(1024)(128)(4,1)S(1)}, s32[]{:S(2)}) async-start(s8[4718592]{0:T(1024)(128)(4,1)} %bitcast.41), calls=%async_computation.10 | async-start | bytes 1048576
  187.4 2.3 copy-start.7
  191.8 162.3 %reduce-scatter.6.cloned.1.call-start = ((), (), s32[]{:S(2)}) async-start(), calls=%async_computation.7 | async-start | bytes 5308416 | tf_op jit(solution)/shard_map/reduce_scatter | solution.py:794
  201.3 152.8 %reduce-scatter.4.cloned.1.call-start = ((), (), s32[]{:S(2)}) async-start(), calls=%async_computation.6 | async-start | bytes 5308416 | tf_op jit(solution)/shard_map/reduce_scatter | solution.py:791
  230.0 61.3 %copy-start.12 = (s32[768]{0:T(1024)S(1)}, s32[768]{0:T(1024)}, u32[]{:S(2)}) copy-start(s32[768]{0:T(1024)} %param.43) | copy-start | bytes 9220
  230.0 62.9 %copy-start.23 = (f32[12]{0:T(128)S(1)}, f32[12]{0:T(128)}, u32[]{:S(2)}) copy-start(f32[12]{0:T(128)} %param.39) | copy-start | bytes 148
  230.0 62.9 %copy-start.24 = (s32[12]{0:T(128)S(1)}, s32[12]{0:T(128)}, u32[]{:S(2)}) copy-start(s32[12]{0:T(128)} %param.42) | copy-start | bytes 148
  345.4 2.0 copy-start.2
  421.0 8.3 %copy-start.9 = (f32[96,3072]{1,0:T(8,128)S(1)}, f32[96,3072]{1,0:T(8,128)}, u32[]{:S(2)}) copy-start(f32[96,3072]{1,0:T(8,128)} %get-tuple-element.112) | copy-start | bytes 3538948
  425.3 5.0 %copy-start.8 = (f32[4,96,768]{2,1,0:T(8,128)S(1)}, f32[4,96,768]{2,1,0:T(8,128)}, u32[]{:S(2)}) copy-start(f32[4,96,768]{2,1,0:T(8,128)} %get-tuple-element.45) | copy-start | bytes 3538948
  427.6 3.7 copy-start.1
Sparse Core Ops, SparseCore 0:
  9.7 76.3 all-gather.3
  87.7 51.2 all-gather.5
  140.6 40.3 all-gather.7
  192.0 48.5 reduce-scatter.7
  242.7 53.3 reduce-scatter.5
  298.2 53.3 reduce-scatter.3

commit v3 on v2

--- a/solution.py
+++ b/solution.py
@@ -26,6 +26,7 @@
 
 NT = (((1,), (1,)), ((), ()))
 NN = (((1,), (0,)), ((), ()))
+TN = (((0,), (0,)), ((), ()))
 
 
 def mm(a, b, dims=NN):
@@ -552,6 +553,21 @@
     )(base, g, weight)
 
 
+(OUT_BIAS, GAIN1, SHIFT1, HIDDEN_SCALE, CON_BIAS, GAIN2, SHIFT2) = range(7)
+(S_OUT_BIAS, S_GAIN1, S_SHIFT1, S_CON_BIAS, S_GAIN2, S_SHIFT2, S_HIDDEN) = range(7)
+
+
+def gelu_parts(x):
+    bell = jnp.exp(-0.5 * (x * x))
+    t = 1.0 / (1.0 + (0.3275911 * root_half) * jnp.abs(x))
+    poly = t * (
+        0.127414796 + t * (-0.142248368 + t * (0.7107068705 + t * (-0.7265760135 + t * 0.5307027145)))
+    )
+    tail = poly * bell
+    cumulative = jnp.where(x < 0.0, tail, 1.0 - tail)
+    return x * cumulative, cumulative + x * bell * density_scale
+
+
 def norm_parts(summed):
     centre = summed - jnp.mean(summed, axis=-1, keepdims=True)
     inverse = lax.rsqrt(jnp.mean(centre * centre, axis=-1, keepdims=True) + epsilon)
@@ -564,6 +580,142 @@
         - jnp.mean(grad_normed, axis=-1, keepdims=True)
         - normed * jnp.mean(grad_normed * normed, axis=-1, keepdims=True)
     )
+
+
+def feed_forward_kernel(
+    steps, chunk,
+    ctx_ref, tok_ref, cot_ref, wo_ref, we_ref, wc_ref, wide_ref, unit_ref,
+    lo_ref, dt1_ref, gctx_ref, sw_ref, su_ref, dwc_ref, dwe_ref, dwo_ref,
+    act_sc, gh_sc, low_sc, gb_sc, ga_sc, ctx_sc, gelu_sc, slope_sc,
+):
+    i = pl.program_id(0)
+    block = tok_ref.shape[0]
+    units = we_ref.shape[1]
+    rows = pl.ds(pl.multiple_of(i * block, block), block)
+
+    @pl.when(i == 0)
+    def _():
+        sw_ref[...] = jnp.zeros_like(sw_ref)
+        su_ref[...] = jnp.zeros_like(su_ref)
+
+    def wide(k):
+        return wide_ref[k : k + 1, :]
+
+    def add_sum(ref, k, cols, value):
+        ref[k : k + 1, cols] += jnp.sum(value, axis=0, keepdims=True)
+
+    full = slice(None)
+    ctx = ctx_ref[...]
+    ctx_sc[:, rows] = ctx
+    summed = mm(ctx, wo_ref[...], TN) + wide(OUT_BIAS) + tok_ref[...].astype(f32)
+    n1, inv1 = norm_parts(summed)
+    s1 = n1 * wide(GAIN1) + wide(SHIFT1)
+    hs = wide(HIDDEN_SCALE)
+    first = s1 * hs
+    low = first.astype(bf16)
+    low_sc[rows, :] = low
+    branch = first + wide(CON_BIAS)
+    for j in range(units // chunk):
+        cols = slice(j * chunk, (j + 1) * chunk)
+        hidden = mm(low, we_ref[:, cols]) + unit_ref[0:1, cols]
+        gelu, slope = gelu_parts(hidden)
+        scale = unit_ref[1:2, cols]
+        gelu_sc[:, cols] = gelu.astype(gelu_sc.dtype)
+        slope_sc[:, cols] = (slope * scale).astype(slope_sc.dtype)
+        act = (gelu * scale).astype(bf16)
+        act_sc[rows, cols] = act
+        branch = branch + mm(act, wc_ref[cols, :])
+    n2, inv2 = norm_parts(branch)
+    s2 = n2 * wide(GAIN2) + wide(SHIFT2)
+    lo_ref[...] = (s2 * hs).astype(bf16)
+    dy = cot_ref[...].astype(f32)
+    e2 = dy * hs
+    add_sum(sw_ref, S_GAIN2, full, e2 * n2)
+    add_sum(sw_ref, S_SHIFT2, full, e2)
+    dt2 = norm_back(e2 * wide(GAIN2), n2, inv2)
+    gb = dt2.astype(bf16)
+    gb_sc[rows, :] = gb
+    add_sum(sw_ref, S_CON_BIAS, full, gb.astype(f32))
+    d_first = dt2
+    for j in range(units // chunk):
+        cols = slice(j * chunk, (j + 1) * chunk)
+        d_act = mm(gb, wc_ref[cols, :], NT)
+        add_sum(su_ref, 1, cols, d_act * gelu_sc[:, cols].astype(f32))
+        gh = d_act * slope_sc[:, cols].astype(f32)
+        add_sum(su_ref, 0, cols, gh)
+        gh = gh.astype(bf16)
+        gh_sc[rows, cols] = gh
+        d_first = d_first + mm(gh, we_ref[:, cols], NT)
+    e1 = d_first * hs
+    add_sum(sw_ref, S_GAIN1, full, e1 * n1)
+    add_sum(sw_ref, S_SHIFT1, full, e1)
+    add_sum(sw_ref, S_HIDDEN, full, dy * s2 + d_first * s1)
+    dt1 = norm_back(e1 * wide(GAIN1), n1, inv1)
+    dt1_ref[...] = dt1
+    ga = dt1.astype(bf16)
+    ga_sc[rows, :] = ga
+    add_sum(sw_ref, S_OUT_BIAS, full, ga.astype(f32))
+    gctx_ref[...] = mm(wo_ref[...], ga, NT).astype(bf16)
+
+    @pl.when(i == steps - 1)
+    def _():
+        for j in range(units // chunk):
+            cols = slice(j * chunk, (j + 1) * chunk)
+            dwc_ref[cols, :] = mm(act_sc[:, cols], gb_sc[...], TN).astype(bf16)
+            dwe_ref[:, cols] = mm(low_sc[...], gh_sc[:, cols], TN).astype(bf16)
+        dwo_ref[...] = mm(ctx_sc[...], ga_sc[...]).astype(bf16)
+
+
+def feed_forward(ctx_t, tokens, cotangent, wo, we, wc, wide, unit, steps=3, chunk=1024, keep=f32):
+    rows, d = tokens.shape
+    units = we.shape[1]
+    block = rows // steps
+    tile = pl.BlockSpec((block, d), lambda i: (i, 0))
+    lanes = pl.BlockSpec((d, block), lambda i: (0, i))
+
+    def once(shape):
+        return pl.BlockSpec(shape, lambda i: (0, 0), pipeline_mode=pl.Buffered(1))
+
+    def const(shape):
+        return pl.BlockSpec(shape, lambda i: (0, 0))
+
+    return pl.pallas_call(
+        functools.partial(feed_forward_kernel, steps, chunk),
+        out_shape=(
+            jax.ShapeDtypeStruct((rows, d), bf16),
+            jax.ShapeDtypeStruct((rows, d), f32),
+            jax.ShapeDtypeStruct((d, rows), bf16),
+            jax.ShapeDtypeStruct((8, d), f32),
+            jax.ShapeDtypeStruct((8, units), f32),
+            jax.ShapeDtypeStruct((units, d), bf16),
+            jax.ShapeDtypeStruct((d, units), bf16),
+            jax.ShapeDtypeStruct((d, d), bf16),
+        ),
+        grid=(steps,),
+        in_specs=[
+            lanes, tile, tile, once((d, d)), once((d, units)), once((units, d)), once((8, d)), once((8, units)),
+        ],
+        out_specs=(
+            tile, tile, lanes, once((8, d)), once((8, units)), once((units, d)), once((d, units)), once((d, d)),
+        ),
+        scratch_shapes=[
+            pltpu.VMEM((rows, units), bf16),
+            pltpu.VMEM((rows, units), bf16),
+            pltpu.VMEM((rows, d), bf16),
+            pltpu.VMEM((rows, d), bf16),
+            pltpu.VMEM((rows, d), bf16),
+            pltpu.VMEM((d, rows), bf16),
+            pltpu.VMEM((block, units), keep),
+            pltpu.VMEM((block, units), keep),
+        ],
+        compiler_params=pltpu.CompilerParams(vmem_limit_bytes=60 * 2**20),
+        cost_estimate=pl.CostEstimate(
+            flops=rows * d * (12 * units + 6 * d),
+            bytes_accessed=4 * d * (4 * units + 2 * d) + 12 * rows * d,
+            transcendentals=2 * rows * units,
+        ),
+        name="feed_forward",
+    )(ctx_t, tokens, cotangent, wo, we, wc, wide, unit)
 
 
 def local(
@@ -609,10 +761,6 @@
     full_expand = lax.all_gather(expand_weight, "wt", axis=0, tiled=True)
     full_contract = lax.all_gather(contract_weight, "wt", axis=0, tiled=True)
     full_attention = lax.all_gather(attention_weight, "wt", axis=0, tiled=True)
-    position = seq_index * row_count + jnp.arange(row_count, dtype=jnp.int32)
-    group_local = position // GLEN
-    own_groups = jnp.arange(GRP_WT, dtype=jnp.int32)
-    chosen = group_local[:, None] == own_groups[None, :]
     first_group = wt_index * GRP_WT
     own_attention = lax.dynamic_slice_in_dim(attention_mask, first_group, GRP_WT, 0).astype(
         jnp.float32
@@ -620,13 +768,24 @@
     own_feedforward = lax.dynamic_slice_in_dim(feedforward_mask, first_group, GRP_WT, 0).astype(
         jnp.float32
     )
-    attention_rows = jnp.sum(jnp.where(chosen, own_attention[None, :], 0.0), axis=1)
-    feedforward_rows = jnp.sum(jnp.where(chosen, own_feedforward[None, :], 0.0), axis=1)
     head_scale = head_mask.astype(jnp.float32) * head_gate
     hidden_scale = hidden_mask.astype(jnp.float32) * hidden_gate
     unit_scale = unit_mask.astype(jnp.float32) * unit_gate
-    first_gain_f = first_gain.astype(jnp.float32)
-    second_gain_f = second_gain.astype(jnp.float32)
+    wide_table = jnp.stack(
+        [
+            output_bias.astype(f32),
+            first_gain.astype(f32),
+            first_shift.astype(f32),
+            hidden_scale,
+            contract_bias.astype(f32),
+            second_gain.astype(f32),
+            second_shift.astype(f32),
+            hidden_scale,
+        ],
+        axis=0,
+    )
+    unit_row = unit_scale * own_feedforward[0]
+    unit_table = jnp.stack([expand_bias.astype(f32)] + [unit_row] * 7, axis=0)
     bias_table = jnp.stack(
         [
             query_bias.astype(jnp.float32).reshape(head_count, head_size),
@@ -655,72 +814,21 @@
         1,
         "context_out",
     )
-    attn_out = jnp.einsum(
-        "it,id->td", context_t, full_output, preferred_element_type=jnp.float32
-    ) + output_bias.astype(jnp.float32)
-    normed_one, inverse_one = norm_parts(tokens.astype(jnp.float32) + attn_out)
-    shaped_one = normed_one * first_gain_f + first_shift.astype(jnp.float32)
-    first_out = shaped_one * hidden_scale
-    first_low = first_out.astype(jnp.bfloat16)
-    hidden = jnp.dot(
-        first_low, full_expand, preferred_element_type=jnp.float32
-    ) + expand_bias.astype(jnp.float32)
-    gelu_out = jax.nn.gelu(hidden, approximate=False)
-    unit_rows_scale = unit_scale[None, :] * feedforward_rows[:, None]
-    activated = (gelu_out * unit_rows_scale).astype(jnp.bfloat16)
-    branch = jnp.dot(
-        activated, full_contract, preferred_element_type=jnp.float32
-    ) + contract_bias.astype(jnp.float32)
-    normed_two, inverse_two = norm_parts(first_out + branch)
-    shaped_two = normed_two * second_gain_f + second_shift.astype(jnp.float32)
-    layer_output = (shaped_two * hidden_scale).astype(jnp.bfloat16)
-    back_attention, back_output, back_expand, back_contract = (
-        full_attention,
-        full_output,
-        full_expand,
-        full_contract,
-    )
-    cotangent = output_cotangent.astype(jnp.float32)
-    grad_shaped_two = cotangent * hidden_scale
-    second_gain_grad = jnp.sum(grad_shaped_two * normed_two, axis=0)
-    second_shift_grad = jnp.sum(grad_shaped_two, axis=0)
-    grad_total_two = norm_back(grad_shaped_two * second_gain_f, normed_two, inverse_two)
-    grad_branch = grad_total_two.astype(jnp.bfloat16)
-    contract_bias_grad = jnp.sum(grad_branch.astype(jnp.float32), axis=0)
-    contract_weight_grad = jnp.einsum(
-        "ti,td->id", activated, grad_branch, preferred_element_type=jnp.float32
-    )
-    grad_activated = jnp.einsum(
-        "td,id->ti", grad_branch, back_contract, preferred_element_type=jnp.float32
-    )
-    unit_gate_grad = unit_mask.astype(jnp.float32) * jnp.sum(
-        grad_activated * gelu_out * feedforward_rows[:, None], axis=0
-    )
-    cumulative = 0.5 * (1.0 + lax.erf(hidden * root_half))
-    gelu_slope = cumulative + hidden * jnp.exp(-0.5 * hidden * hidden) * density_scale
-    grad_hidden = (grad_activated * unit_rows_scale * gelu_slope).astype(jnp.bfloat16)
-    expand_bias_grad = jnp.sum(grad_hidden.astype(jnp.float32), axis=0)
-    expand_weight_grad = jnp.einsum(
-        "td,tf->df", first_low, grad_hidden, preferred_element_type=jnp.float32
-    )
-    grad_first = grad_total_two + jnp.einsum(
-        "tf,df->td", grad_hidden, back_expand, preferred_element_type=jnp.float32
-    )
-    grad_shaped_one = grad_first * hidden_scale
-    first_gain_grad = jnp.sum(grad_shaped_one * normed_one, axis=0)
-    first_shift_grad = jnp.sum(grad_shaped_one, axis=0)
-    hidden_gate_grad = hidden_mask.astype(jnp.float32) * jnp.sum(
-        cotangent * shaped_two + grad_first * shaped_one, axis=0
-    )
-    grad_total_one = norm_back(grad_shaped_one * first_gain_f, normed_one, inverse_one)
-    grad_attn = grad_total_one.astype(jnp.bfloat16)
-    output_bias_grad = jnp.sum(grad_attn.astype(jnp.float32), axis=0)
-    output_weight_grad = jnp.einsum(
-        "it,td->id", context_t, grad_attn, preferred_element_type=jnp.float32
-    )
-    grad_context_t = jnp.einsum(
-        "td,id->it", grad_attn, back_output, preferred_element_type=jnp.float32
-    ).astype(jnp.bfloat16)
+    (
+        layer_output,
+        grad_total_one,
+        grad_context_t,
+        wide_sums,
+        unit_sums,
+        contract_weight_grad,
+        expand_weight_grad,
+        output_weight_grad,
+    ) = feed_forward(
+        context_t, tokens, output_cotangent, full_output, full_expand, full_contract, wide_table, unit_table
+    )
+    con_piece = lax.psum_scatter(contract_weight_grad, "wt", scatter_dimension=0, tiled=True)
+    exp_piece = lax.psum_scatter(expand_weight_grad, "wt", scatter_dimension=0, tiled=True)
+    out_piece = lax.psum_scatter(output_weight_grad, "wt", scatter_dimension=0, tiled=True)
     arriving = exchange(
         grad_context_t,
         (local_ctx, GLEN),
@@ -761,22 +869,24 @@
     attention_weight_grad = jnp.einsum(
         "td,tc->dc", tokens_all, grad_packed, preferred_element_type=jnp.float32
     )
-    tokens_grad = tokens_back(grad_total_one, grad_pieces, back_attention)
+    tokens_grad = tokens_back(grad_total_one, grad_pieces, full_attention)
     width_rows = jnp.stack(
         [
             query_bias_grad,
             value_bias_grad,
-            output_bias_grad,
-            first_gain_grad,
-            first_shift_grad,
-            contract_bias_grad,
-            second_gain_grad,
-            second_shift_grad,
-            hidden_gate_grad,
+            wide_sums[S_OUT_BIAS],
+            wide_sums[S_GAIN1],
+            wide_sums[S_SHIFT1],
+            wide_sums[S_CON_BIAS],
+            wide_sums[S_GAIN2],
+            wide_sums[S_SHIFT2],
+            wide_sums[S_HIDDEN] * hidden_mask.astype(f32),
         ],
         axis=0,
     )
-    unit_rows = jnp.stack([expand_bias_grad, unit_gate_grad], axis=0)
+    unit_rows = jnp.stack(
+        [unit_sums[0], unit_sums[1] * (unit_mask.astype(f32) * own_feedforward[0])], axis=0
+    )
     own_wide, own_units = model_width // wt_count, unit_gate.shape[0] // wt_count
     by_shard = jnp.concatenate(
         [
@@ -788,15 +898,6 @@
     )
     used = by_shard.shape[1]
     by_shard = jnp.pad(by_shard, ((0, 0), (0, -used % 1024))).reshape(wt_count, -1, 128)
-    con_piece = lax.psum_scatter(
-        contract_weight_grad.astype(bf16), "wt", scatter_dimension=0, tiled=True
-    )
-    exp_piece = lax.psum_scatter(
-        expand_weight_grad.astype(bf16), "wt", scatter_dimension=0, tiled=True
-    )
-    out_piece = lax.psum_scatter(
-        output_weight_grad.astype(bf16), "wt", scatter_dimension=0, tiled=True
-    )
     con_sum, exp_sum, out_sum, att_sum, vec_sum = reduce_out(
         wt_count,
         con_piece.reshape(seq_count, own_wide, model_width),

time: 445 us -> 405 us (0.910); the launches traced: 438 us -> 405 us
  matrix products: 94.4 us -> 6.6 us
  Pallas kernels: 293 us -> 334 us
  waiting for transfers between devices: 2.16 us -> 19.8 us
  other arithmetic: 7.13 us -> 2.06 us
    dot_general x9 -> x0, matrix products: 87.8 us -> none  [the longest x1 27.6 us: local(): jnp.dot(first_low, full_expand, preferred_element_type=jnp.float32)]
    pallas_call x0 -> x1, Pallas kernels: none -> 56.9 us  [feed_forward(): pl.pallas_call(functools.partial(feed_forward_kernel, steps, chunk), out_...]
    pallas_call x1, Pallas kernels: 66.8 us -> 46.2 us  [reduce_out(): pl.pallas_call(functools.partial(reduce_kernel, n), out_shape=(jax.ShapeD...]
    all_gather x1, waiting for transfers between devices: 0.01 us -> 16.6 us  [local(): full_contract = lax.all_gather(contract_weight, 'wt', axis=0, tiled=True)]
    reduce_sum x5 -> x0, other arithmetic: 5.08 us -> none  [the longest x1 2.31 us: local(): output_bias_grad = jnp.sum(grad_attn.astype(jnp.float32), axis=0)]
    pallas_call x3, Pallas kernels: 73.4 us -> 78.2 us  [exchange(): pl.pallas_call(functools.partial(exchange_kernel, src_of, dst_of), out_sh...]
    unnamed x66 -> x50, local copies, waits for them, and re-layouts: 10 us -> 8.72 us
  transfers between devices with their start and end apart: 6 -> 6, of which waited for: 0 -> 1; matrix products, arithmetic and copies ran while one was open for 26% -> 5% of each run, Pallas kernels for 52% -> 71%
where the time goes in v3:
time: 405 us
  Pallas kernels  334 us (82%)
  local copies, waits for them, and re-layouts  25.4 us (6%)
  waiting for transfers between devices  19.8 us (5%)
  between operations  16.4 us (4%)
  matrix products  6.6 us (2%)
    pallas_call x3, Pallas kernels, exchange(): pl.pallas_call(functools.partial(exchange_kernel, src_of, dst_of), out_sh...  78.2 us
    pallas_call x1, Pallas kernels, attend_back(): pl.pallas_call(functools.partial(attend_back_kernel, heads), out_shape=(j...  59.7 us
    pallas_call x1, Pallas kernels, feed_forward(): pl.pallas_call(functools.partial(feed_forward_kernel, steps, chunk), out_...  56.9 us
    pallas_call x1, Pallas kernels, reduce_out(): pl.pallas_call(functools.partial(reduce_kernel, n), out_shape=(jax.ShapeD...  46.2 us
    pallas_call x1, Pallas kernels, gather_in(): pl.pallas_call(functools.partial(gather_kernel, n), out_shape=(jax.ShapeD...  45.7 us
    pallas_call x1, Pallas kernels, attend(): pl.pallas_call(functools.partial(attend_kernel, heads), out_shape=(jax.Sh...  40.8 us
    all_gather x1, waiting for transfers between devices, local(): full_contract = lax.all_gather(contract_weight, 'wt', axis=0, tiled=True)  16.6 us
    unnamed x50, local copies, waits for them, and re-layouts  8.72 us
  transfers between devices with their start and end apart: 6, of which 1 were waited for; matrix products, arithmetic and copies ran while one was open for 5% of the time, Pallas kernels for 71%

profile of v3, /device:TPU:0, one launch (start us, length us, event | category | flops | bytes accessed | tf_op | source)
XLA Modules:
  0.0 404.7 jit_solution(9646880457747839984)
XLA Ops:
  7.3 0.7 all-gather.4.cloned.1.call-update
  8.0 0.7 all-gather.6.cloned.1.call-update
  8.7 0.7 all-gather.8.cloned.1.call-update
  9.5 1.2 dynamic_slice.28
  11.4 0.7 convert_multiply_fusion.2
  12.2 0.1 stack_reshape.23.scale_ref
  12.3 0.8 reshape.98
  13.1 0.8 reshape.99
  14.0 0.1 stack_reshape.22
  14.1 0.7 dynamic-slice_reduce_fusion.lens_ref
  14.8 1.7 constant_dynamic-slice_fusion.cols_ref
  16.4 45.7 %gather_in.1 = (bf16[3072,768]{1,0:T(8,128)(2,1)}, bf16[8,96,576]{2,1,0:T(8,128)(2,1)}, bf16[8,96,768]{2,1,0:T(8,128)(2,1)}) custom-call(bf16[768,768]{1,0:T(8,128)(2,1)} %tok_ref.3, bf16[96,576]{1,0:T(8,128)(2,1)} %constant_dynamic-slice_fusion.cols_ref, bf16[96,768]{1,0:T(8,128)(2,1)} %out_ref.1), custom_call_target="tpu_custom_call" | custom-call | tf_op jit(solution)/shard_map/gather_in/pallas_call | solution.py:342
  62.1 0.6 pad_maximum_fusion.1.vec_ref
  62.7 40.8 %attend.1 = (bf16[3072,576]{1,0:T(8,128)(2,1)}, bf16[192,3072]{1,0:T(8,128)(2,1)}, f32[3,1,3072]{2,1,0:T(1,128)}) custom-call(s32[2]{0:T(128)} %dynamic-slice_reduce_fusion.lens_ref, bf16[3072,768]{1,0:T(8,128)(2,1)} %get-tuple-element.40.tok_ref, bf16[768,576]{1,0:T(8,128)(2,1)} %bitcast.46, f32[2,576]{1,0:T(2,128)} %pad_maximum_fusion.1.vec_ref), custom_call_target="tpu_custom_call" | custom-call | flops 20434649088 | bytes 8257536 | tf_op jit(solution)/shard_map/attend/pallas_call | solution.py:101
  103.6 15.6 %context_out.1.ctx_ref = bf16[768,768]{1,0:T(8,128)(2,1)} custom-call(bf16[192,3072]{1,0:T(8,128)(2,1)} %get-tuple-element.42.x_ref.ctx_ref), custom_call_target="tpu_custom_call" | custom-call | tf_op jit(solution)/shard_map/context_out/pallas_call | solution.py:384
  119.3 0.6 dynamic_slice.29
  120.7 0.8 stack.122.unit_ref
  121.5 0.6 stack.118.wide_ref
  122.2 16.6 %all-gather.6.cloned.1.call-done.wc_ref = bf16[3072,768]{1,0:T(8,128)(2,1)} async-done(((bf16[384,768]{1,0:T(8,128)(2,1)}), bf16[3072,768]{1,0:T(8,128)(2,1)}) %all-gather.6.cloned.1.call-update) | async-done | bytes 4718608 | tf_op jit(solution)/shard_map/all_gather | solution.py:762
  138.8 56.9 %feed_forward.1 = (bf16[768,768]{1,0:T(8,128)(2,1)}, f32[768,768]{1,0:T(8,128)}, bf16[768,768]{1,0:T(8,128)(2,1)}, f32[8,768]{1,0:T(8,128)}, f32[8,3072]{1,0:T(8...) custom-call(bf16[768,768]{1,0:T(8,128)(2,1)} %context_out.1.ctx_ref, ...), custom_call_target="tpu_custom_call" | custom-call | flops 24461180928 | bytes 49545216 | tf_op jit(solution)/shard_map/feed_forward/pallas_call | solution.py:682
  195.8 0.5 reduce-scatter.4.cloned.1.call-update
  196.4 0.5 reduce-scatter.6.cloned.1.call-update
  197.0 1.0 slice_reduce_fusion
  198.0 16.9 %context_grad_in.1.gctx_ref = bf16[192,3072]{1,0:T(8,128)(2,1)} custom-call(bf16[768,768]{1,0:T(8,128)(2,1)} %get-tuple-element.47.x_ref), custom_call_target="tpu_custom_call" | custom-call | tf_op jit(solution)/shard_map/context_grad_in/pallas_call | solution.py:384
  214.9 59.7 %attend_back.1 = (bf16[3072,576]{1,0:T(8,128)(2,1)}, f32[8,576]{1,0:T(8,128)}, f32[8,192]{1,0:T(8,128)}) custom-call(s32[2]{0:T(128)} %dynamic-slice_reduce_fusion.lens_ref, bf16[3072,576]{1,0:T(8,128)(2,1)} %get-tuple-element.46.packed_ref, bf16[192,3072]{1,0:T(8,128)(2,1)} %get-tuple-element.42.x_ref.ctx_ref, bf16[192,3072]{1,0:T(8,128)(2,1)} %context_grad_in.1.gctx_ref, ...), custom_call_target="tpu_custom_call" | custom-call | flops 44291850240 | bytes 10616832 | tf_op jit(solution)/shard_map/attend_back/pallas_call | solution.py:205
  274.6 0.7 slice_reduce_fusion.2
  275.4 0.1 stack.123
  275.5 0.1 dynamic_update_slice.13
  275.8 0.1 dynamic_update_slice.14
  276.4 0.7 slice_reduce_fusion.5
  277.1 0.1 reshape_squeeze.9
  277.2 0.1 reduce_sum.9
  277.3 0.4 multiply_dynamic-update-slice_fusion
  277.7 0.1 concatenate.5
  277.8 0.6 copy.48
  278.5 6.6 %convolution_convert_fusion = bf16[768,576]{0,1:T(8,128)(2,1)S(1)} fusion(bf16[3072,768]{1,0:T(8,128)(2,1)} %get-tuple-element.40.tok_ref, bf16[3072,576]{1,0:T(8,128)(2,1)} %get-tuple-element.49), kind=kOutput, calls=%fused_computation | convolution fusion | flops 2718351360 | bytes 9142272 | tf_op jit(solution)/shard_map/td,tc->dc/dot_general | solution.py:869
  285.1 1.3 copy.44
  286.4 45.7 %packed_grad_out.1.g_ref = bf16[4,768,576]{2,1,0:T(8,128)(2,1)} custom-call(bf16[4,768,576]{2,1,0:T(8,128)(2,1)} %bitcast.27), custom_call_target="tpu_custom_call" | custom-call | tf_op jit(solution)/shard_map/packed_grad_out/pallas_call | solution.py:384
  332.1 2.0 copy-done.2
  334.1 6.8 %tokens_back.1 = f32[768,768]{1,0:T(8,128)} custom-call(f32[768,768]{1,0:T(8,128)S(1)} %copy-done.3, bf16[4,768,576]{2,1,0:T(8,128)(2,1)} %packed_grad_out.1.g_ref, bf16[768,2304]{1,0:T(8,128)(2,1)S(1)} %copy-done.2), custom_call_target="tpu_custom_call" | custom-call | flops 2717908992 | bytes 8257536 | tf_op jit(solution)/shard_map/tokens_back/pallas_call | solution.py:538
  340.9 46.2 %reduce_out.1 = (f32[4,96,768]{2,1,0:T(8,128)}, f32[96,3072]{1,0:T(8,128)}, f32[96,768]{1,0:T(8,128)}, f32[96,2304]{1,0:T(8,128)}, f32[16,128]{1,0:T(8,128)}) custom-call(bf16[4,96,768]{2,1,0:T(8,128)(2,1)} %bitcast.36, bf16[96,3072]{1,0:T(8,128)(2,1)} %reduce-scatter.6.cloned.1.call-done.exp_ref, bf16[96,768]{1,0:T(8,128)(2,1)} %reduce-scatter.8.cloned.1.call-done.out_ref, ...), custom_call_target="tpu_custom_call" | custom-call | tf_op jit(solution)/shard_map/reduce_out/pallas_call | solution.py:494
  387.1 1.6 fusion.3
  388.7 1.4 fusion.2
  390.2 1.3 slice.97
  391.4 2.2 copy.58
  393.7 1.7 copy.59
  395.4 1.0 copy.60
  396.4 1.0 copy.61
  (93 shorter events, 1.5 us)
Async XLA Ops:
  7.2 6.9 %copy-start = (s32[8,2]{0,1:T(2,128)S(1)}, s32[8,2]{0,1:T(2,128)}, u32[]{:S(2)}) copy-start(s32[8,2]{0,1:T(2,128)} %param.47) | copy-start | bytes 196
  7.2 115.0 %all-gather.4.cloned.1.call-start = ((), (), s32[]{:S(2)}) async-start(), calls=%async_computation.3 | async-start | bytes 5308416 | tf_op jit(solution)/shard_map/all_gather | solution.py:761
  7.9 130.9 %all-gather.6.cloned.1.call-start = ((), (), s32[]{:S(2)}) async-start(), calls=%async_computation.4 | async-start | bytes 5308416 | tf_op jit(solution)/shard_map/all_gather | solution.py:762
  8.7 323.4 %all-gather.8.cloned.1.call-start = ((), (), s32[]{:S(2)}) async-start(), calls=%async_computation.5 | async-start | bytes 3981312 | tf_op jit(solution)/shard_map/all_gather | solution.py:763
  9.4 331.5 %reduce-scatter.8.cloned.1.call-start = ((), (), s32[]{:S(2)}) async-start(), calls=%async_computation.8 | async-start | bytes 1327104 | tf_op jit(solution)/shard_map/reduce_scatter | solution.py:831
  12.3 91.2 %copy-start.10 = (f32[1,576]{1,0:T(1,128)}, f32[1,576]{1,0:T(1,128)S(1)}, u32[]{:S(2)}) copy-start(f32[1,576]{1,0:T(1,128)S(1)} %stack_reshape.23.scale_ref) | copy-start | bytes 6916
  103.5 15.8 %copy-start.21 = (s32[8]{0:T(128)S(1)}, s32[8]{0:T(128)}, u32[]{:S(2)}) copy-start(s32[8]{0:T(128)} %param.46) | copy-start | bytes 100
  103.5 17.0 %copy-start.11 = (bf16[3072]{0:T(1024)(128)(2,1)S(1)}, bf16[3072]{0:T(1024)(128)(2,1)}, u32[]{:S(2)}) copy-start(bf16[3072]{0:T(1024)(128)(2,1)} %param.34) | copy-start | bytes 18436
  103.5 17.0 %copy-start.8 = (s32[768]{0:T(1024)S(1)}, s32[768]{0:T(1024)}, u32[]{:S(2)}) copy-start(s32[768]{0:T(1024)} %param.43) | copy-start | bytes 9220
  103.5 17.0 %copy-start.12 = (f32[768]{0:T(1024)S(1)}, f32[768]{0:T(1024)}, u32[]{:S(2)}) copy-start(f32[768]{0:T(1024)} %param.40) | copy-start | bytes 9220
  103.5 17.0 %copy-start.13 = (bf16[768]{0:T(1024)(128)(2,1)S(1)}, bf16[768]{0:T(1024)(128)(2,1)}, u32[]{:S(2)}) copy-start(bf16[768]{0:T(1024)(128)(2,1)} %param.30) | copy-start | bytes 4612
  103.6 17.0 %copy-start.14 = (bf16[768]{0:T(1024)(128)(2,1)S(1)}, bf16[768]{0:T(1024)(128)(2,1)}, u32[]{:S(2)}) copy-start(bf16[768]{0:T(1024)(128)(2,1)} %param.31) | copy-start | bytes 4612
  103.6 17.1 %copy-start.15 = (bf16[768]{0:T(1024)(128)(2,1)S(1)}, bf16[768]{0:T(1024)(128)(2,1)}, u32[]{:S(2)}) copy-start(bf16[768]{0:T(1024)(128)(2,1)} %param.32) | copy-start | bytes 4612
  103.6 17.1 %copy-start.16 = (bf16[768]{0:T(1024)(128)(2,1)S(1)}, bf16[768]{0:T(1024)(128)(2,1)}, u32[]{:S(2)}) copy-start(bf16[768]{0:T(1024)(128)(2,1)} %param.36) | copy-start | bytes 4612
  103.6 17.1 %copy-start.17 = (bf16[768]{0:T(1024)(128)(2,1)S(1)}, bf16[768]{0:T(1024)(128)(2,1)}, u32[]{:S(2)}) copy-start(bf16[768]{0:T(1024)(128)(2,1)} %param.37) | copy-start | bytes 4612
  103.6 17.1 %copy-start.18 = (bf16[768]{0:T(1024)(128)(2,1)S(1)}, bf16[768]{0:T(1024)(128)(2,1)}, u32[]{:S(2)}) copy-start(bf16[768]{0:T(1024)(128)(2,1)} %param.38) | copy-start | bytes 4612
  103.6 17.1 %copy-start.6 = (s32[3072]{0:T(1024)S(1)}, s32[3072]{0:T(1024)}, u32[]{:S(2)}) copy-start(s32[3072]{0:T(1024)} %param.44) | copy-start | bytes 36868
  103.6 17.1 %copy-start.9 = (f32[3072]{0:T(1024)S(1)}, f32[3072]{0:T(1024)}, u32[]{:S(2)}) copy-start(f32[3072]{0:T(1024)} %param.41) | copy-start | bytes 36868
  195.8 145.1 %reduce-scatter.4.cloned.1.call-start = ((), (), s32[]{:S(2)}) async-start(), calls=%async_computation.6 | async-start | bytes 5308416 | tf_op jit(solution)/shard_map/reduce_scatter | solution.py:829
  196.4 144.5 %reduce-scatter.6.cloned.1.call-start = ((), (), s32[]{:S(2)}) async-start(), calls=%async_computation.7 | async-start | bytes 5308416 | tf_op jit(solution)/shard_map/reduce_scatter | solution.py:830
  214.9 61.1 %copy-start.7 = (f32[8,768]{1,0:T(8,128)S(1)}, f32[8,768]{1,0:T(8,128)}, u32[]{:S(2)}) copy-start(f32[8,768]{1,0:T(8,128)} %get-tuple-element.54) | copy-start | bytes 73732
  214.9 62.4 %copy-start.19 = (f32[12]{0:T(128)S(1)}, f32[12]{0:T(128)}, u32[]{:S(2)}) copy-start(f32[12]{0:T(128)} %param.39) | copy-start | bytes 148
  214.9 62.4 %copy-start.20 = (s32[12]{0:T(128)S(1)}, s32[12]{0:T(128)}, u32[]{:S(2)}) copy-start(s32[12]{0:T(128)} %param.42) | copy-start | bytes 148
  286.4 45.7 %copy-start.3 = (f32[768,768]{1,0:T(8,128)S(1)}, f32[768,768]{1,0:T(8,128)}, u32[]{:S(2)}) copy-start(f32[768,768]{1,0:T(8,128)} %get-tuple-element.45.base_ref) | copy-start | bytes 7077892
  332.1 2.0 copy-start.2
  387.1 8.3 %copy-start.5 = (f32[96,3072]{1,0:T(8,128)S(1)}, f32[96,3072]{1,0:T(8,128)}, u32[]{:S(2)}) copy-start(f32[96,3072]{1,0:T(8,128)} %get-tuple-element.104) | copy-start | bytes 3538948
  391.4 5.0 %copy-start.4 = (f32[4,96,768]{2,1,0:T(8,128)S(1)}, f32[4,96,768]{2,1,0:T(8,128)}, u32[]{:S(2)}) copy-start(f32[4,96,768]{2,1,0:T(8,128)} %get-tuple-element.61) | copy-start | bytes 3538948
  393.7 3.7 copy-start.1
Sparse Core Ops, SparseCore 0:
  9.7 75.6 all-gather.3
  87.1 51.7 all-gather.5
  140.5 40.3 all-gather.7
  195.9 33.0 reduce-scatter.7
  231.1 52.7 reduce-scatter.3
  286.1 53.3 reduce-scatter.5

commit v4 on v3

--- a/solution.py
+++ b/solution.py
@@ -56,9 +56,9 @@
         rows = pl.ds(pl.multiple_of(i * TQ, TQ), TQ)
         x = mm(tok_ref[rows, :], w_ref[...]) + vec_ref[0:1, :]
         x = (x * vec_ref[1:2, :]).astype(bf16)
-        packed_ref[rows, :] = x
         for h in range(heads):
             at = 3 * HD * h
+            packed_ref[h, rows, :] = x[:, at : at + 3 * HD]
             q_sc[h, rows, :] = x[:, at : at + HD]
             k_sc[h, rows, :] = x[:, at + HD : at + 2 * HD]
             vt_sc[h, 0:HD, rows] = x[:, at + 2 * HD : at + 3 * HD].T
@@ -101,7 +101,7 @@
     return pl.pallas_call(
         functools.partial(attend_kernel, heads),
         out_shape=(
-            jax.ShapeDtypeStruct((GLEN, width), bf16),
+            jax.ShapeDtypeStruct((heads, GLEN, 3 * HD), bf16),
             jax.ShapeDtypeStruct((HD * heads, GLEN), bf16),
             jax.ShapeDtypeStruct((heads, 1, GLEN), f32),
         ),
@@ -123,113 +123,152 @@
 
 
 def attend_back_kernel(
-    heads, lens_ref, packed_ref, ctx_ref, gctx_ref, lse_ref, scale_ref,
-    out_ref, sums_ref, gate_ref,
-    q_sc, k_sc, v_sc, kt_sc, g_sc, delta_sc, dqt_sc, dk_sc, dv_sc,
+    place_ref, packed_ref, ctx_ref, gctx_ref, lse_ref, scale_ref,
+    out_ref, own_ref, p1_ref, p2_ref, p3_ref, sums_ref, gate_ref,
+    q_sc, k_sc, v_sc, kt_sc, delta_sc, dqt_sc, dk_sc, dv_sc,
 ):
     def split(i, carry):
         rows = pl.ds(pl.multiple_of(i * TQ, TQ), TQ)
-        x = packed_ref[rows, :]
+        x = packed_ref[0, rows, :]
         inner = gctx_ref[:, rows].astype(f32) * ctx_ref[:, rows].astype(f32)
-        for h in range(heads):
-            at = 3 * HD * h
-            q_sc[h, rows, :] = x[:, at : at + HD]
-            k = x[:, at + HD : at + 2 * HD]
-            k_sc[h, rows, :] = k
-            kt_sc[h, :, rows] = k.T
-            v_sc[h, rows, :] = x[:, at + 2 * HD : at + 3 * HD]
-            g_sc[h, :, rows] = gctx_ref[HD * h : HD * (h + 1), rows]
-            delta_sc[h, :, rows] = jnp.sum(inner[HD * h : HD * (h + 1), :], axis=0, keepdims=True)
+        delta_sc[:, rows] = jnp.sum(inner, axis=0, keepdims=True)
+        q_sc[rows, :] = x[:, 0:HD]
+        k = x[:, HD : 2 * HD]
+        k_sc[rows, :] = k
+        kt_sc[:, rows] = k.T
+        v_sc[rows, :] = x[:, 2 * HD : 3 * HD]
         return carry
 
     lax.fori_loop(0, GLEN // TQ, split, 0)
     dk_sc[...] = jnp.zeros_like(dk_sc)
     dv_sc[...] = jnp.zeros_like(dv_sc)
 
-    def one_head(h, carry):
-        def tile(q_at, own_at, own_len):
-            rows = pl.ds(q_at, TQ)
-            q = q_sc[h, rows, :]
-            g = g_sc[h, :, rows]
-            lse = lse_ref[h, :, rows]
-            delta = delta_sc[h, :, rows]
-            dq = jnp.zeros((HD, TQ), f32)
-            pieces = [(j * KC, PROMPT // KC) for j in range(PROMPT // KC)]
-            pieces = [c for c, _ in pieces] + [own_at + j * KC for j in range(own_len // KC)]
-            for start in pieces:
-                keys = pl.ds(start, KC)
-                s = mm(k_sc[h, keys, :], q, NT)
-                p = jnp.exp2(s * exp2_scale - lse)
-                dp = mm(v_sc[h, keys, :], g)
-                ds = (p * (dp - delta)).astype(bf16)
-                dv_sc[h, keys, :] += mm(p.astype(bf16), g, NT)
-                dk_sc[h, keys, :] += mm(ds, q)
-                dq = dq + mm(kt_sc[h, :, keys], ds)
-            dqt_sc[h, :, rows] = dq * score_scale
-
-        query_tiles(lens_ref[0] == SHORT, tile)
-        return carry
-
-    lax.fori_loop(0, heads, one_head, 0)
+    def tile(q_at, own_at, own_len):
+        rows = pl.ds(q_at, TQ)
+        q = q_sc[rows, :]
+        g = gctx_ref[:, rows]
+        lse = lse_ref[0, :, rows]
+        delta = delta_sc[:, rows]
+        dq = jnp.zeros((HD, TQ), f32)
+        starts = [j * KC for j in range(PROMPT // KC)]
+        starts = starts + [own_at + j * KC for j in range(own_len // KC)]
+        for start in starts:
+            keys = pl.ds(start, KC)
+            s = mm(k_sc[keys, :], q, NT)
+            p = jnp.exp2(s * exp2_scale - lse)
+            dp = mm(v_sc[keys, :], g)
+            ds = (p * (dp - delta)).astype(bf16)
+            dv_sc[keys, :] += mm(p.astype(bf16), g, NT)
+            dk_sc[keys, :] += mm(ds, q)
+            dq = dq + mm(kt_sc[:, keys], ds)
+        dqt_sc[:, rows] = dq * score_scale
+
+    query_tiles(place_ref[1] == SHORT, tile)
     sums_ref[...] = jnp.zeros_like(sums_ref)
     gate_ref[...] = jnp.zeros_like(gate_ref)
 
     def place(i, carry):
         rows = pl.ds(pl.multiple_of(i * TQ, TQ), TQ)
-        for h in range(heads):
-            at = 3 * HD * h
-            dq = dqt_sc[h, :, rows].T.astype(bf16)
-            dk = (dk_sc[h, rows, :] * score_scale).astype(bf16)
-            dv = dv_sc[h, rows, :].astype(bf16).astype(f32)
-            gate_ref[0:1, HD * h : HD * (h + 1)] += jnp.sum(
-                dv * v_sc[h, rows, :].astype(f32), axis=0, keepdims=True
-            )
-            dv = (dv * scale_ref[:, at + 2 * HD : at + 3 * HD]).astype(bf16)
-            out_ref[rows, at : at + HD] = dq
-            out_ref[rows, at + HD : at + 2 * HD] = dk
-            out_ref[rows, at + 2 * HD : at + 3 * HD] = dv
-            sums_ref[0:1, at : at + HD] += jnp.sum(dq.astype(f32), axis=0, keepdims=True)
-            sums_ref[0:1, at + 2 * HD : at + 3 * HD] += jnp.sum(
-                dv.astype(f32), axis=0, keepdims=True
-            )
+        dq = dqt_sc[:, rows].T.astype(bf16)
+        dk = (dk_sc[rows, :] * score_scale).astype(bf16)
+        dv = dv_sc[rows, :].astype(bf16).astype(f32)
+        gate_ref[0:1, :] += jnp.sum(dv * v_sc[rows, :].astype(f32), axis=0, keepdims=True)
+        dv = (dv * scale_ref[0]).astype(bf16)
+        out_ref[rows, 0:HD] = dq
+        out_ref[rows, HD : 2 * HD] = dk
+        out_ref[rows, 2 * HD : 3 * HD] = dv
+        sums_ref[0:1, :] += jnp.sum(dq.astype(f32), axis=0, keepdims=True)
+        sums_ref[1:2, :] += jnp.sum(dv.astype(f32), axis=0, keepdims=True)
         return carry
 
     lax.fori_loop(0, GLEN // TQ, place, 0)
-
-
-def attend_back(lens, packed, ctx, gctx, lse, scale, heads):
-    width = 3 * HD * heads
-    whole = pl.BlockSpec(memory_space=pltpu.VMEM)
-    rows64 = pltpu.VMEM((heads, GLEN, HD), bf16)
-    rows64f = pltpu.VMEM((heads, GLEN, HD), f32)
+    s = place_ref[0]
+    count = own_ref.shape[0]
+    for k, ref in enumerate((own_ref, p1_ref, p2_ref, p3_ref)):
+        ref[...] = out_ref[pl.ds(pl.multiple_of(flip(s, k) * count, count), count), :]
+
+
+def attend_back(place, packed, ctx, gctx, lse, scale, h):
+    heads = packed.shape[0]
+    rows64 = pltpu.VMEM((GLEN, HD), bf16)
+    piece = (GLEN // 4, 3 * HD)
+
+    def spec(shape, at):
+        return pl.BlockSpec(shape, lambda i: at)
+
     return pl.pallas_call(
-        functools.partial(attend_back_kernel, heads),
-        out_shape=(
-            jax.ShapeDtypeStruct((GLEN, width), bf16),
-            jax.ShapeDtypeStruct((8, width), f32),
-            jax.ShapeDtypeStruct((8, HD * heads), f32),
-        ),
-        in_specs=[pl.BlockSpec(memory_space=pltpu.SMEM)] + [whole] * 5,
-        out_specs=(whole, whole, whole),
+        attend_back_kernel,
+        grid=(1,),
+        out_shape=(jax.ShapeDtypeStruct((GLEN, 3 * HD), bf16),)
+        + (jax.ShapeDtypeStruct(piece, bf16),) * 4
+        + (jax.ShapeDtypeStruct((8, HD), f32), jax.ShapeDtypeStruct((8, HD), f32)),
+        in_specs=[
+            pl.BlockSpec(memory_space=pltpu.SMEM),
+            spec((1, GLEN, 3 * HD), (h, 0, 0)),
+            spec((HD, GLEN), (h, 0)),
+            spec((HD, GLEN), (h, 0)),
+            spec((1, 1, GLEN), (h, 0, 0)),
+            spec((1, 1, HD), (h, 0, 0)),
+        ],
+        out_specs=(spec((GLEN, 3 * HD), (0, 0)),)
+        + (spec(piece, (0, 0)),) * 4
+        + (spec((8, HD), (0, 0)),) * 2,
         scratch_shapes=[
             rows64,
             rows64,
             rows64,
-            pltpu.VMEM((heads, HD, GLEN), bf16),
-            pltpu.VMEM((heads, HD, GLEN), bf16),
-            pltpu.VMEM((heads, 1, GLEN), f32),
-            pltpu.VMEM((heads, HD, GLEN), f32),
-            rows64f,
-            rows64f,
+            pltpu.VMEM((HD, GLEN), bf16),
+            pltpu.VMEM((1, GLEN), f32),
+            pltpu.VMEM((HD, GLEN), f32),
+            pltpu.VMEM((GLEN, HD), f32),
+            pltpu.VMEM((GLEN, HD), f32),
         ],
-        compiler_params=pltpu.CompilerParams(vmem_limit_bytes=56 * 2**20),
+        compiler_params=pltpu.CompilerParams(vmem_limit_bytes=48 * 2**20),
         cost_estimate=pl.CostEstimate(
-            flops=heads * 10 * 256 * 5767168,
-            bytes_accessed=2 * GLEN * (3 * width),
-            transcendentals=heads * 5767168,
+            flops=10 * 256 * 5767168, bytes_accessed=2 * GLEN * (9 * HD), transcendentals=5767168
         ),
         name="attend_back",
-    )(lens, packed, ctx, gctx, lse, scale)
+    )(place, packed, ctx, gctx, lse, scale)
+
+
+def projection_grad_kernel(steps, n, tok_ref, *refs):
+    g_refs, out_ref, acc = refs[:-2], refs[-2], refs[-1]
+    i = pl.program_id(0)
+
+    @pl.when(i == 0)
+    def _():
+        acc[...] = jnp.zeros_like(acc)
+
+    cols = 3 * HD
+    for h, g_ref in enumerate(g_refs):
+        acc[:, cols * h : cols * (h + 1)] += mm(tok_ref[...], g_ref[...], TN)
+
+    @pl.when(i == steps - 1)
+    def _():
+        own = out_ref.shape[1]
+        for k in range(n):
+            out_ref[k] = acc[k * own : (k + 1) * own, :].astype(bf16)
+
+
+def projection_grad(n, tokens_all, grads):
+    rows, d = tokens_all.shape
+    steps = 4
+    block = rows // steps
+    width = 3 * HD * len(grads)
+    return pl.pallas_call(
+        functools.partial(projection_grad_kernel, steps, n),
+        out_shape=jax.ShapeDtypeStruct((n, d // n, width), bf16),
+        grid=(steps,),
+        in_specs=[pl.BlockSpec((block, d), lambda i: (i, 0))]
+        + [pl.BlockSpec((block, 3 * HD), lambda i: (i, 0))] * len(grads),
+        out_specs=pl.BlockSpec((n, d // n, width), lambda i: (0, 0, 0)),
+        scratch_shapes=[pltpu.VMEM((d, width), f32)],
+        compiler_params=pltpu.CompilerParams(vmem_limit_bytes=48 * 2**20),
+        cost_estimate=pl.CostEstimate(
+            flops=2 * rows * d * width, bytes_accessed=2 * rows * (d + width), transcendentals=0
+        ),
+        name="projection_grad",
+    )(tokens_all, *grads)
 
 
 def send(src, dst, sems, k, peer):
@@ -393,9 +432,9 @@
 
 
 def reduce_kernel(
-    n, con_ref, exp_ref, out_ref, att_ref, vec_ref, con_o, exp_o, out_o, att_o, vec_o,
-    r_con, r_exp, r_out, h_att, m_att, r_att, r_vec, r_vec2, m_vec, m_ce, g_ce, m_row, g_att,
-    s_a, r_a, s_b, r_b, s_c, r_c, s_d, r_d, s_e, r_e, s_f, r_f, s_g, r_g, s_h, r_h, s_i, r_i,
+    n, con_ref, out_ref, att_ref, vec_ref, con_o, out_o, att_o, vec_o,
+    r_con, r_out, h_att, m_att, r_att, r_vec, r_vec2, m_vec, m_ce, g_ce, m_row, g_att,
+    s_a, r_a, s_b, r_b, s_c, r_c, s_e, r_e, s_f, r_f, s_g, r_g, s_h, r_h, s_i, r_i,
 ):
     s, w = lax.axis_index("seq"), lax.axis_index("wt")
     z, c = w // 2, lax.rem(w, 2)
@@ -404,11 +443,6 @@
     mate = (s, flip(w, 1))
     wt_peers = [(s, lax.rem(w + j, n)) for j in range(1, n)]
     meet(seq_peers + wt_peers)
-    wide = exp_ref.shape[1] // 4
-
-    def lanes(p):
-        return pl.ds(pl.multiple_of(p * wide, 128), wide)
-
     pair = [
         send(att_ref.at[2 * k + 1 - c], h_att.at[k], (s_a, r_a), k, mate) for k in range(n // 2)
     ]
@@ -419,13 +453,8 @@
     cons = [
         send(con_ref.at[p], r_con.at[s], (s_c, r_c), k, (p, w)) for k, p in enumerate(others)
     ]
-    exps = [
-        send(exp_ref.at[:, lanes(p)], r_exp.at[s], (s_d, r_d), k, (p, w))
-        for k, p in enumerate(others)
-    ]
     outs = [send(out_ref, r_out.at[s], (s_e, r_e), k, (p, w)) for k, p in enumerate(others)]
     r_con[s] = con_ref[s]
-    r_exp[s] = exp_ref[:, lanes(s)]
     r_out[s] = out_ref[...]
     r_vec[w] = vec_ref[w]
     for copy in pair:
@@ -452,10 +481,7 @@
 
     for copy in cons:
         copy.wait_recv()
-    m_ce[0] = add4(r_con).astype(bf16)
-    for copy in exps:
-        copy.wait_recv()
-    m_ce[1] = add4(r_exp).astype(bf16)
+    m_ce[...] = add4(r_con).astype(bf16)
     g_ce[s] = m_ce[...]
     ces = [send(m_ce, g_ce.at[s], (s_h, r_h), k, p) for k, p in enumerate(seq_peers)]
     for copy in atts:
@@ -475,35 +501,32 @@
     for copy in ces:
         copy.wait_recv()
     for k in range(4):
-        con_o[k] = g_ce[k, 0].astype(f32)
-        exp_o[:, k * wide : (k + 1) * wide] = g_ce[k, 1].astype(f32)
+        con_o[k] = g_ce[k].astype(f32)
     for copy in rows:
         copy.wait_recv()
     cols = g_att.shape[2]
     for k in range(4):
         att_o[:, k * cols : (k + 1) * cols] = g_att[k].astype(f32)
-    for copy in pair + vecs + cons + exps + outs + atts + vecs2 + ces + rows:
+    for copy in pair + vecs + cons + outs + atts + vecs2 + ces + rows:
         copy.wait_send()
 
 
-def reduce_out(n, con, expand, out, att, vec):
+def reduce_out(n, con, out, att, vec):
     r, d = out.shape
     cols = att.shape[2]
     vshape = vec.shape[1:]
-    counts = (n // 2, n - 1, 3, 3, 3, n // 2 - 1, 3, 3, 3)
+    counts = (n // 2, n - 1, 3, 3, n // 2 - 1, 3, 3, 3)
     return pl.pallas_call(
         functools.partial(reduce_kernel, n),
         out_shape=(
             jax.ShapeDtypeStruct(con.shape, f32),
-            jax.ShapeDtypeStruct(expand.shape, f32),
             jax.ShapeDtypeStruct(out.shape, f32),
             jax.ShapeDtypeStruct((r, 4 * cols), f32),
             jax.ShapeDtypeStruct(vshape, f32),
         ),
-        in_specs=[IN_VMEM] * 5,
-        out_specs=(IN_VMEM,) * 5,
+        in_specs=[IN_VMEM] * 4,
+        out_specs=(IN_VMEM,) * 4,
         scratch_shapes=[
-            pltpu.VMEM((4, r, d), bf16),
             pltpu.VMEM((4, r, d), bf16),
             pltpu.VMEM((4, r, d), bf16),
             pltpu.VMEM((n // 2, r, cols), bf16),
@@ -512,45 +535,55 @@
             pltpu.VMEM((n,) + vshape, f32),
             pltpu.VMEM((4,) + vshape, f32),
             pltpu.VMEM(vshape, f32),
-            pltpu.VMEM((2, r, d), bf16),
-            pltpu.VMEM((4, 2, r, d), bf16),
+            pltpu.VMEM((r, d), bf16),
+            pltpu.VMEM((4, r, d), bf16),
             pltpu.VMEM((r, cols), bf16),
             pltpu.VMEM((4, r, cols), bf16),
         ]
         + [sem for count in counts for sem in dma_sems(count)],
         compiler_params=remote_params(4),
         name="reduce_out",
-    )(con, expand, out, att, vec)
-
-
-def tokens_grad_kernel(base_ref, g_ref, w_ref, o_ref):
-    cols = g_ref.shape[2]
-    total = base_ref[...]
-    for k in range(4):
-        total = total + mm(g_ref[k], w_ref[:, k * cols : (k + 1) * cols], NT)
-    o_ref[...] = total
-
-
-def tokens_back(base, g, weight):
+    )(con, out, att, vec)
+
+
+def tokens_back_kernel(heads, place_ref, base_ref, w_ref, *refs):
+    o_ref, pieces = refs[-1], refs[:-1]
+    cols = 3 * HD
+    for s in range(4):
+
+        @pl.when(place_ref[0] == s)
+        def _(s=s):
+            total = base_ref[...]
+            for h in range(heads):
+                for k in range(4):
+                    at = (heads * (s ^ k) + h) * cols
+                    total = total + mm(pieces[4 * h + k][...], w_ref[:, at : at + cols], NT)
+            o_ref[...] = total
+
+
+def tokens_back(place, base, weight, pieces):
     rows, d = base.shape
-    cols = g.shape[2]
     block = rows // 3
+    cols = 3 * HD
     return pl.pallas_call(
-        tokens_grad_kernel,
+        functools.partial(tokens_back_kernel, len(pieces) // 4),
         out_shape=jax.ShapeDtypeStruct((rows, d), f32),
         grid=(3,),
         in_specs=[
+            pl.BlockSpec(memory_space=pltpu.SMEM),
             pl.BlockSpec((block, d), lambda i: (i, 0)),
-            pl.BlockSpec((4, block, cols), lambda i: (0, i, 0)),
             pl.BlockSpec(weight.shape, lambda i: (0, 0)),
-        ],
+        ]
+        + [pl.BlockSpec((block, cols), lambda i: (i, 0))] * len(pieces),
         out_specs=pl.BlockSpec((block, d), lambda i: (i, 0)),
         compiler_params=pltpu.CompilerParams(vmem_limit_bytes=48 * 2**20),
         cost_estimate=pl.CostEstimate(
-            flops=8 * rows * d * cols, bytes_accessed=8 * rows * d + 8 * d * cols, transcendentals=0
+            flops=2 * rows * d * cols * len(pieces),
+            bytes_accessed=8 * rows * d + 8 * d * cols * len(pieces),
+            transcendentals=0,
         ),
         name="tokens_back",
-    )(base, g, weight)
+    )(place, base, weight, *pieces)
 
 
 (OUT_BIAS, GAIN1, SHIFT1, HIDDEN_SCALE, CON_BIAS, GAIN2, SHIFT2) = range(7)
@@ -584,8 +617,8 @@
 
 def feed_forward_kernel(
     steps, chunk,
-    ctx_ref, tok_ref, cot_ref, wo_ref, we_ref, wc_ref, wide_ref, unit_ref,
-    lo_ref, dt1_ref, gctx_ref, sw_ref, su_ref, dwc_ref, dwe_ref, dwo_ref,
+    place_ref, ctx_ref, tok_ref, cot_ref, wo_ref, we_ref, wc_ref, wide_ref, unit_ref,
+    lo_ref, dt1_ref, gctx_ref, sw_ref, su_ref, dwc_ref, mine_ref, mate_ref, dwo_ref,
     act_sc, gh_sc, low_sc, gb_sc, ga_sc, ctx_sc, gelu_sc, slope_sc,
 ):
     i = pl.program_id(0)
@@ -662,22 +695,38 @@
         for j in range(units // chunk):
             cols = slice(j * chunk, (j + 1) * chunk)
             dwc_ref[cols, :] = mm(act_sc[:, cols], gb_sc[...], TN).astype(bf16)
-            dwe_ref[:, cols] = mm(low_sc[...], gh_sc[:, cols], TN).astype(bf16)
+            part = mm(low_sc[...], gh_sc[:, cols], TN).astype(bf16)
+            own, wide_cols = mine_ref.shape[2:]
+            for c in range(2):
+
+                @pl.when(place_ref[2] == c)
+                def _(part=part, j=j, c=c):
+                    for q in range(chunk // wide_cols):
+                        at = j * (chunk // wide_cols) + q
+                        inner = slice(q * wide_cols, (q + 1) * wide_cols)
+                        for z in range(mine_ref.shape[1]):
+                            mine = (2 * z + c) * own
+                            mate = (2 * z + 1 - c) * own
+                            mine_ref[at, z] = part[mine : mine + own, inner]
+                            mate_ref[at, z] = part[mate : mate + own, inner]
+
         dwo_ref[...] = mm(ctx_sc[...], ga_sc[...]).astype(bf16)
 
 
-def feed_forward(ctx_t, tokens, cotangent, wo, we, wc, wide, unit, steps=3, chunk=1024, keep=f32):
+def feed_forward(n, place, ctx_t, tokens, cotangent, wo, we, wc, wide, unit):
+    steps, chunk, keep = 3, 768, f32
     rows, d = tokens.shape
     units = we.shape[1]
     block = rows // steps
+    halves = (4, n // 2, d // n, units // 4)
     tile = pl.BlockSpec((block, d), lambda i: (i, 0))
     lanes = pl.BlockSpec((d, block), lambda i: (0, i))
 
     def once(shape):
         return pl.BlockSpec(shape, lambda i: (0, 0), pipeline_mode=pl.Buffered(1))
 
-    def const(shape):
-        return pl.BlockSpec(shape, lambda i: (0, 0))
+    def once4(shape):
+        return pl.BlockSpec(shape, lambda i: (0, 0, 0, 0), pipeline_mode=pl.Buffered(1))
 
     return pl.pallas_call(
         functools.partial(feed_forward_kernel, steps, chunk),
@@ -688,15 +737,18 @@
             jax.ShapeDtypeStruct((8, d), f32),
             jax.ShapeDtypeStruct((8, units), f32),
             jax.ShapeDtypeStruct((units, d), bf16),
-            jax.ShapeDtypeStruct((d, units), bf16),
+            jax.ShapeDtypeStruct(halves, bf16),
+            jax.ShapeDtypeStruct(halves, bf16),
             jax.ShapeDtypeStruct((d, d), bf16),
         ),
         grid=(steps,),
         in_specs=[
+            pl.BlockSpec(memory_space=pltpu.SMEM),
             lanes, tile, tile, once((d, d)), once((d, units)), once((units, d)), once((8, d)), once((8, units)),
         ],
         out_specs=(
-            tile, tile, lanes, once((8, d)), once((8, units)), once((units, d)), once((d, units)), once((d, d)),
+            tile, tile, lanes, once((8, d)), once((8, units)), once((units, d)),
+            once4(halves), once4(halves), once((d, d)),
         ),
         scratch_shapes=[
             pltpu.VMEM((rows, units), bf16),
@@ -715,7 +767,31 @@
             transcendentals=2 * rows * units,
         ),
         name="feed_forward",
-    )(ctx_t, tokens, cotangent, wo, we, wc, wide, unit)
+    )(place, ctx_t, tokens, cotangent, wo, we, wc, wide, unit)
+
+
+def expand_reduce(mine, got, s, w, n):
+    z = w // 2
+
+    def at(q):
+        return lax.dynamic_index_in_dim(mine, q, 0, False).astype(f32) + lax.dynamic_index_in_dim(
+            got, q, 0, False
+        ).astype(f32)
+
+    own = at(s)
+    for k in (1, 2, 3):
+        piece = at(s ^ k).astype(bf16)
+        own = own + lax.ppermute(piece, "seq", [(j, j ^ k) for j in range(4)]).astype(f32)
+    total = lax.dynamic_index_in_dim(own, z, 0, False)
+    for j in range(1, n // 2):
+        piece = lax.dynamic_index_in_dim(own, lax.rem(z + j, n // 2), 0, False).astype(bf16)
+        total = total + lax.ppermute(piece, "wt", [(k, (k + 2 * j) % n) for k in range(n)]).astype(f32)
+    total = total.astype(bf16)
+    parts = [total] + [lax.ppermute(total, "seq", [(j, j ^ k) for j in range(4)]) for k in (1, 2, 3)]
+    parts = jnp.stack(parts)
+    return jnp.concatenate(
+        [lax.dynamic_index_in_dim(parts, s ^ q, 0, False) for q in range(4)], axis=1
+    ).astype(f32)
 
 
 def local(
@@ -803,6 +879,7 @@
     factor = jnp.stack([constant, constant, constant * own_scale[:, None]], axis=1)
     vec = jnp.stack([own_bias.reshape(local_width), factor.reshape(local_width)], axis=0)
     lens = lax.dynamic_slice_in_dim(continuation_lengths, first_group, GRP_WT, 0)[0]
+    place = jnp.stack([seq_index, lens[0], lax.rem(wt_index, 2)])
     packed, mixed_heads, log_sums = attend(lens, tokens_all, own_weight, vec, local_heads)
     local_ctx = local_heads * head_size
     context_t = exchange(
@@ -821,13 +898,14 @@
         wide_sums,
         unit_sums,
         contract_weight_grad,
-        expand_weight_grad,
+        exp_mine,
+        exp_mate,
         output_weight_grad,
     ) = feed_forward(
-        context_t, tokens, output_cotangent, full_output, full_expand, full_contract, wide_table, unit_table
+        wt_count, place, context_t, tokens, output_cotangent, full_output, full_expand, full_contract, wide_table, unit_table
     )
     con_piece = lax.psum_scatter(contract_weight_grad, "wt", scatter_dimension=0, tiled=True)
-    exp_piece = lax.psum_scatter(expand_weight_grad, "wt", scatter_dimension=0, tiled=True)
+    output_weight_grad, con_piece = lax.optimization_barrier((output_weight_grad, con_piece))
     out_piece = lax.psum_scatter(output_weight_grad, "wt", scatter_dimension=0, tiled=True)
     arriving = exchange(
         grad_context_t,
@@ -838,38 +916,29 @@
         2,
         "context_grad_in",
     )
-    grad_packed, sums, gate_sums = attend_back(
-        lens,
-        packed,
-        mixed_heads,
-        arriving,
-        log_sums,
-        vec[1:2],
-        local_heads,
-    )
+    exp_got = lax.ppermute(exp_mate, "wt", [(k, k ^ 1) for k in range(wt_count)])
+    value_scale = factor[:, 2:3, :]
+    backs, pieces, exp_own = [], [], None
+    for h in range(local_heads):
+        back = attend_back(place, packed, mixed_heads, arriving, log_sums, value_scale, h)
+        backs.append(back)
+        pieces.append(back[1])
+        for k in (1, 2, 3):
+            pieces.append(lax.ppermute(back[1 + k], "seq", [(j, j ^ k) for j in range(4)]))
+    exp_sum = expand_reduce(exp_mine, exp_got, seq_index, wt_index, wt_count)
+    sums = jnp.stack([back[5] for back in backs])
+    gate_sums = jnp.stack([back[6] for back in backs])
     head_own = own_mask.astype(jnp.float32) * own_attention[0] / own_gate
-    head_own = head_own * jnp.sum(gate_sums[0].reshape(local_heads, head_size), axis=1)
+    head_own = head_own * jnp.sum(gate_sums[:, 0], axis=1)
     head_partial = lax.dynamic_update_slice_in_dim(
         jnp.zeros((head_count,), jnp.float32), head_own, seq_index * local_heads, 0
     )
-    sums = sums[0].reshape(local_heads, 3, head_size)
     zeros_wide = jnp.zeros((model_width,), jnp.float32)
     at_own = seq_index * local_heads * head_size
     query_bias_grad = lax.dynamic_update_slice_in_dim(zeros_wide, sums[:, 0].reshape(-1), at_own, 0)
-    value_bias_grad = lax.dynamic_update_slice_in_dim(zeros_wide, sums[:, 2].reshape(-1), at_own, 0)
-    grad_pieces = exchange(
-        grad_packed.reshape(seq_count, row_count, local_width),
-        (seq_count, row_count, local_width),
-        (row_count, local_width),
-        lambda ref, p: ref.at[p],
-        lambda ref, p: ref.at[p],
-        3,
-        "packed_grad_out",
-    )
-    attention_weight_grad = jnp.einsum(
-        "td,tc->dc", tokens_all, grad_packed, preferred_element_type=jnp.float32
-    )
-    tokens_grad = tokens_back(grad_total_one, grad_pieces, full_attention)
+    value_bias_grad = lax.dynamic_update_slice_in_dim(zeros_wide, sums[:, 1].reshape(-1), at_own, 0)
+    attention_weight_grad = projection_grad(wt_count, tokens_all, [back[0] for back in backs])
+    tokens_grad = tokens_back(place, grad_total_one, full_attention, pieces)
     width_rows = jnp.stack(
         [
             query_bias_grad,
@@ -898,12 +967,11 @@
     )
     used = by_shard.shape[1]
     by_shard = jnp.pad(by_shard, ((0, 0), (0, -used % 1024))).reshape(wt_count, -1, 128)
-    con_sum, exp_sum, out_sum, att_sum, vec_sum = reduce_out(
+    con_sum, out_sum, att_sum, vec_sum = reduce_out(
         wt_count,
         con_piece.reshape(seq_count, own_wide, model_width),
-        exp_piece,
         out_piece,
-        attention_weight_grad.astype(bf16).reshape(wt_count, own_wide, local_width),
+        attention_weight_grad,
         by_shard,
     )
     vec_sum = vec_sum.reshape(-1)

time: 405 us -> 436 us (1.077); the launches traced: 405 us -> 429 us
  Pallas kernels: 334 us -> 275 us
  waiting for transfers between devices: 19.8 us -> 53.1 us
  starting transfers between devices: 0.23 us -> 24 us
  local copies, waits for them, and re-layouts: 25.4 us -> 44.4 us
  other arithmetic: 2.06 us -> 16.5 us
  matrix products: 6.6 us -> 0 us
    pallas_call x3 -> x2, Pallas kernels: 78.2 us -> 32.5 us  [exchange(): pl.pallas_call(functools.partial(exchange_kernel, src_of, dst_of), out_sh...]
    ppermute x0 -> x19, waiting for transfers between devices: none -> 37.1 us  [the longest x9 37 us: local(): lax.ppermute(back[1 + k], 'seq', [(j, j ^ k) for j in range(4)])]
    ppermute x0 -> x19, starting transfers between devices: none -> 23.8 us  [the longest x9 11 us: local(): lax.ppermute(back[1 + k], 'seq', [(j, j ^ k) for j in range(4)])]
    pallas_call x1, Pallas kernels: 46.2 us -> 32.3 us  [reduce_out(): pl.pallas_call(functools.partial(reduce_kernel, n), out_shape=(jax.ShapeD...]
    pallas_call x2 -> x5, Pallas kernels: 66.4 us -> 75.9 us  [the longest x3 61.4 us: attend_back(): pl.pallas_call(attend_back_kernel, grid=(1,), out_shape=(jax.ShapeDtypeSt...]
    pallas_call x1, Pallas kernels: 56.9 us -> 48.1 us  [feed_forward(): pl.pallas_call(functools.partial(feed_forward_kernel, steps, chunk), out_...]
    another operation x7, local copies, waits for them, and re-layouts: 0.49 us -> 8.21 us  [local(): jnp.stack([query_bias_grad, value_bias_grad, wide_sums[S_OUT_BIAS], wide_...]
    unnamed x50 -> x109, local copies, waits for them, and re-layouts: 8.72 us -> 15.7 us
  transfers between devices with their start and end apart: 6 -> 24, of which waited for: 1 -> 6; matrix products, arithmetic and copies ran while one was open for 5% -> 10% of each run, Pallas kernels for 71% -> 45%
where the time goes in v4:
time: 436 us; the launch traced here: 429 us
  Pallas kernels  275 us (63%)
  waiting for transfers between devices  53.1 us (12%)
  local copies, waits for them, and re-layouts  44.4 us (10%)
  starting transfers between devices  24 us (6%)
  other arithmetic  16.5 us (4%)
  between operations  16.1 us (4%)
    pallas_call x3, Pallas kernels, attend_back(): pl.pallas_call(attend_back_kernel, grid=(1,), out_shape=(jax.ShapeDtypeSt...  61.4 us
    pallas_call x1, Pallas kernels, feed_forward(): pl.pallas_call(functools.partial(feed_forward_kernel, steps, chunk), out_...  48.1 us
    pallas_call x1, Pallas kernels, gather_in(): pl.pallas_call(functools.partial(gather_kernel, n), out_shape=(jax.ShapeD...  45.7 us
    pallas_call x1, Pallas kernels, attend(): pl.pallas_call(functools.partial(attend_kernel, heads), out_shape=(jax.Sh...  41 us
    ppermute x9, waiting for transfers between devices, local(): lax.ppermute(back[1 + k], 'seq', [(j, j ^ k) for j in range(4)])  37 us
    pallas_call x2, Pallas kernels, exchange(): pl.pallas_call(functools.partial(exchange_kernel, src_of, dst_of), out_sh...  32.5 us
    pallas_call x1, Pallas kernels, reduce_out(): pl.pallas_call(functools.partial(reduce_kernel, n), out_shape=(jax.ShapeD...  32.3 us
    unnamed x109, local copies, waits for them, and re-layouts  15.7 us
  transfers between devices with their start and end apart: 24, of which 6 were waited for; matrix products, arithmetic and copies ran while one was open for 10% of the time, Pallas kernels for 45%

profile of v4, /device:TPU:0, one launch (start us, length us, event | category | flops | bytes accessed | tf_op | source)
XLA Modules:
  0.0 429.4 jit_solution(10310630403600187254)
XLA Ops:
  10.7 1.7 constant_dynamic-slice_fusion.cols_ref
  12.4 45.7 %gather_in.1 = (bf16[3072,768]{1,0:T(8,128)(2,1)}, bf16[8,96,576]{2,1,0:T(8,128)(2,1)}, bf16[8,96,768]{2,1,0:T(8,128)(2,1)}) custom-call(bf16[768,768]{1,0:T(8,128)(2,1)} %tok_ref.3, bf16[96,576]{1,0:T(8,128)(2,1)} %constant_dynamic-slice_fusion.cols_ref, bf16[96,768]{1,0:T(8,128)(2,1)} %out_ref.1), custom_call_target="tpu_custom_call" | custom-call | tf_op jit(solution)/shard_map/gather_in/pallas_call | solution.py:381
  59.4 41.0 %attend.1 = (bf16[3,3072,192]{2,1,0:T(8,128)(2,1)}, bf16[192,3072]{1,0:T(8,128)(2,1)}, f32[3,1,3072]{2,1,0:T(1,128)}) custom-call(s32[2]{0:T(128)} %get-tuple-element.104.lens_ref, bf16[3072,768]{1,0:T(8,128)(2,1)} %get-tuple-element.60.tok_ref, bf16[768,576]{1,0:T(8,128)(2,1)} %bitcast.95, f32[2,576]{1,0:T(2,128)} %pad_maximum_fusion.2.vec_ref), custom_call_target="tpu_custom_call" | custom-call | flops 20434649088 | bytes 8257536 | tf_op jit(solution)/shard_map/attend/pallas_call | solution.py:101
  100.6 15.7 %context_out.1.ctx_ref = bf16[768,768]{1,0:T(8,128)(2,1)} custom-call(bf16[192,3072]{1,0:T(8,128)(2,1)} %get-tuple-element.62.x_ref.ctx_ref), custom_call_target="tpu_custom_call" | custom-call | tf_op jit(solution)/shard_map/context_out/pallas_call | solution.py:423
  120.9 14.0 %all-gather.6.cloned.1.call-done.wc_ref = bf16[3072,768]{1,0:T(8,128)(2,1)} async-done(((bf16[384,768]{1,0:T(8,128)(2,1)}), bf16[3072,768]{1,0:T(8,128)(2,1)}) %all-gather.6.cloned.1.call-update) | async-done | bytes 4718608 | tf_op jit(solution)/shard_map/all_gather | solution.py:838
  134.9 48.1 %feed_forward.1 = (bf16[768,768]{1,0:T(8,128)(2,1)}, f32[768,768]{1,0:T(8,128)}, bf16[768,768]{1,0:T(8,128)(2,1)}, f32[8,768]{1,0:T(8,128)}, f32[8,3072]{1,0:T(8...) custom-call(s32[3]{0:T(128)} %pad_add_fusion.place_ref, ...), custom_call_target="tpu_custom_call" | custom-call | flops 24461180928 | bytes 49545216 | tf_op jit(solution)/shard_map/feed_forward/pallas_call | solution.py:731
  184.0 16.8 %context_grad_in.1.gctx_ref = bf16[192,3072]{1,0:T(8,128)(2,1)} custom-call(bf16[768,768]{1,0:T(8,128)(2,1)} %get-tuple-element.67.x_ref), custom_call_target="tpu_custom_call" | custom-call | tf_op jit(solution)/shard_map/context_grad_in/pallas_call | solution.py:423
  200.8 1.6 slice_reduce_fusion
  203.0 1.3 copy-done.5
  205.1 20.1 %attend_back.5 = (bf16[3072,192]{1,0:T(8,128)(2,1)S(1)}, bf16[768,192]{1,0:T(8,128)(2,1)S(1)}, bf16[768,192]{1,0:T(8,128)(2,1)S(1)}, bf16[768,192]{1,0:T(8,128)(...) custom-call(s32[3]{0:T(128)S(1)} %copy-done.14, ...), custom_call_target="tpu_custom_call" | custom-call | flops 14763950080 | bytes 3538944 | tf_op jit(solution)/shard_map/attend_back/pallas_call | solution.py:199
  227.5 20.2 %attend_back.4 = (bf16[3072,192]{1,0:T(8,128)(2,1)S(1)}, bf16[768,192]{1,0:T(8,128)(2,1)S(1)}, bf16[768,192]{1,0:T(8,128)(2,1)S(1)}, bf16[768,192]{1,0:T(8,128)(...) custom-call(s32[3]{0:T(128)S(1)} %copy-done.14, ...), custom_call_target="tpu_custom_call" | custom-call | flops 14763950080 | bytes 3538944 | tf_op jit(solution)/shard_map/attend_back/pallas_call | solution.py:199
  249.9 21.1 %attend_back.3 = (bf16[3072,192]{1,0:T(8,128)(2,1)S(1)}, bf16[768,192]{1,0:T(8,128)(2,1)S(1)}, bf16[768,192]{1,0:T(8,128)(2,1)S(1)}, bf16[768,192]{1,0:T(8,128)(...) custom-call(s32[3]{0:T(128)S(1)} %copy-done.15, ...), custom_call_target="tpu_custom_call" | custom-call | flops 14763950080 | bytes 3538944 | tf_op jit(solution)/shard_map/attend_back/pallas_call | solution.py:199
  272.5 2.9 fusion.2
  275.4 1.6 collective-permute-start.10
  277.0 1.5 collective-permute-start.11
  279.6 1.3 stack.185
  283.7 1.3 stack.180
  285.6 1.3 dynamic_update_slice.14
  287.0 1.3 reduce.5
  288.2 1.4 stack.181
  289.6 1.4 stack.182
  291.0 1.3 copy.43
  292.4 1.3 stack.183
  293.7 1.4 maximum_bitcast_fusion
  295.1 1.5 reshape.104
  296.7 1.7 collective-permute-start.6
  298.4 1.4 collective-permute-start.7
  299.8 1.3 pad_maximum_fusion.1
  302.2 1.5 concatenate.8
  304.2 1.6 collective-permute-start.3
  305.8 2.3 fusion.1
  308.3 4.8 %collective-permute-done.6.refs_9_ = bf16[768,192]{1,0:T(8,128)(2,1)} collective-permute-done((bf16[768,192]{1,0:T(8,128)(2,1)}, bf16[768,192]{1,0:T(8,128)(2,1)}, u32[]{:S(2)}, u32[]{:S(2)}) %collective-permute-start.6) | collective-permute-done | bytes 294944 | tf_op jit(solution)/shard_map/ppermute | solution.py:927
  313.2 1.3 collective-permute-start.14
  314.5 5.3 %collective-permute-done.7.refs_10_ = bf16[768,192]{1,0:T(8,128)(2,1)} collective-permute-done((bf16[768,192]{1,0:T(8,128)(2,1)}, bf16[768,192]{1,0:T(8,128)(2,1)}, u32[]{:S(2)}, u32[]{:S(2)}) %collective-permute-start.7) | collective-permute-done | bytes 294944 | tf_op jit(solution)/shard_map/ppermute | solution.py:927
  321.0 6.6 %projection_grad.1.att_ref = bf16[8,96,576]{2,1,0:T(8,128)(2,1)S(1)} custom-call(bf16[3072,768]{1,0:T(8,128)(2,1)} %get-tuple-element.60.tok_ref, bf16[3072,192]{1,0:T(8,128)(2,1)S(1)} %copy-done.2, bf16[3072,192]{1,0:T(8,128)(2,1)S(1)} %get-tuple-element.86.refs_1_, bf16[3072,192]{1,0:T(8,128)(2,1)S(1)} %get-tuple-element.87.refs_2_), custom_call_target="tpu_custom_call" | custom-call | flops 2717908992 | bytes 8257536 | tf_op jit(solution)/shard_map/projection_grad/pallas_call | solution.py:258
  329.3 2.4 collective-permute-start.4
  332.4 1.5 collective-permute-start
  333.9 2.0 collective-permute-start.1
  336.7 16.7 %collective-permute-done.4.refs_6_ = bf16[768,192]{1,0:T(8,128)(2,1)S(1)} collective-permute-done((bf16[768,192]{1,0:T(8,128)(2,1)S(1)}, bf16[768,192]{1,0:T(8,128)(2,1)S(1)}, u32[]{:S(2)}, u32[]{:S(2)}) %collective-permute-start.4) | collective-permute-done | bytes 294944 | tf_op jit(solution)/shard_map/ppermute | solution.py:927
  353.5 4.8 %collective-permute-start.17 = (bf16[96,768]{1,0:T(8,128)(2,1)S(1)}, bf16[96,768]{1,0:T(8,128)(2,1)}, u32[]{:S(2)}, u32[]{:S(2)}) collective-permute-start(bf16[96,768]{1,0:T(8,128)(2,1)S(1)} %fusion.7), channel_id=1, source_target_pairs={{0,16},{8,24},{16,0},{24,8},{1,17},{9,25},{17,1},{25,9},{2,18},{10... | collective-permute-start | bytes 442376 | tf_op jit(solution)/shard_map/ppermute | solution.py:790
  358.3 1.5 collective-permute-start.18
  359.8 10.1 %collective-permute-done.1.refs_2_ = bf16[768,192]{1,0:T(8,128)(2,1)S(1)} collective-permute-done((bf16[768,192]{1,0:T(8,128)(2,1)}, bf16[768,192]{1,0:T(8,128)(2,1)S(1)}, u32[]{:S(2)}, u32[]{:S(2)}) %collective-permute-start.1) | collective-permute-done | bytes 294944 | tf_op jit(solution)/shard_map/ppermute | solution.py:927
  371.9 7.9 %tokens_back.1 = f32[768,768]{1,0:T(8,128)} custom-call(s32[3]{0:T(128)S(1)} %copy-done.16, f32[768,768]{1,0:T(8,128)} %get-tuple-element.65.base_ref, bf16[768,2304]{1,0:T(8,128)(2,1)} %all-gather.8.cloned.1.call-done.w_ref, bf16[768,192]{1,0:T(8,128)(2,1)S(1)} %copy-done.9, bf16[768,192]{1,0:T(8,128)(2,1)S(1)} %collective-permute-done.refs_1_, ...), custom_call_target="tpu_custom_call" | custom-call | flops 2717908992 | bytes 18874368 | tf_op jit(solution)/shard_map/tokens_back/pallas_call | solution.py:568
  382.1 32.3 %reduce_out.1 = (f32[4,96,768]{2,1,0:T(8,128)}, f32[96,768]{1,0:T(8,128)}, f32[96,2304]{1,0:T(8,128)}, f32[16,128]{1,0:T(8,128)}) custom-call(bf16[4,96,768]{2,1,0:T(8,128)(2,1)} %bitcast.83, bf16[96,768]{1,0:T(8,128)(2,1)} %reduce-scatter.5.cloned.1.call-done.out_ref, bf16[8,96,576]{2,1,0:T(8,128)(2,1)} %copy-done, f32[8,16,128]{2,1,0:T(8,128)} %bitcast.85), custom_call_target="tpu_custom_call" | custom-call | tf_op jit(solution)/shard_map/reduce_out/pallas_call | solution.py:519
  414.4 1.6 fusion.17
  416.0 1.4 fusion.16
  417.4 1.3 slice.99
  418.7 2.2 copy.54
  (192 shorter events, 33.0 us)
Async XLA Ops:
  7.2 113.6 %all-gather.4.cloned.1.call-start = ((), (), s32[]{:S(2)}) async-start(), calls=%async_computation.2 | async-start | bytes 5308416 | tf_op jit(solution)/shard_map/all_gather | solution.py:837
  8.0 50.1 %copy-start.47 = (s32[8,2]{0,1:T(2,128)S(1)}, s32[8,2]{0,1:T(2,128)}, u32[]{:S(2)}) copy-start(s32[8,2]{0,1:T(2,128)} %param.47) | copy-start | bytes 196
  8.0 126.9 %all-gather.6.cloned.1.call-start = ((), (), s32[]{:S(2)}) async-start(), calls=%async_computation.3 | async-start | bytes 5308416 | tf_op jit(solution)/shard_map/all_gather | solution.py:838
  8.7 270.8 %reduce-scatter.3.cloned.1.call-start = ((), (), s32[]{:S(2)}) async-start(), calls=%async_computation.5 | async-start | bytes 5308416 | tf_op jit(solution)/shard_map/reduce_scatter | solution.py:907
  100.4 16.3 %copy-start.51 = (s32[8]{0:T(128)S(1)}, s32[8]{0:T(128)}, u32[]{:S(2)}) copy-start(s32[8]{0:T(128)} %param.46) | copy-start | bytes 100
  100.4 17.5 %copy-start.37 = (bf16[3072]{0:T(1024)(128)(2,1)S(1)}, bf16[3072]{0:T(1024)(128)(2,1)}, u32[]{:S(2)}) copy-start(bf16[3072]{0:T(1024)(128)(2,1)} %param.34) | copy-start | bytes 18436
  100.4 17.6 %copy-start.34 = (s32[768]{0:T(1024)S(1)}, s32[768]{0:T(1024)}, u32[]{:S(2)}) copy-start(s32[768]{0:T(1024)} %param.43) | copy-start | bytes 9220
  100.4 17.6 %copy-start.38 = (f32[768]{0:T(1024)S(1)}, f32[768]{0:T(1024)}, u32[]{:S(2)}) copy-start(f32[768]{0:T(1024)} %param.40) | copy-start | bytes 9220
  100.5 17.6 %copy-start.39 = (bf16[768]{0:T(1024)(128)(2,1)S(1)}, bf16[768]{0:T(1024)(128)(2,1)}, u32[]{:S(2)}) copy-start(bf16[768]{0:T(1024)(128)(2,1)} %param.30) | copy-start | bytes 4612
  100.5 17.6 %copy-start.40 = (bf16[768]{0:T(1024)(128)(2,1)S(1)}, bf16[768]{0:T(1024)(128)(2,1)}, u32[]{:S(2)}) copy-start(bf16[768]{0:T(1024)(128)(2,1)} %param.31) | copy-start | bytes 4612
  100.5 17.6 %copy-start.41 = (bf16[768]{0:T(1024)(128)(2,1)S(1)}, bf16[768]{0:T(1024)(128)(2,1)}, u32[]{:S(2)}) copy-start(bf16[768]{0:T(1024)(128)(2,1)} %param.32) | copy-start | bytes 4612
  100.5 17.6 %copy-start.42 = (bf16[768]{0:T(1024)(128)(2,1)S(1)}, bf16[768]{0:T(1024)(128)(2,1)}, u32[]{:S(2)}) copy-start(bf16[768]{0:T(1024)(128)(2,1)} %param.36) | copy-start | bytes 4612
  100.5 17.6 %copy-start.43 = (bf16[768]{0:T(1024)(128)(2,1)S(1)}, bf16[768]{0:T(1024)(128)(2,1)}, u32[]{:S(2)}) copy-start(bf16[768]{0:T(1024)(128)(2,1)} %param.37) | copy-start | bytes 4612
  100.5 17.6 %copy-start.44 = (bf16[768]{0:T(1024)(128)(2,1)S(1)}, bf16[768]{0:T(1024)(128)(2,1)}, u32[]{:S(2)}) copy-start(bf16[768]{0:T(1024)(128)(2,1)} %param.38) | copy-start | bytes 4612
  100.5 17.7 %copy-start.33 = (s32[3072]{0:T(1024)S(1)}, s32[3072]{0:T(1024)}, u32[]{:S(2)}) copy-start(s32[3072]{0:T(1024)} %param.44) | copy-start | bytes 36868
  100.5 17.7 %copy-start.36 = (f32[3072]{0:T(1024)S(1)}, f32[3072]{0:T(1024)}, u32[]{:S(2)}) copy-start(f32[3072]{0:T(1024)} %param.41) | copy-start | bytes 36868
  183.0 176.8 %all-gather.8.cloned.1.call-start = ((), (), s32[]{:S(2)}) async-start(), calls=%async_computation.4 | async-start | bytes 3981312 | tf_op jit(solution)/shard_map/all_gather | solution.py:839
  183.6 198.5 %reduce-scatter.5.cloned.1.call-start = ((), (), s32[]{:S(2)}) async-start(), calls=%async_computation.6 | async-start | bytes 1327104 | tf_op jit(solution)/shard_map/reduce_scatter | solution.py:909
  183.7 88.8 %collective-permute-start.9 = (bf16[4,4,96,768]{3,2,1,0:T(8,128)(2,1)}, bf16[4,4,96,768]{3,2,1,0:T(8,128)(2,1)}, u32[]{:S(2)}, u32[]{:S(2)}) collective-permute-start(bf16[4,4,96,768]{3,2,1,0:T(8,128)(2,1)} %get-tuple-element.100), channel_id=1, source_target_pairs={{0,1},{1,0},{2,3},{3,2},{4,5},{5,4},{6,7},{7,6},{8,9},{9,8},{10,11... | collective-permute-start | bytes 7077896 | tf_op jit(solution)/shard_map/ppermute | solution.py:919
  184.0 19.0 %copy-start.3 = (bf16[192,3072]{1,0:T(8,128)(2,1)S(1)}, bf16[192,3072]{1,0:T(8,128)(2,1)}, u32[]{:S(2)}) copy-start(bf16[192,3072]{1,0:T(8,128)(2,1)} %get-tuple-element.62.x_ref.ctx_ref) | copy-start | bytes 3538948
  184.0 19.0 %copy-start.14 = (s32[3]{0:T(128)S(1)}, s32[3]{0:T(128)}, u32[]{:S(2)}) copy-start(s32[3]{0:T(128)} %pad_add_fusion.place_ref) | copy-start | bytes 40
  205.1 22.4 %copy-start.4 = (bf16[192,3072]{1,0:T(8,128)(2,1)S(1)}, bf16[192,3072]{1,0:T(8,128)(2,1)}, u32[]{:S(2)}) copy-start(bf16[192,3072]{1,0:T(8,128)(2,1)} %get-tuple-element.62.x_ref.ctx_ref) | copy-start | bytes 3538948
  205.1 22.4 %copy-start.28 = (f32[3,1,3072]{2,1,0:T(1,128)S(1)}, f32[3,1,3072]{2,1,0:T(1,128)}, u32[]{:S(2)}) copy-start(f32[3,1,3072]{2,1,0:T(1,128)} %get-tuple-element.68.lse_ref) | copy-start | bytes 110596
  227.5 22.4 %copy-start.15 = (s32[3]{0:T(128)S(1)}, s32[3]{0:T(128)}, u32[]{:S(2)}) copy-start(s32[3]{0:T(128)} %pad_add_fusion.place_ref) | copy-start | bytes 40
  249.9 21.1 %copy-start.6 = (bf16[768,192]{1,0:T(8,128)(2,1)}, bf16[768,192]{1,0:T(8,128)(2,1)S(1)}, u32[]{:S(2)}) copy-start(bf16[768,192]{1,0:T(8,128)(2,1)S(1)} %get-tuple-element.73.refs_4_) | copy-start | bytes 884740
  249.9 22.6 %copy-start.29 = (bf16[4,4,96,768]{3,2,1,0:T(8,128)(2,1)S(1)}, bf16[4,4,96,768]{3,2,1,0:T(8,128)(2,1)}, u32[]{:S(2)}) copy-start(bf16[4,4,96,768]{3,2,1,0:T(8,128)(2,1)} %get-tuple-element.99) | copy-start | bytes 7077892
  275.4 28.2 %collective-permute-start.10 = (bf16[4,96,768]{2,1,0:T(8,128)(2,1)}, bf16[4,96,768]{2,1,0:T(8,128)(2,1)}, u32[]{:S(2)}, u32[]{:S(2)}) collective-permute-start(bf16[4,96,768]{2,1,0:T(8,128)(2,1)} %get-tuple-element.106), channel_id=1, source_target_pairs={{0,8},{8,0},{16,24},{24,16},{1,9},{9,1},{17,25},{25,17},{2,10},{10... | collective-permute-start | bytes 1769480 | tf_op jit(solution)/shard_map/ppermute | solution.py:784
  277.0 27.2 %collective-permute-start.11 = (bf16[4,96,768]{2,1,0:T(8,128)(2,1)}, bf16[4,96,768]{2,1,0:T(8,128)(2,1)}, u32[]{:S(2)}, u32[]{:S(2)}) collective-permute-start(bf16[4,96,768]{2,1,0:T(8,128)(2,1)} %get-tuple-element.108), channel_id=1, source_target_pairs={{0,16},{8,24},{16,0},{24,8},{1,17},{9,25},{17,1},{25,9},{2,18},{10... | collective-permute-start | bytes 1769480 | tf_op jit(solution)/shard_map/ppermute | solution.py:784
  278.4 27.4 %collective-permute-start.12 = (bf16[4,96,768]{2,1,0:T(8,128)(2,1)}, bf16[4,96,768]{2,1,0:T(8,128)(2,1)}, u32[]{:S(2)}, u32[]{:S(2)}) collective-permute-start(bf16[4,96,768]{2,1,0:T(8,128)(2,1)} %get-tuple-element.107), channel_id=1, source_target_pairs={{0,24},{8,16},{16,8},{24,0},{1,25},{9,17},{17,9},{25,1},{2,26},{10... | collective-permute-start | bytes 1769480 | tf_op jit(solution)/shard_map/ppermute | solution.py:784
  296.7 16.5 %collective-permute-start.6 = (bf16[768,192]{1,0:T(8,128)(2,1)}, bf16[768,192]{1,0:T(8,128)(2,1)}, u32[]{:S(2)}, u32[]{:S(2)}) collective-permute-start(bf16[768,192]{1,0:T(8,128)(2,1)} %copy-done.26), channel_id=1, source_target_pairs={{0,8},{8,0},{16,24},{24,16},{1,9},{9,1},{17,25},{25,17},{2,10},{10... | collective-permute-start | bytes 884744 | tf_op jit(solution)/shard_map/ppermute | solution.py:927
  298.4 21.4 %collective-permute-start.7 = (bf16[768,192]{1,0:T(8,128)(2,1)}, bf16[768,192]{1,0:T(8,128)(2,1)}, u32[]{:S(2)}, u32[]{:S(2)}) collective-permute-start(bf16[768,192]{1,0:T(8,128)(2,1)} %copy-done.25), channel_id=1, source_target_pairs={{0,16},{8,24},{16,0},{24,8},{1,17},{9,25},{17,1},{25,9},{2,18},{10... | collective-permute-start | bytes 884744 | tf_op jit(solution)/shard_map/ppermute | solution.py:927
  303.7 24.9 %collective-permute-start.8 = (bf16[768,192]{1,0:T(8,128)(2,1)}, bf16[768,192]{1,0:T(8,128)(2,1)S(1)}, u32[]{:S(2)}, u32[]{:S(2)}) collective-permute-start(bf16[768,192]{1,0:T(8,128)(2,1)} %copy-done.24), channel_id=1, source_target_pairs={{0,24},{8,16},{16,8},{24,0},{1,25},{9,17},{17,9},{25,1},{2,26},{10... | collective-permute-start | bytes 884744 | tf_op jit(solution)/shard_map/ppermute | solution.py:927
  304.2 27.4 %collective-permute-start.3 = (bf16[768,192]{1,0:T(8,128)(2,1)}, bf16[768,192]{1,0:T(8,128)(2,1)S(1)}, u32[]{:S(2)}, u32[]{:S(2)}) collective-permute-start(bf16[768,192]{1,0:T(8,128)(2,1)} %copy-done.23), channel_id=1, source_target_pairs={{0,8},{8,0},{16,24},{24,16},{1,9},{9,1},{17,25},{25,17},{2,10},{10... | collective-permute-start | bytes 884744 | tf_op jit(solution)/shard_map/ppermute | solution.py:927
  305.8 15.1 %copy-start.2 = (bf16[3072,192]{1,0:T(8,128)(2,1)S(1)}, bf16[3072,192]{1,0:T(8,128)(2,1)}, u32[]{:S(2)}) copy-start(bf16[3072,192]{1,0:T(8,128)(2,1)} %copy-done.1) | copy-start | bytes 3538948
  308.1 24.3 %collective-permute-start.13 = (bf16[96,768]{1,0:T(8,128)(2,1)S(1)}, bf16[96,768]{1,0:T(8,128)(2,1)S(1)}, u32[]{:S(2)}, u32[]{:S(2)}) collective-permute-start(bf16[96,768]{1,0:T(8,128)(2,1)S(1)} %get-tuple-element.109), channel_id=1, source_target_pairs={{0,2},{1,3},{2,4},{3,5},{4,6},{5,7},{6,0},{7,1},{8,10},{9,11},{10,... | collective-permute-start | bytes 442376 | tf_op jit(solution)/shard_map/ppermute | solution.py:788
  313.2 20.7 %collective-permute-start.14 = (bf16[96,768]{1,0:T(8,128)(2,1)S(1)}, bf16[96,768]{1,0:T(8,128)(2,1)S(1)}, u32[]{:S(2)}, u32[]{:S(2)}) collective-permute-start(bf16[96,768]{1,0:T(8,128)(2,1)S(1)} %get-tuple-element.111), channel_id=1, source_target_pairs={{0,4},{1,5},{2,6},{3,7},{4,0},{5,1},{6,2},{7,3},{8,12},{9,13},{10,... | collective-permute-start | bytes 442376 | tf_op jit(solution)/shard_map/ppermute | solution.py:788
  319.8 16.1 %collective-permute-start.15 = (bf16[96,768]{1,0:T(8,128)(2,1)S(1)}, bf16[96,768]{1,0:T(8,128)(2,1)S(1)}, u32[]{:S(2)}, u32[]{:S(2)}) collective-permute-start(bf16[96,768]{1,0:T(8,128)(2,1)S(1)} %get-tuple-element.110), channel_id=1, source_target_pairs={{0,6},{1,7},{2,0},{3,1},{4,2},{5,3},{6,4},{7,5},{8,14},{9,15},{10,... | collective-permute-start | bytes 442376 | tf_op jit(solution)/shard_map/ppermute | solution.py:788
  320.9 48.9 %copy-start.16 = (s32[3]{0:T(128)S(1)}, s32[3]{0:T(128)}, u32[]{:S(2)}) copy-start(s32[3]{0:T(128)} %pad_add_fusion.place_ref) | copy-start | bytes 40
  328.5 41.4 %copy-start.7 = (bf16[768,192]{1,0:T(8,128)(2,1)S(1)}, bf16[768,192]{1,0:T(8,128)(2,1)}, u32[]{:S(2)}) copy-start(bf16[768,192]{1,0:T(8,128)(2,1)} %copy-done.6) | copy-start | bytes 884740
  328.5 41.4 %copy-start.9 = (bf16[768,192]{1,0:T(8,128)(2,1)S(1)}, bf16[768,192]{1,0:T(8,128)(2,1)}, u32[]{:S(2)}) copy-start(bf16[768,192]{1,0:T(8,128)(2,1)} %copy-done.8) | copy-start | bytes 884740
  329.3 24.2 %collective-permute-start.4 = (bf16[768,192]{1,0:T(8,128)(2,1)S(1)}, bf16[768,192]{1,0:T(8,128)(2,1)S(1)}, u32[]{:S(2)}, u32[]{:S(2)}) collective-permute-start(bf16[768,192]{1,0:T(8,128)(2,1)S(1)} %copy-done.22), channel_id=1, source_target_pairs={{0,16},{8,24},{16,0},{24,8},{1,17},{9,25},{17,1},{25,9},{2,18},{10... | collective-permute-start | bytes 884744 | tf_op jit(solution)/shard_map/ppermute | solution.py:927
  332.4 21.1 %collective-permute-start.5 = (bf16[768,192]{1,0:T(8,128)(2,1)S(1)}, bf16[768,192]{1,0:T(8,128)(2,1)S(1)}, u32[]{:S(2)}, u32[]{:S(2)}) collective-permute-start(bf16[768,192]{1,0:T(8,128)(2,1)S(1)} %copy-done.20), channel_id=1, source_target_pairs={{0,24},{8,16},{16,8},{24,0},{1,25},{9,17},{17,9},{25,1},{2,26},{10... | collective-permute-start | bytes 884744 | tf_op jit(solution)/shard_map/ppermute | solution.py:927
  332.4 25.8 %collective-permute-start = (bf16[768,192]{1,0:T(8,128)(2,1)S(1)}, bf16[768,192]{1,0:T(8,128)(2,1)S(1)}, u32[]{:S(2)}, u32[]{:S(2)}) collective-permute-start(bf16[768,192]{1,0:T(8,128)(2,1)S(1)} %copy-done.18), channel_id=1, source_target_pairs={{0,8},{8,0},{16,24},{24,16},{1,9},{9,1},{17,25},{25,17},{2,10},{10... | collective-permute-start | bytes 884744 | tf_op jit(solution)/shard_map/ppermute | solution.py:927
  333.9 36.0 %collective-permute-start.1 = (bf16[768,192]{1,0:T(8,128)(2,1)}, bf16[768,192]{1,0:T(8,128)(2,1)S(1)}, u32[]{:S(2)}, u32[]{:S(2)}) collective-permute-start(bf16[768,192]{1,0:T(8,128)(2,1)} %get-tuple-element.71), channel_id=1, source_target_pairs={{0,16},{8,24},{16,0},{24,8},{1,17},{9,25},{17,1},{25,9},{2,18},{10... | collective-permute-start | bytes 884744 | tf_op jit(solution)/shard_map/ppermute | solution.py:927
  335.9 34.0 %collective-permute-start.2 = (bf16[768,192]{1,0:T(8,128)(2,1)}, bf16[768,192]{1,0:T(8,128)(2,1)S(1)}, u32[]{:S(2)}, u32[]{:S(2)}) collective-permute-start(bf16[768,192]{1,0:T(8,128)(2,1)} %get-tuple-element.72), channel_id=1, source_target_pairs={{0,24},{8,16},{16,8},{24,0},{1,25},{9,17},{17,9},{25,1},{2,26},{10... | collective-permute-start | bytes 884744 | tf_op jit(solution)/shard_map/ppermute | solution.py:927
  353.4 26.4 %collective-permute-start.16 = (bf16[96,768]{1,0:T(8,128)(2,1)S(1)}, bf16[96,768]{1,0:T(8,128)(2,1)S(1)}, u32[]{:S(2)}, u32[]{:S(2)}) collective-permute-start(bf16[96,768]{1,0:T(8,128)(2,1)S(1)} %fusion.7), channel_id=1, source_target_pairs={{0,8},{8,0},{16,24},{24,16},{1,9},{9,1},{17,25},{25,17},{2,10},{10... | collective-permute-start | bytes 442376 | tf_op jit(solution)/shard_map/ppermute | solution.py:790
  353.5 26.4 %collective-permute-start.17 = (bf16[96,768]{1,0:T(8,128)(2,1)S(1)}, bf16[96,768]{1,0:T(8,128)(2,1)}, u32[]{:S(2)}, u32[]{:S(2)}) collective-permute-start(bf16[96,768]{1,0:T(8,128)(2,1)S(1)} %fusion.7), channel_id=1, source_target_pairs={{0,16},{8,24},{16,0},{24,8},{1,17},{9,25},{17,1},{25,9},{2,18},{10... | collective-permute-start | bytes 442376 | tf_op jit(solution)/shard_map/ppermute | solution.py:790
  358.3 21.5 %collective-permute-start.18 = (bf16[96,768]{1,0:T(8,128)(2,1)S(1)}, bf16[96,768]{1,0:T(8,128)(2,1)}, u32[]{:S(2)}, u32[]{:S(2)}) collective-permute-start(bf16[96,768]{1,0:T(8,128)(2,1)S(1)} %fusion.7), channel_id=1, source_target_pairs={{0,24},{8,16},{16,8},{24,0},{1,25},{9,17},{17,9},{25,1},{2,26},{10... | collective-permute-start | bytes 442376 | tf_op jit(solution)/shard_map/ppermute | solution.py:790
  (28 other events, 100.2 us)
Sparse Core Ops, SparseCore 0:
  9.7 71.6 all-gather.3
  83.0 51.7 all-gather.5
  183.1 53.7 reduce-scatter.2
  238.4 39.8 all-gather.7
  280.4 31.9 reduce-scatter.4

commit v5 on v3

v5 whole, which is shorter than its diff:
```python
import functools

import jax
import jax.numpy as jnp
from jax import lax
from jax.experimental import pallas as pl
from jax.experimental.pallas import tpu as pltpu
from jax.sharding import PartitionSpec as P

PROMPT = 1024
GRP_WT = 1
GLEN = 3072
SHORT = 512
LONG = 1536
HD = 64
TQ = 512
KC = 512

epsilon = 1e-06
score_scale = 0.125
exp2_scale = 0.125 * 1.4426950408889634
root_half = 0.7071067811865476
density_scale = 0.3989422804014327
bf16 = jnp.bfloat16
f32 = jnp.float32

NT = (((1,), (1,)), ((), ()))
NN = (((1,), (0,)), ((), ()))
TN = (((0,), (0,)), ((), ()))


def mm(a, b, dims=NN):
    return lax.dot_general(a, b, dims, preferred_element_type=f32)


def natural_at(short_first, i):
    other = jnp.where(i == 2, 5, i - 1)
    return jnp.where(short_first | (i < 2), i, other)


def ordered_at(short_first, j):
    other = jnp.where(j == 5, 2, j + 1)
    return jnp.where(short_first | (j < 2), j, other)


def query_tiles(tile):
    def prompt(i, carry):
        tile(i, ())
        return carry

    def longer(i, carry):
        tile(i, (3, 4, 5))
        return carry

    lax.fori_loop(0, 2, prompt, 0)
    tile(2, (2,))
    lax.fori_loop(3, 6, longer, 0)


def remote(src, dst, sems, k, peer):
    return pltpu.make_async_remote_copy(
        src_ref=src,
        dst_ref=dst,
        send_sem=sems[0].at[k],
        recv_sem=sems[1].at[k],
        device_id=peer,
        device_id_type=pl.DeviceIdType.MESH,
    )


def send(src, dst, sems, k, peer):
    copy = remote(src, dst, sems, k, peer)
    copy.start()
    return copy


def attend_kernel(
    heads, lens_ref, tok_ref, w_ref, vec_ref, packed_ref, ctx_ref, lse_ref, full_ref,
    q_sc, k_sc, vt_sc, ct_sc, local_sem, s_sem, r_sem,
):
    s, w = lax.axis_index("seq"), lax.axis_index("wt")
    others = [flip(s, k) for k in (1, 2, 3)]
    short_first = lens_ref[0] == SHORT
    meet([(p, w) for p in others])
    width = heads * HD
    count = GLEN // 4

    def project(i, carry):
        rows = pl.ds(pl.multiple_of(i * TQ, TQ), TQ)
        x = mm(tok_ref[natural_at(short_first, i)], w_ref[...]) + vec_ref[0:1, :]
        x = (x * vec_ref[1:2, :]).astype(bf16)
        for h in range(heads):
            at = 3 * HD * h
            packed_ref[h, rows, :] = x[:, at : at + 3 * HD]
            q_sc[h, rows, :] = x[:, at : at + HD]
            k_sc[h, rows, :] = x[:, at + HD : at + 2 * HD]
            vt_sc[h, :, rows] = x[:, at + 2 * HD : at + 3 * HD].T
        return carry

    lax.fori_loop(0, GLEN // TQ, project, 0)

    def leaving(h):
        rows = pl.ds(pl.multiple_of(h * HD, HD), HD)
        there = full_ref.at[pl.ds(pl.multiple_of(s * width + h * HD, HD), HD), :]

        def part(p):
            return ctx_ref.at[rows, pl.ds(pl.multiple_of(p * count, 128), count)]

        copies = [
            remote(part(p), there, (s_sem, r_sem), 3 * h + k, (p, w)) for k, p in enumerate(others)
        ]
        return copies, pltpu.make_async_copy(part(s), there, local_sem.at[h])

    def one_head(h, carry):
        def tile(i, own_blocks):
            rows = pl.ds(pl.multiple_of(i * TQ, TQ), TQ)
            q = q_sc[h, rows, :]
            s1 = mm(k_sc[h, 0:PROMPT, :], q, NT)
            top = jnp.max(s1, axis=0, keepdims=True)
            if own_blocks:
                own = slice(own_blocks[0] * KC, (own_blocks[-1] + 1) * KC)
                s2 = mm(k_sc[h, own, :], q, NT)
                top = jnp.maximum(top, jnp.max(s2, axis=0, keepdims=True))
            top = top * exp2_scale
            p1 = jnp.exp2(s1 * exp2_scale - top)
            o = mm(vt_sc[h, :, 0:PROMPT], p1.astype(bf16))
            total = jnp.sum(p1, axis=0, keepdims=True)
            if own_blocks:
                p2 = jnp.exp2(s2 * exp2_scale - top)
                o = o + mm(vt_sc[h, :, own], p2.astype(bf16))
                total = total + jnp.sum(p2, axis=0, keepdims=True)
            ct_sc[i] = (o / total).astype(bf16)
            lse_ref[h, :, rows] = top + jnp.log2(total)

        query_tiles(tile)

        def settle(j, carry):
            rows = pl.ds(pl.multiple_of(h * HD, HD), HD)
            lanes = pl.ds(pl.multiple_of(j * SHORT, SHORT), SHORT)
            ctx_ref[rows, lanes] = ct_sc[ordered_at(short_first, j)]
            return carry

        lax.fori_loop(0, GLEN // SHORT, settle, 0)
        copies, own = leaving(h)
        for copy in copies:
            copy.start()
        own.start()
        return carry

    lax.fori_loop(0, heads, one_head, 0)
    for h in range(heads):
        copies, own = leaving(h)
        own.wait()
        for copy in copies:
            copy.wait()


def attend(lens, tokens_all, weight, vec, heads):
    width = 3 * HD * heads
    return pl.pallas_call(
        functools.partial(attend_kernel, heads),
        out_shape=(
            jax.ShapeDtypeStruct((heads, GLEN, 3 * HD), bf16),
            jax.ShapeDtypeStruct((HD * heads, GLEN), bf16),
            jax.ShapeDtypeStruct((heads, 1, GLEN), f32),
            jax.ShapeDtypeStruct((4 * HD * heads, GLEN // 4), bf16),
        ),
        in_specs=[pl.BlockSpec(memory_space=pltpu.SMEM), IN_VMEM, IN_VMEM, IN_VMEM],
        out_specs=(IN_VMEM, IN_VMEM, IN_VMEM, ANYWHERE),
        scratch_shapes=[
            pltpu.VMEM((heads, GLEN, HD), bf16),
            pltpu.VMEM((heads, GLEN, HD), bf16),
            pltpu.VMEM((heads, HD, GLEN), bf16),
            pltpu.VMEM((GLEN // TQ, HD, TQ), bf16),
            pltpu.SemaphoreType.DMA((heads,)),
        ]
        + dma_sems(3 * heads),
        compiler_params=remote_params(1),
        cost_estimate=pl.CostEstimate(
            flops=2 * GLEN * 768 * width + heads * 4 * 256 * 5767168,
            bytes_accessed=2 * GLEN * (768 + width),
            transcendentals=heads * 5767168,
        ),
        name="attend",
    )(lens, tokens_all.reshape(GLEN // TQ, TQ, -1), weight, vec)


def attend_back_kernel(
    heads, n, lens_ref, packed_hbm, ctx_ref, g_hbm, lse_ref, scale_ref, tok_hbm, mine_hbm, mate_hbm,
    pieces_o, dw_o, exp_o, late_o,
    packed_v, tok_v, mine_v, got, e2, gh0, gh1, gh2, st0, st1, st2,
    q_sc, k_sc, v_sc, kt_sc, g_sc, g_nat, delta_sc, delta_nat, dqt_sc, dk_sc, dv_sc, acc,
    l_in, l_g, l_out, s_g, r_g, s_p, r_p, s_c, r_c, s_e, r_e,
):
    s, w = lax.axis_index("seq"), lax.axis_index("wt")
    others = [flip(s, k) for k in (1, 2, 3)]
    mate = (s, flip(w, 1))
    short_first = lens_ref[0] == SHORT
    count = GLEN // 4
    width = heads * HD
    gh, stage = (gh0, gh1, gh2)[:heads], (st0, st1, st2)[:heads]
    loads = [
        pltpu.make_async_copy(packed_hbm.at[h], packed_v.at[h], l_in.at[h]) for h in range(heads)
    ] + [
        pltpu.make_async_copy(mine_hbm, mine_v, l_in.at[heads]),
        pltpu.make_async_copy(tok_hbm, tok_v, l_in.at[heads + 1]),
    ]
    for copy in loads:
        copy.start()
    meet([(p, w) for p in others] + [mate])

    def coming(h, own=False):
        def part(p):
            return g_hbm.at[pl.ds(pl.multiple_of(p * width + h * HD, HD), HD), :]

        there = gh[h].at[:, pl.ds(pl.multiple_of(s * count, 128), count)]
        if own:
            return pltpu.make_async_copy(part(s), there, l_g.at[h])
        return [remote(part(p), there, (s_g, r_g), 3 * h + k, (p, w)) for k, p in enumerate(others)]

    def leaving(h):
        copies = [
            remote(stage[h].at[p], pieces_o.at[h, s], (s_p, r_p), 3 * h + k, (p, w))
            for k, p in enumerate(others)
        ]
        return copies, pltpu.make_async_copy(stage[h].at[s], pieces_o.at[h, s], l_out.at[h])

    over_pair = remote(mate_hbm, got, (s_c, r_c), 0, mate)
    over_plane = [
        remote(got.at[p], e2.at[s], (s_e, r_e), k, (p, w)) for k, p in enumerate(others)
    ]
    for h in range(heads):
        for copy in coming(h) + [coming(h, True)]:
            copy.start()
        if h == 0:
            over_pair.start()
    late_o[...] = jnp.zeros_like(late_o)
    zs = exp_o.shape[0]

    def prologue(h):
        loads[h].wait()

        def split(i, carry):
            rows = pl.ds(pl.multiple_of(i * TQ, TQ), TQ)
            x = packed_v[h, rows, :]
            q_sc[i] = x[:, 0:HD]
            k = x[:, HD : 2 * HD]
            k_sc[i] = k
            kt_sc[i] = k.T
            v_sc[i] = x[:, 2 * HD : 3 * HD]
            return carry

        lax.fori_loop(0, GLEN // TQ, split, 0)
        dk_sc[...] = jnp.zeros_like(dk_sc)
        dv_sc[...] = jnp.zeros_like(dv_sc)
        if h == 0:
            loads[heads].wait()
            over_pair.wait_recv()

            def pair_sum(i, carry):
                q, z = i // zs, lax.rem(i, zs)
                got[q, z] = (got[q, z].astype(f32) + mine_v[q, z].astype(f32)).astype(bf16)
                return carry

            lax.fori_loop(0, 4 * zs, pair_sum, 0)
        coming(h, True).wait()
        for copy in coming(h):
            copy.wait_recv()
        if h == 0:
            for copy in over_plane:
                copy.start()
            e2[s] = got[s]

        def inner(j, carry):
            lanes = pl.ds(pl.multiple_of(j * TQ, TQ), TQ)
            g = gh[h][:, lanes]
            g_nat[j] = g
            product = g.astype(f32) * ctx_ref[HD * h : HD * (h + 1), lanes].astype(f32)
            delta_nat[j] = jnp.sum(product, axis=0, keepdims=True)
            return carry

        def order(i, carry):
            g_sc[i] = g_nat[natural_at(short_first, i)]
            delta_sc[i] = delta_nat[natural_at(short_first, i)]
            return carry

        lax.fori_loop(0, GLEN // TQ, inner, 0)
        lax.fori_loop(0, GLEN // TQ, order, 0)

    def epilogue(h):
        half = SHORT // 2
        lanes = slice(HD * h, HD * (h + 1))

        def settle(j, carry):
            i = ordered_at(short_first, j)
            dq = dqt_sc[i].T.astype(bf16)
            dk = (dk_sc[i] * score_scale).astype(bf16)
            dv = dv_sc[i].astype(bf16).astype(f32)
            late_o[2:3, lanes] += jnp.sum(dv * v_sc[i].astype(f32), axis=0, keepdims=True)
            dv = (dv * scale_ref[h]).astype(bf16)
            late_o[0:1, lanes] += jnp.sum(dq.astype(f32), axis=0, keepdims=True)
            late_o[1:2, lanes] += jnp.sum(dv.astype(f32), axis=0, keepdims=True)
            for r in range(2):
                u = 2 * j + r
                p, there = u // 3, pl.ds(pl.multiple_of(lax.rem(u, 3) * half, half), half)
                rows = slice(r * half, (r + 1) * half)
                stage[h][p, there, 0:HD] = dq[rows]
                stage[h][p, there, HD : 2 * HD] = dk[rows]
                stage[h][p, there, 2 * HD : 3 * HD] = dv[rows]
            return carry

        lax.fori_loop(0, GLEN // SHORT, settle, 0)
        copies, own = leaving(h)
        for copy in copies:
            copy.start()
        own.start()

    def tile_of(h):
        def tile(i, own_blocks):
            q = q_sc[i]
            g = g_sc[i]
            lse = lse_ref[h, :, pl.ds(pl.multiple_of(i * TQ, TQ), TQ)]
            delta = delta_sc[i]
            dq = jnp.zeros((HD, TQ), f32)
            for j in (0, 1) + own_blocks:
                sc = mm(k_sc[j], q, NT)
                p = jnp.exp2(sc * exp2_scale - lse)
                dp = mm(v_sc[j], g)
                ds = (p * (dp - delta)).astype(bf16)
                dv_sc[j] += mm(p.astype(bf16), g, NT)
                dk_sc[j] += mm(ds, q)
                dq = dq + mm(kt_sc[j], ds)
            dqt_sc[i] = dq * score_scale

        return tile

    def one_head(h, carry):
        for j in range(heads):

            @pl.when(h == j)
            def _(j=j):
                prologue(j)

        query_tiles(tile_of(h))
        for j in range(heads):

            @pl.when(h == j)
            def _(j=j):
                epilogue(j)

        return carry

    lax.fori_loop(0, heads, one_head, 0)
    loads[heads + 1].wait()
    acc[...] = jnp.zeros_like(acc)

    def weight_grad(p, carry):
        x = tok_v[pl.ds(pl.multiple_of(p * count, count), count), :]
        for h in range(heads):
            acc[:, 3 * HD * h : 3 * HD * (h + 1)] += mm(x, stage[h][p], TN)
        return carry

    lax.fori_loop(0, 4, weight_grad, 0)
    own_rows = dw_o.shape[1]
    for k in range(n):
        dw_o[k] = acc[k * own_rows : (k + 1) * own_rows, :].astype(bf16)
    for copy in over_plane:
        copy.wait_recv()

    def plane_sum(z, carry):
        t = [e2[q, z].astype(f32) for q in range(4)]
        exp_o[z] = ((t[0] + t[1]) + (t[2] + t[3])).astype(bf16)
        return carry

    lax.fori_loop(0, zs, plane_sum, 0)
    for h in range(heads):
        copies, own = leaving(h)
        own.wait()
        for copy in copies:
            copy.wait()
        for copy in coming(h):
            copy.wait_send()
    over_pair.wait_send()
    for copy in over_plane:
        copy.wait_send()


def attend_back(n, lens, packed, ctx, g, lse, scale, tokens_all, mine, mate):
    heads = packed.shape[0]
    width = 3 * HD * heads
    d = tokens_all.shape[1]
    count = GLEN // 4
    _, zs, own, wide = mine.shape
    blocks = GLEN // TQ
    rows64 = pltpu.VMEM((blocks, TQ, HD), bf16)
    blocks64 = pltpu.VMEM((blocks, HD, TQ), bf16)
    lanes64 = pltpu.VMEM((HD, GLEN), bf16)
    return pl.pallas_call(
        functools.partial(attend_back_kernel, heads, n),
        out_shape=(
            jax.ShapeDtypeStruct((heads, 4, count, 3 * HD), bf16),
            jax.ShapeDtypeStruct((n, d // n, width), bf16),
            jax.ShapeDtypeStruct((zs, own, wide), bf16),
            jax.ShapeDtypeStruct((8, HD * heads), f32),
        ),
        in_specs=[pl.BlockSpec(memory_space=pltpu.SMEM)]
        + [ANYWHERE, IN_VMEM, ANYWHERE, IN_VMEM, IN_VMEM, ANYWHERE, ANYWHERE, ANYWHERE],
        out_specs=(ANYWHERE, IN_VMEM, IN_VMEM, IN_VMEM),
        scratch_shapes=[
            pltpu.VMEM(packed.shape, bf16),
            pltpu.VMEM(tokens_all.shape, bf16),
            pltpu.VMEM(mine.shape, bf16),
            pltpu.VMEM(mine.shape, bf16),
            pltpu.VMEM(mine.shape, bf16),
            lanes64,
            lanes64,
            lanes64,
        ]
        + [pltpu.VMEM((4, count, 3 * HD), bf16)] * 3
        + [
            rows64,
            rows64,
            rows64,
            blocks64,
            blocks64,
            blocks64,
            pltpu.VMEM((blocks, 1, TQ), f32),
            pltpu.VMEM((blocks, 1, TQ), f32),
            pltpu.VMEM((blocks, HD, TQ), f32),
            pltpu.VMEM((blocks, TQ, HD), f32),
            pltpu.VMEM((blocks, TQ, HD), f32),
            pltpu.VMEM((d, width), f32),
            pltpu.SemaphoreType.DMA((heads + 2,)),
            pltpu.SemaphoreType.DMA((heads,)),
            pltpu.SemaphoreType.DMA((heads,)),
        ]
        + dma_sems(3 * heads)
        + dma_sems(3 * heads)
        + dma_sems(1)
        + dma_sems(3),
        compiler_params=remote_params(2),
        cost_estimate=pl.CostEstimate(
            flops=heads * 10 * 256 * 5767168 + 2 * GLEN * d * width,
            bytes_accessed=2 * GLEN * (3 * width + d),
            transcendentals=heads * 5767168,
        ),
        name="attend_back",
    )(lens, packed, ctx, g, lse, scale, tokens_all, mine, mate)


def meet(peers):
    barrier = pltpu.get_barrier_semaphore()
    for peer in peers:
        pl.semaphore_signal(barrier, inc=1, device_id=peer, device_id_type=pl.DeviceIdType.MESH)
    pl.semaphore_wait(barrier, len(peers))


def flip(index, bits):
    for bit in (1, 2):
        if bits & bit:
            index = index + bit - 2 * bit * ((index // bit) % 2)
    return index


def remote_params(number):
    return pltpu.CompilerParams(
        collective_id=number, has_side_effects=True, vmem_limit_bytes=56 * 2**20
    )


ANYWHERE = pl.BlockSpec(memory_space=pl.ANY)
IN_VMEM = pl.BlockSpec(memory_space=pltpu.VMEM)


def dma_sems(count):
    return [pltpu.SemaphoreType.DMA((count,)), pltpu.SemaphoreType.DMA((count,))]


def gather_kernel(
    n, tok_ref, cols_ref, out_ref, tok_all, cols_all, out_all,
    tok_buf, cols_buf, out_buf, local_sem, s_tok, r_tok, s_w, r_w, s_f, r_f,
):
    s, w = lax.axis_index("seq"), lax.axis_index("wt")
    rows = tok_ref.shape[0]
    half = rows // 2
    by_x, by_y, mate = (flip(s, 1), w), (flip(s, 2), w), (s, flip(w, 1))
    far = [(s, lax.rem(w + 2 * j, n)) for j in range(1, n // 2)]
    meet([by_x, by_y, mate] + far)

    def part(owner, k):
        return pl.ds(pl.multiple_of(owner * rows + k * half, half), half)

    tok = (s_tok, r_tok)
    first = [pl.ds(0, half), pl.ds(half, half)]
    x0 = send(tok_ref.at[first[0]], tok_all.at[part(s, 0)], tok, 0, by_x)
    y1 = send(tok_ref.at[first[1]], tok_all.at[part(s, 1)], tok, 1, by_y)
    x1 = send(tok_ref.at[first[1]], tok_all.at[part(s, 1)], tok, 2, by_x)
    y0 = send(tok_ref.at[first[0]], tok_all.at[part(s, 0)], tok, 3, by_y)
    held = []
    for k, peer in enumerate(far + [mate]):
        for i, (src, dst) in enumerate(((cols_ref, cols_all), (out_ref, out_all))):
            held.append(send(src, dst.at[w], (s_w, r_w), 2 * k + i, peer))
    own = []
    for i, (src, buf) in enumerate(((tok_ref, tok_buf), (cols_ref, cols_buf), (out_ref, out_buf))):
        own.append(pltpu.make_async_copy(src, buf, local_sem.at[i]))
        own[-1].start()
    for copy in own:
        copy.wait()
    targets = (
        (tok_buf, tok_all.at[pl.ds(pl.multiple_of(s * rows, rows), rows)]),
        (cols_buf, cols_all.at[w]),
        (out_buf, out_all.at[w]),
    )
    own = []
    for i, (buf, dst) in enumerate(targets):
        own.append(pltpu.make_async_copy(buf, dst, local_sem.at[3 + i]))
        own[-1].start()
    passed = []
    x0.wait_recv()
    there = tok_all.at[part(flip(s, 1), 0)]
    passed.append(send(there, there, tok, 4, by_y))
    y1.wait_recv()
    there = tok_all.at[part(flip(s, 2), 1)]
    passed.append(send(there, there, tok, 5, by_x))
    for j in range(1, n // 2):
        origin = lax.rem(w + n - 2 * j, n)
        for i, dst in enumerate((cols_all, out_all)):
            k = 2 * (j - 1) + i
            held[k].wait_recv()
            passed.append(send(dst.at[origin], dst.at[origin], (s_f, r_f), k, mate))
    for copy in own:
        copy.wait()
    x1.wait_recv()
    y0.wait_recv()
    for copy in held[n - 2 :]:
        copy.wait_recv()
    for copy in passed:
        copy.wait_recv()
    for copy in [x0, x1, y0, y1] + held + passed:
        copy.wait_send()


def gather_in(n, tokens, own_columns, output_weight):
    rows, d = tokens.shape
    return pl.pallas_call(
        functools.partial(gather_kernel, n),
        out_shape=(
            jax.ShapeDtypeStruct((4 * rows, d), bf16),
            jax.ShapeDtypeStruct((n,) + own_columns.shape, bf16),
            jax.ShapeDtypeStruct((n,) + output_weight.shape, bf16),
        ),
        in_specs=[ANYWHERE] * 3,
        out_specs=(ANYWHERE,) * 3,
        scratch_shapes=[
            pltpu.VMEM(tokens.shape, bf16),
            pltpu.VMEM(own_columns.shape, bf16),
            pltpu.VMEM(output_weight.shape, bf16),
            pltpu.SemaphoreType.DMA((6,)),
        ]
        + dma_sems(6)
        + dma_sems(n)
        + dma_sems(n - 2),
        compiler_params=remote_params(0),
        name="gather_in",
    )(tokens, own_columns, output_weight)


def final_kernel(
    heads, n, base_hbm, pieces_hbm, w_hbm, con_ref, out_ref, att_ref, exp_ref, vec_ref, late_ref,
    tok_o, g_con, r_out, g_exp, g_att, r_vec2, r_late2,
    base_v, pieces_v, w_v, r_con, h_att, m_att, r_att, r_exp, r_vec, r_late,
    l_in, *sems,
):
    s, w = lax.axis_index("seq"), lax.axis_index("wt")
    z, c = w // 2, lax.rem(w, 2)
    nz = n // 2
    others = [flip(s, k) for k in (1, 2, 3)]
    seq_peers = [(p, w) for p in others]
    mate = (s, flip(w, 1))
    wt_peers = [(s, lax.rem(w + j, n)) for j in range(1, n)]
    names = ("pair", "vec", "late", "con", "exp", "out", "att", "vec2", "late2", "con2", "exp2", "att2")
    sem = {name: (sems[2 * k], sems[2 * k + 1]) for k, name in enumerate(names)}
    loads = [
        pltpu.make_async_copy(src, dst, l_in.at[k])
        for k, (src, dst) in enumerate(((pieces_hbm, pieces_v), (w_hbm, w_v), (base_hbm, base_v)))
    ]
    for copy in loads:
        copy.start()
    meet(seq_peers + wt_peers)
    pair = [send(att_ref.at[2 * k + 1 - c], h_att.at[k], sem["pair"], k, mate) for k in range(nz)]
    cons = [send(con_ref.at[p], r_con.at[s], sem["con"], k, (p, w)) for k, p in enumerate(others)]
    far = [lax.rem(z + j, nz) for j in range(1, nz)]
    exps = [
        send(exp_ref.at[k], r_exp.at[z], sem["exp"], j, (s, 2 * k + c)) for j, k in enumerate(far)
    ]
    vecs = [
        send(vec_ref.at[lax.rem(w + j, n)], r_vec.at[w], sem["vec"], j - 1, wt_peers[j - 1])
        for j in range(1, n)
    ]
    lates = [send(late_ref, r_late.at[w], sem["late"], j, p) for j, p in enumerate(wt_peers)]
    outs = [send(out_ref, r_out.at[s], sem["out"], k, p) for k, p in enumerate(seq_peers)]
    r_con[s] = con_ref[s]
    r_exp[z] = exp_ref[z]
    r_vec[w] = vec_ref[w]
    r_late[w] = late_ref[...]
    r_out[s] = out_ref[...]
    for copy in pair:
        copy.wait_recv()
    for k in range(nz):
        m_att[k] = (att_ref[2 * k + c].astype(f32) + h_att[k].astype(f32)).astype(bf16)
    atts = [send(m_att.at[k], r_att.at[z], sem["att"], j, (s, 2 * k + c)) for j, k in enumerate(far)]
    r_att[z] = m_att[z]
    for copy in loads:
        copy.wait()
    cols = 3 * HD
    rows = tok_o.shape[0]
    block = rows // 3

    def tokens_block(i, carry):
        there = pl.ds(pl.multiple_of(i * block, block), block)
        total = base_v[there, :]
        for h in range(heads):
            for k in range(4):
                at = (heads * k + h) * cols
                total = total + mm(pieces_v[h, k, there, :], w_v[:, at : at + cols], NT)
        tok_o[there, :] = total
        return carry

    lax.fori_loop(0, 1, tokens_block, 0)

    def total_of(ref, count):
        total = ref[0].astype(f32)
        for k in range(1, count):
            total = total + ref[k].astype(f32)
        return total

    for copy in cons:
        copy.wait_recv()
    g_con[s] = total_of(r_con, 4).astype(bf16)
    con2 = [send(g_con.at[s], g_con.at[s], sem["con2"], k, p) for k, p in enumerate(seq_peers)]
    for copy in vecs + lates:
        copy.wait_recv()
    r_vec2[s] = total_of(r_vec, n)
    r_late2[s] = total_of(r_late, n)
    vec2 = [send(r_vec2.at[s], r_vec2.at[s], sem["vec2"], k, p) for k, p in enumerate(seq_peers)]
    late2 = [send(r_late2.at[s], r_late2.at[s], sem["late2"], k, p) for k, p in enumerate(seq_peers)]
    lax.fori_loop(1, 2, tokens_block, 0)
    for copy in exps:
        copy.wait_recv()
    g_exp[s] = total_of(r_exp, nz).astype(bf16)
    exp2 = [send(g_exp.at[s], g_exp.at[s], sem["exp2"], k, p) for k, p in enumerate(seq_peers)]
    for copy in atts:
        copy.wait_recv()
    g_att[s] = total_of(r_att, nz).astype(bf16)
    att2 = [send(g_att.at[s], g_att.at[s], sem["att2"], k, p) for k, p in enumerate(seq_peers)]
    lax.fori_loop(2, 3, tokens_block, 0)
    for copy in outs + con2 + vec2 + late2 + exp2 + att2:
        copy.wait_recv()
    for copy in pair + cons + exps + vecs + lates + outs + atts + con2 + vec2 + late2 + exp2 + att2:
        copy.wait_send()


def final(n, base, pieces, weight, con, out, att, exp_part, vec, late):
    heads = pieces.shape[0]
    r, d = out.shape
    cols = att.shape[2]
    nz = n // 2
    wide = exp_part.shape[2]
    counts = (nz, n - 1, n - 1, 3, nz - 1, 3, nz - 1, 3, 3, 3, 3, 3)
    return pl.pallas_call(
        functools.partial(final_kernel, heads, n),
        out_shape=(
            jax.ShapeDtypeStruct(base.shape, f32),
            jax.ShapeDtypeStruct((4, r, d), bf16),
            jax.ShapeDtypeStruct((4, r, d), bf16),
            jax.ShapeDtypeStruct((4, r, wide), bf16),
            jax.ShapeDtypeStruct((4, r, cols), bf16),
            jax.ShapeDtypeStruct((4,) + vec.shape[1:], f32),
            jax.ShapeDtypeStruct((4,) + late.shape, f32),
        ),
        in_specs=[ANYWHERE] * 3 + [IN_VMEM] * 6,
        out_specs=(IN_VMEM,) * 7,
        scratch_shapes=[
            pltpu.VMEM(base.shape, f32),
            pltpu.VMEM(pieces.shape, bf16),
            pltpu.VMEM(weight.shape, bf16),
            pltpu.VMEM((4, r, d), bf16),
            pltpu.VMEM((nz, r, cols), bf16),
            pltpu.VMEM((nz, r, cols), bf16),
            pltpu.VMEM((nz, r, cols), bf16),
            pltpu.VMEM((nz, r, wide), bf16),
            pltpu.VMEM((n,) + vec.shape[1:], f32),
            pltpu.VMEM((n,) + late.shape, f32),
            pltpu.SemaphoreType.DMA((3,)),
        ]
        + [sem for count in counts for sem in dma_sems(count)],
        compiler_params=remote_params(3),
        cost_estimate=pl.CostEstimate(
            flops=8 * base.shape[0] * d * cols, bytes_accessed=8 * d * cols, transcendentals=0
        ),
        name="final",
    )(base, pieces, weight, con, out, att, exp_part, vec, late)


def finish_kernel(
    n, heads, place_ref, head_ref, con_ref, out_ref, exp_ref, att_ref, vec_ref, late_ref,
    con_o, out_o, exp_o, att_o, *rest,
):
    vec_os, unit_os, query_o, value_o, gate_o = rest[:7], rest[7:9], rest[9], rest[10], rest[11]

    def add4(parts):
        return (parts[0] + parts[1]) + (parts[2] + parts[3])

    out_o[...] = add4([out_ref[k].astype(f32) for k in range(4)])
    wide, cols = exp_ref.shape[2], att_ref.shape[2]
    for k in range(4):
        con_o[k] = con_ref[k].astype(f32)
        exp_o[:, k * wide : (k + 1) * wide] = exp_ref[k].astype(f32)
        att_o[:, k * cols : (k + 1) * cols] = att_ref[k].astype(f32)
    vec = add4([vec_ref[k] for k in range(4)])
    own = vec_os[0].shape[1]
    for k, ref in enumerate(vec_os):
        ref[...] = vec[k : k + 1, 0:own]
    for k, ref in enumerate(unit_os):
        ref[...] = vec[8 + k : 9 + k, :]
    rows = [jnp.concatenate([late_ref[k, j : j + 1, :] for k in range(4)], axis=1) for j in range(2)]
    for k in range(n):

        @pl.when(place_ref[3] == k)
        def _(k=k):
            query_o[...] = rows[0][:, k * own : (k + 1) * own]
            value_o[...] = rows[1][:, k * own : (k + 1) * own]

    gates = []
    for k in range(4):
        for h in range(heads):
            part = late_ref[k, 2:3, HD * h : HD * (h + 1)]
            gates.append(jnp.sum(part, axis=1, keepdims=True))
    gate_o[...] = jnp.concatenate(gates, axis=1) * head_ref[...]


def finish(n, heads, place, head_row, con, out, exp_all, att, vec, late):
    r, d = out.shape[1:]
    wide, cols = exp_all.shape[2], att.shape[2]
    units = vec.shape[2]
    row = jax.ShapeDtypeStruct((1, r), f32)
    return pl.pallas_call(
        functools.partial(finish_kernel, n, heads),
        out_shape=(
            jax.ShapeDtypeStruct(con.shape, f32),
            jax.ShapeDtypeStruct((r, d), f32),
            jax.ShapeDtypeStruct((r, 4 * wide), f32),
            jax.ShapeDtypeStruct((r, 4 * cols), f32),
        )
        + (row,) * 7
        + (jax.ShapeDtypeStruct((1, units), f32),) * 2
        + (row,) * 2
        + (jax.ShapeDtypeStruct((1, 4 * heads), f32),),
        in_specs=[pl.BlockSpec(memory_space=pltpu.SMEM)] + [IN_VMEM] * 7,
        out_specs=(IN_VMEM,) * 16,
        compiler_params=pltpu.CompilerParams(vmem_limit_bytes=32 * 2**20),
        name="finish",
    )(place, head_row, con, out, exp_all, att, vec, late)


(OUT_BIAS, GAIN1, SHIFT1, HIDDEN_SCALE, CON_BIAS, GAIN2, SHIFT2, HIDDEN_MASK) = range(8)
(S_OUT_BIAS, S_GAIN1, S_SHIFT1, S_CON_BIAS, S_GAIN2, S_SHIFT2, S_HIDDEN) = range(7)


def gelu_parts(x):
    bell = jnp.exp(-0.5 * (x * x))
    t = 1.0 / (1.0 + (0.3275911 * root_half) * jnp.abs(x))
    poly = t * (
        0.127414796 + t * (-0.142248368 + t * (0.7107068705 + t * (-0.7265760135 + t * 0.5307027145)))
    )
    tail = poly * bell
    cumulative = jnp.where(x < 0.0, tail, 1.0 - tail)
    return x * cumulative, cumulative + x * bell * density_scale


def norm_parts(summed):
    centre = summed - jnp.mean(summed, axis=-1, keepdims=True)
    inverse = lax.rsqrt(jnp.mean(centre * centre, axis=-1, keepdims=True) + epsilon)
    return (centre * inverse, inverse)


def norm_back(grad_normed, normed, inverse):
    return inverse * (
        grad_normed
        - jnp.mean(grad_normed, axis=-1, keepdims=True)
        - normed * jnp.mean(grad_normed * normed, axis=-1, keepdims=True)
    )


def feed_forward_kernel(
    steps, chunk,
    place_ref, ctx_ref, tok_ref, cot_ref, wo_ref, we_ref, wc_ref, wide_ref, unit_ref,
    lo_ref, dt1_ref, gctx_ref, vec_ref, dwc_ref, mine_ref, mate_ref, dwo_ref,
    sw_ref, su_ref, act_sc, gh_sc, low_sc, gb_sc, ga_sc, ctx_sc, gelu_sc, slope_sc,
):
    i = pl.program_id(0)
    block = tok_ref.shape[0]
    units = we_ref.shape[1]
    rows = pl.ds(pl.multiple_of(i * block, block), block)

    @pl.when(i == 0)
    def _():
        sw_ref[...] = jnp.zeros_like(sw_ref)
        su_ref[...] = jnp.zeros_like(su_ref)

    def wide(k):
        return wide_ref[k : k + 1, :]

    def add_sum(ref, k, cols, value):
        ref[k : k + 1, cols] += jnp.sum(value, axis=0, keepdims=True)

    full = slice(None)
    ctx = ctx_ref[...]
    ctx_sc[:, rows] = ctx
    summed = mm(ctx, wo_ref[...], TN) + wide(OUT_BIAS) + tok_ref[...].astype(f32)
    n1, inv1 = norm_parts(summed)
    s1 = n1 * wide(GAIN1) + wide(SHIFT1)
    hs = wide(HIDDEN_SCALE)
    first = s1 * hs
    low = first.astype(bf16)
    low_sc[rows, :] = low
    branch = first + wide(CON_BIAS)
    for j in range(units // chunk):
        cols = slice(j * chunk, (j + 1) * chunk)
        hidden = mm(low, we_ref[:, cols]) + unit_ref[0:1, cols]
        gelu, slope = gelu_parts(hidden)
        scale = unit_ref[1:2, cols]
        gelu_sc[:, cols] = gelu.astype(gelu_sc.dtype)
        slope_sc[:, cols] = (slope * scale).astype(slope_sc.dtype)
        act = (gelu * scale).astype(bf16)
        act_sc[rows, cols] = act
        branch = branch + mm(act, wc_ref[cols, :])
    n2, inv2 = norm_parts(branch)
    s2 = n2 * wide(GAIN2) + wide(SHIFT2)
    lo_ref[...] = (s2 * hs).astype(bf16)
    dy = cot_ref[...].astype(f32)
    e2 = dy * hs
    add_sum(sw_ref, S_GAIN2, full, e2 * n2)
    add_sum(sw_ref, S_SHIFT2, full, e2)
    dt2 = norm_back(e2 * wide(GAIN2), n2, inv2)
    gb = dt2.astype(bf16)
    gb_sc[rows, :] = gb
    add_sum(sw_ref, S_CON_BIAS, full, gb.astype(f32))
    d_first = dt2
    for j in range(units // chunk):
        cols = slice(j * chunk, (j + 1) * chunk)
        d_act = mm(gb, wc_ref[cols, :], NT)
        add_sum(su_ref, 1, cols, d_act * gelu_sc[:, cols].astype(f32))
        gh = d_act * slope_sc[:, cols].astype(f32)
        add_sum(su_ref, 0, cols, gh)
        gh = gh.astype(bf16)
        gh_sc[rows, cols] = gh
        d_first = d_first + mm(gh, we_ref[:, cols], NT)
    e1 = d_first * hs
    add_sum(sw_ref, S_GAIN1, full, e1 * n1)
    add_sum(sw_ref, S_SHIFT1, full, e1)
    add_sum(sw_ref, S_HIDDEN, full, dy * s2 + d_first * s1)
    dt1 = norm_back(e1 * wide(GAIN1), n1, inv1)
    dt1_ref[...] = dt1
    ga = dt1.astype(bf16)
    ga_sc[rows, :] = ga
    add_sum(sw_ref, S_OUT_BIAS, full, ga.astype(f32))
    gctx_ref[...] = mm(wo_ref[...], ga, NT).astype(bf16)

    @pl.when(i == steps - 1)
    def _():
        for j in range(units // chunk):
            cols = slice(j * chunk, (j + 1) * chunk)
            dwc_ref[cols, :] = mm(act_sc[:, cols], gb_sc[...], TN).astype(bf16)
            part = mm(low_sc[...], gh_sc[:, cols], TN).astype(bf16)
            own, wide_cols = mine_ref.shape[2:]
            for c in range(2):

                @pl.when(place_ref[2] == c)
                def _(part=part, j=j, c=c):
                    for q in range(chunk // wide_cols):
                        at = j * (chunk // wide_cols) + q
                        inner = slice(q * wide_cols, (q + 1) * wide_cols)
                        for z in range(mine_ref.shape[1]):
                            mine = (2 * z + c) * own
                            mate = (2 * z + 1 - c) * own
                            mine_ref[at, z] = part[mine : mine + own, inner]
                            mate_ref[at, z] = part[mate : mate + own, inner]

        dwo_ref[...] = mm(ctx_sc[...], ga_sc[...]).astype(bf16)
        vec_ref[...] = jnp.zeros_like(vec_ref)
        sw_ref[S_HIDDEN : S_HIDDEN + 1, :] *= wide(HIDDEN_MASK)
        su_ref[1:2, :] *= unit_ref[2:3, :]
        own_wide, own_units = mine_ref.shape[2], vec_ref.shape[2]
        for k in range(vec_ref.shape[0]):
            vec_ref[k, 0:8, 0:own_wide] = sw_ref[:, k * own_wide : (k + 1) * own_wide]
            vec_ref[k, 8:16, :] = su_ref[:, k * own_units : (k + 1) * own_units]


def feed_forward(n, place, ctx_t, tokens, cotangent, wo, we, wc, wide, unit):
    steps, chunk, keep = 3, 768, f32
    rows, d = tokens.shape
    units = we.shape[1]
    block = rows // steps
    halves = (4, n // 2, d // n, units // 4)
    tile = pl.BlockSpec((block, d), lambda i: (i, 0))
    lanes = pl.BlockSpec((d, block), lambda i: (0, i))

    def once(shape):
        return pl.BlockSpec(shape, lambda i: (0, 0), pipeline_mode=pl.Buffered(1))

    def once3(shape):
        return pl.BlockSpec(shape, lambda i: (0, 0, 0), pipeline_mode=pl.Buffered(1))

    def once4(shape):
        return pl.BlockSpec(shape, lambda i: (0, 0, 0, 0), pipeline_mode=pl.Buffered(1))

    return pl.pallas_call(
        functools.partial(feed_forward_kernel, steps, chunk),
        out_shape=(
            jax.ShapeDtypeStruct((rows, d), bf16),
            jax.ShapeDtypeStruct((rows, d), f32),
            jax.ShapeDtypeStruct((d, rows), bf16),
            jax.ShapeDtypeStruct((n, 16, units // n), f32),
            jax.ShapeDtypeStruct((units, d), bf16),
            jax.ShapeDtypeStruct(halves, bf16),
            jax.ShapeDtypeStruct(halves, bf16),
            jax.ShapeDtypeStruct((d, d), bf16),
        ),
        grid=(steps,),
        in_specs=[
            pl.BlockSpec(memory_space=pltpu.SMEM),
            lanes, tile, tile, once((d, d)), once((d, units)), once((units, d)), once((8, d)), once((8, units)),
        ],
        out_specs=(
            tile, tile, lanes, once3((n, 16, units // n)), once((units, d)),
            once4(halves), once4(halves), once((d, d)),
        ),
        scratch_shapes=[
            pltpu.VMEM((8, d), f32),
            pltpu.VMEM((8, units), f32),
            pltpu.VMEM((rows, units), bf16),
            pltpu.VMEM((rows, units), bf16),
            pltpu.VMEM((rows, d), bf16),
            pltpu.VMEM((rows, d), bf16),
            pltpu.VMEM((rows, d), bf16),
            pltpu.VMEM((d, rows), bf16),
            pltpu.VMEM((block, units), keep),
            pltpu.VMEM((block, units), keep),
        ],
        compiler_params=pltpu.CompilerParams(vmem_limit_bytes=60 * 2**20),
        cost_estimate=pl.CostEstimate(
            flops=rows * d * (12 * units + 6 * d),
            bytes_accessed=4 * d * (4 * units + 2 * d) + 12 * rows * d,
            transcendentals=2 * rows * units,
        ),
        name="feed_forward",
    )(place, ctx_t, tokens, cotangent, wo, we, wc, wide, unit)


def local(
    tokens,
    output_cotangent,
    attention_weight,
    query_bias,
    value_bias,
    output_weight,
    output_bias,
    first_gain,
    first_shift,
    expand_weight,
    expand_bias,
    contract_weight,
    contract_bias,
    second_gain,
    second_shift,
    head_gate,
    hidden_gate,
    unit_gate,
    head_mask,
    hidden_mask,
    unit_mask,
    attention_mask,
    feedforward_mask,
    continuation_lengths,
):
    row_count = tokens.shape[0]
    seq_count = lax.axis_size("seq")
    head_count = head_gate.shape[0]
    model_width = hidden_gate.shape[0]
    head_size = model_width // head_count
    local_heads = head_count // seq_count
    seq_index = lax.axis_index("seq")
    wt_index = lax.axis_index("wt")
    local_width = 3 * head_size * local_heads
    wt_count = lax.axis_size("wt")
    own_columns = lax.dynamic_slice_in_dim(attention_weight, seq_index * local_width, local_width, 1)
    tokens_all, own_weight, full_output = gather_in(wt_count, tokens, own_columns, output_weight)
    own_weight = own_weight.reshape(model_width, local_width)
    full_output = full_output.reshape(model_width, model_width)
    full_expand = lax.all_gather(expand_weight, "wt", axis=0, tiled=True)
    full_contract = lax.all_gather(contract_weight, "wt", axis=0, tiled=True)
    full_attention = lax.all_gather(attention_weight, "wt", axis=0, tiled=True)
    first_group = wt_index * GRP_WT
    own_attention = lax.dynamic_slice_in_dim(attention_mask, first_group, GRP_WT, 0).astype(
        jnp.float32
    )
    own_feedforward = lax.dynamic_slice_in_dim(feedforward_mask, first_group, GRP_WT, 0).astype(
        jnp.float32
    )
    head_scale = head_mask.astype(jnp.float32) * head_gate
    hidden_scale = hidden_mask.astype(jnp.float32) * hidden_gate
    unit_scale = unit_mask.astype(jnp.float32) * unit_gate
    wide_table = jnp.stack(
        [
            output_bias.astype(f32),
            first_gain.astype(f32),
            first_shift.astype(f32),
            hidden_scale,
            contract_bias.astype(f32),
            second_gain.astype(f32),
            second_shift.astype(f32),
            hidden_mask.astype(f32),
        ],
        axis=0,
    )
    unit_row = unit_scale * own_feedforward[0]
    unit_kept = unit_mask.astype(f32) * own_feedforward[0]
    unit_table = jnp.stack([expand_bias.astype(f32), unit_row] + [unit_kept] * 6, axis=0)
    bias_table = jnp.stack(
        [
            query_bias.astype(jnp.float32).reshape(head_count, head_size),
            jnp.zeros((head_count, head_size), jnp.float32),
            value_bias.astype(jnp.float32).reshape(head_count, head_size),
        ],
        axis=1,
    )
    own_scale = lax.dynamic_slice_in_dim(head_scale, seq_index * local_heads, local_heads, 0)
    own_scale = own_scale * own_attention[0]
    own_mask = lax.dynamic_slice_in_dim(head_mask, seq_index * local_heads, local_heads, 0)
    own_gate = lax.dynamic_slice_in_dim(head_gate, seq_index * local_heads, local_heads, 0)
    own_bias = lax.dynamic_slice_in_dim(bias_table, seq_index * local_heads, local_heads, 0)
    constant = jnp.ones((local_heads, head_size), jnp.float32)
    factor = jnp.stack([constant, constant, constant * own_scale[:, None]], axis=1)
    vec = jnp.stack([own_bias.reshape(local_width), factor.reshape(local_width)], axis=0)
    lens = lax.dynamic_slice_in_dim(continuation_lengths, first_group, GRP_WT, 0)[0]
    place = jnp.stack([seq_index, lens[0], lax.rem(wt_index, 2), wt_index])
    packed, own_context, log_sums, context_t = attend(lens, tokens_all, own_weight, vec, local_heads)
    (
        layer_output,
        grad_total_one,
        grad_context_t,
        vec_sums,
        contract_weight_grad,
        exp_mine,
        exp_mate,
        output_weight_grad,
    ) = feed_forward(
        wt_count, place, context_t, tokens, output_cotangent, full_output, full_expand, full_contract, wide_table, unit_table
    )
    con_piece = lax.psum_scatter(contract_weight_grad, "wt", scatter_dimension=0, tiled=True)
    output_weight_grad, con_piece = lax.optimization_barrier((output_weight_grad, con_piece))
    out_piece = lax.psum_scatter(output_weight_grad, "wt", scatter_dimension=0, tiled=True)
    pieces, projection_grad, exp_part, late_sums = attend_back(
        wt_count,
        lens,
        packed,
        own_context,
        grad_context_t,
        log_sums,
        factor[:, 2:3, :],
        tokens_all,
        exp_mine,
        exp_mate,
    )
    own_wide = model_width // wt_count
    tokens_grad, con_all, out_all, exp_all, att_all, vec_all, late_all = final(
        wt_count,
        grad_total_one,
        pieces,
        full_attention,
        con_piece.reshape(seq_count, own_wide, model_width),
        out_piece,
        projection_grad,
        exp_part,
        vec_sums,
        late_sums,
    )
    head_row = (head_mask.astype(f32) / head_gate).reshape(1, head_count)
    con_sum, out_sum, exp_sum, att_sum, *rows = finish(
        wt_count, local_heads, place, head_row, con_all, out_all, exp_all, att_all, vec_all, late_all
    )
    wide = [row.reshape(own_wide) for row in rows[:7]]
    units = [row.reshape(-1) for row in rows[7:9]]
    return (
        layer_output,
        tokens_grad,
        att_sum,
        rows[9].reshape(own_wide),
        rows[10].reshape(own_wide),
        out_sum,
        wide[S_OUT_BIAS],
        wide[S_GAIN1],
        wide[S_SHIFT1],
        exp_sum,
        units[0],
        con_sum.reshape(seq_count * own_wide, model_width),
        wide[S_CON_BIAS],
        wide[S_GAIN2],
        wide[S_SHIFT2],
        rows[11].reshape(head_count),
        wide[S_HIDDEN],
        units[1],
    )


def solution(mesh):
    return jax.shard_map(
        local,
        mesh=mesh,
        in_specs=(
            P(("wt", "seq"), None),
            P(("wt", "seq"), None),
            P("wt", None),
            P(),
            P(),
            P("wt", None),
            P(),
            P(),
            P(),
            P("wt", None),
            P(),
            P("wt", None),
            P(),
            P(),
            P(),
            P(),
            P(),
            P(),
            P(),
            P(),
            P(),
            P(),
            P(),
            P(),
        ),
        out_specs=(
            P(("wt", "seq"), None),
            P(("wt", "seq"), None),
            P("wt", None),
            P("wt"),
            P("wt"),
            P("wt", None),
            P("wt"),
            P("wt"),
            P("wt"),
            P("wt", None),
            P("wt"),
            P("wt", None),
            P("wt"),
            P("wt"),
            P("wt"),
            P(),
            P("wt"),
            P("wt"),
        ),
        check_vma=False,
    )
```

time: 405 us -> 414 us (1.022)
  waiting for transfers between devices: 19.8 us -> 72.3 us
  Pallas kernels: 334 us -> 299 us
  matrix products: 6.6 us -> 0 us
  local copies, waits for them, and re-layouts: 25.4 us -> 20.7 us
    reduce_scatter x1, waiting for transfers between devices: 0.01 us -> 53.3 us  [local(): lax.psum_scatter(contract_weight_grad, 'wt', scatter_dimension=0, tiled=T...]
    pallas_call x6 -> x3, Pallas kernels: 191 us -> 147 us  [the longest x1 95.7 us: attend_back(): pl.pallas_call(functools.partial(attend_back_kernel, heads, n), out_shape...]
    pallas_call x1, Pallas kernels: 40.8 us -> 48 us  [attend(): pl.pallas_call(functools.partial(attend_kernel, heads), out_shape=(jax.Sh...]
    dot_general x1 -> x0, matrix products: 6.6 us -> none  [local(): jnp.einsum('td,tc->dc', tokens_all, grad_packed, preferred_element_type=j...]
    slice x8 -> x1, local copies, waits for them, and re-layouts: 6.81 us -> 0.51 us  [local(): place = jnp.stack([seq_index, lens[0], lax.rem(wt_index, 2), wt_index])]
    unnamed x50 -> x23, local copies, waits for them, and re-layouts: 8.72 us -> 7.29 us
  transfers between devices with their start and end apart: 6 -> 5, of which waited for: 1 -> 2; matrix products, arithmetic and copies ran while one was open for 5% -> 4% of each run, Pallas kernels for 71% -> 46%
where the time goes in v5:
time: 414 us
  Pallas kernels  299 us (72%)
  waiting for transfers between devices  72.3 us (17%)
  local copies, waits for them, and re-layouts  20.7 us (5%)
  between operations  15.7 us (4%)
  other arithmetic  5.97 us (1%)
    pallas_call x1, Pallas kernels, attend_back(): pl.pallas_call(functools.partial(attend_back_kernel, heads, n), out_shape...  95.7 us
    pallas_call x1, Pallas kernels, feed_forward(): pl.pallas_call(functools.partial(feed_forward_kernel, steps, chunk), out_...  58.8 us
    reduce_scatter x1, waiting for transfers between devices, local(): lax.psum_scatter(contract_weight_grad, 'wt', scatter_dimension=0, tiled=T...  53.3 us
    pallas_call x1, Pallas kernels, final(): pl.pallas_call(functools.partial(final_kernel, heads, n), out_shape=(jax....  48.2 us
    pallas_call x1, Pallas kernels, attend(): pl.pallas_call(functools.partial(attend_kernel, heads), out_shape=(jax.Sh...  48 us
    pallas_call x1, Pallas kernels, gather_in(): pl.pallas_call(functools.partial(gather_kernel, n), out_shape=(jax.ShapeD...  45.7 us
    all_gather x1, waiting for transfers between devices, local(): full_contract = lax.all_gather(contract_weight, 'wt', axis=0, tiled=True)  17 us
  transfers between devices with their start and end apart: 5, of which 2 were waited for; matrix products, arithmetic and copies ran while one was open for 4% of the time, Pallas kernels for 46%

profile of v5, /device:TPU:0, one launch (start us, length us, event | category | flops | bytes accessed | tf_op | source)
XLA Modules:
  0.0 414.2 jit_solution(15021186930406413491)
XLA Ops:
  7.3 0.7 all-gather.4.cloned.1.call-update
  8.0 0.7 all-gather.6.cloned.1.call-update
  8.7 1.2 dynamic_slice.22
  10.6 0.7 fusion.2
  11.3 0.1 dynamic-slice_multiply_fusion
  11.4 0.1 stack.95.scale_ref
  11.5 0.1 stack_reshape.23
  11.6 0.8 reshape.110
  12.3 0.8 reshape.111
  13.1 0.1 pad.4.clone
  13.2 0.1 fusion.1
  13.3 0.1 stack_reshape.22
  13.3 1.4 fusion.3
  14.7 0.5 slice.6
  15.2 1.2 dynamic_slice.23
  17.1 0.7 stack.124
  17.8 0.7 convert_element_type.12
  18.5 0.7 convert_multiply_fusion.2
  19.2 0.7 reshape.112
  19.9 0.7 reshape.113
  20.6 0.7 reshape.114
  21.3 0.7 reshape.115
  22.0 0.7 reshape.116
  22.7 0.7 reshape.117
  23.3 1.7 constant_dynamic-slice_fusion.cols_ref
  25.0 45.7 %gather_in.1 = (bf16[3072,768]{1,0:T(8,128)(2,1)}, bf16[8,96,576]{2,1,0:T(8,128)(2,1)}, bf16[8,96,768]{2,1,0:T(8,128)(2,1)}) custom-call(bf16[768,768]{1,0:T(8,128)(2,1)} %tok_ref.3, bf16[96,576]{1,0:T(8,128)(2,1)} %constant_dynamic-slice_fusion.cols_ref, bf16[96,768]{1,0:T(8,128)(2,1)} %out_ref.1), custom_call_target="tpu_custom_call" | custom-call | tf_op jit(solution)/shard_map/gather_in/pallas_call | solution.py:545
  70.7 0.8 stack.117.unit_ref
  71.5 0.6 stack.112.wide_ref
  72.1 1.2 pad_add_fusion.place_ref
  73.4 0.6 pad_maximum_fusion.vec_ref
  74.0 48.0 %attend.1 = (bf16[3,3072,192]{2,1,0:T(8,128)(2,1)}, bf16[192,3072]{1,0:T(8,128)(2,1)}, f32[3,1,3072]{2,1,0:T(1,128)}, bf16[768,768]{1,0:T(8,128)(2,1)}) custom-call(s32[2]{0:T(128)} %get-tuple-element.106.lens_ref, bf16[6,512,768]{2,1,0:T(8,128)(2,1)} %bitcast.36, bf16[768,576]{1,0:T(8,128)(2,1)} %bitcast.39, f32[2,576]{1,0:T(2,128)} %pad_maximum_fusion.vec_ref), custom_call_target="tpu_custom_call" | custom-call | flops 20434649088 | bytes 8257536 | tf_op jit(solution)/shard_map/attend/pallas_call | solution.py:160
  122.0 17.0 %all-gather.6.cloned.1.call-done.wc_ref = bf16[3072,768]{1,0:T(8,128)(2,1)} async-done(((bf16[384,768]{1,0:T(8,128)(2,1)}), bf16[3072,768]{1,0:T(8,128)(2,1)}) %all-gather.6.cloned.1.call-update) | async-done | bytes 4718608 | tf_op jit(solution)/shard_map/all_gather | solution.py:1002
  139.0 58.8 %feed_forward.1 = (bf16[768,768]{1,0:T(8,128)(2,1)}, f32[768,768]{1,0:T(8,128)}, bf16[768,768]{1,0:T(8,128)(2,1)}, f32[8,16,384]{2,1,0:T(8,128)}, bf16[3072,768]...) custom-call(s32[4]{0:T(128)} %pad_add_fusion.place_ref, ...), custom_call_target="tpu_custom_call" | custom-call | flops 24461180928 | bytes 49545216 | tf_op jit(solution)/shard_map/feed_forward/pallas_call | solution.py:918
  197.9 0.0 all-gather.8.cloned.1.call-start
  197.9 0.5 all-gather.8.cloned.1.call-update
  198.5 53.3 %reduce-scatter.3.cloned.1.call-done = bf16[384,768]{1,0:T(8,128)(2,1)} async-done(((bf16[3072,768]{1,0:T(8,128)(2,1)}), bf16[384,768]{1,0:T(8,128)(2,1)}) %reduce-scatter.3.cloned.1.call-update) | async-done | bytes 589840 | tf_op jit(solution)/shard_map/reduce_scatter | solution.py:1061
  251.8 95.7 %attend_back.1 = (bf16[3,4,768,192]{3,2,1,0:T(8,128)(2,1)}, bf16[8,96,576]{2,1,0:T(8,128)(2,1)}, bf16[4,96,768]{2,1,0:T(8,128)(2,1)}, f32[8,192]{1,0:T(8,128)}) custom-call(s32[2]{0:T(128)} %get-tuple-element.106.lens_ref, bf16[3,3072,192]{2,1,0:T(8,128)(2,1)} %get-tuple-element.68.packed_hbm, bf16[192,3072]{1,0:T(8,128)(2,1)} %get-tuple-element.69.ctx_ref, ...), custom_call_target="tpu_custom_call" | custom-call | flops 47009759232 | bytes 15335424 | tf_op jit(solution)/shard_map/attend_back/pallas_call | solution.py:398
  347.6 48.2 %final.1 = (f32[768,768]{1,0:T(8,128)}, bf16[4,96,768]{2,1,0:T(8,128)(2,1)}, bf16[4,96,768]{2,1,0:T(8,128)(2,1)}, bf16[4,96,768]{2,1,0:T(8,128)(2,1)}, bf16[4,96...) custom-call(f32[768,768]{1,0:T(8,128)} %get-tuple-element.67.base_hbm, ...), custom_call_target="tpu_custom_call" | custom-call | flops 2717908992 | bytes 3538944 | tf_op jit(solution)/shard_map/final/pallas_call | solution.py:670
  395.9 1.1 copy-done
  397.0 1.1 copy-done.1
  398.0 1.1 copy-done.2
  399.1 1.0 copy-done.3
  400.1 0.9 copy-done.4
  401.0 0.8 copy-done.5
  401.8 2.8 finish.1
  404.6 0.6 reduce.1
  405.2 0.6 reduce.2
  405.8 1.4 copy.43
  (29 shorter events, 0.3 us)
Async XLA Ops:
  7.2 63.5 %copy-start.9 = (f32[3072]{0:T(1024)S(1)}, f32[3072]{0:T(1024)}, u32[]{:S(2)}) copy-start(f32[3072]{0:T(1024)} %param.41) | copy-start | bytes 36868
  7.2 63.5 %copy-start.8 = (s32[3072]{0:T(1024)S(1)}, s32[3072]{0:T(1024)}, u32[]{:S(2)}) copy-start(s32[3072]{0:T(1024)} %param.44) | copy-start | bytes 36868
  7.2 114.8 %all-gather.4.cloned.1.call-start = ((), (), s32[]{:S(2)}) async-start(), calls=%async_computation.2 | async-start | bytes 5308416 | tf_op jit(solution)/shard_map/all_gather | solution.py:1001
  7.9 131.0 %all-gather.6.cloned.1.call-start = ((), (), s32[]{:S(2)}) async-start(), calls=%async_computation.3 | async-start | bytes 5308416 | tf_op jit(solution)/shard_map/all_gather | solution.py:1002
  8.7 243.1 %reduce-scatter.3.cloned.1.call-start = ((), (), s32[]{:S(2)}) async-start(), calls=%async_computation.5 | async-start | bytes 5308416 | tf_op jit(solution)/shard_map/reduce_scatter | solution.py:1061
  11.5 110.5 %copy-start.10 = (f32[3,1,64]{2,1,0:T(1,128)}, f32[3,1,64]{2,1,0:T(1,128)S(1)}, u32[]{:S(2)}) copy-start(f32[3,1,64]{2,1,0:T(1,128)S(1)} %stack.95.scale_ref) | copy-start | bytes 2308
  197.9 149.7 %all-gather.8.cloned.1.call-start = ((), (), s32[]{:S(2)}) async-start(), calls=%async_computation.4 | async-start | bytes 3981312 | tf_op jit(solution)/shard_map/all_gather | solution.py:1003
  198.4 149.2 %reduce-scatter.5.cloned.1.call-start = ((), (), s32[]{:S(2)}) async-start(), calls=%async_computation.6 | async-start | bytes 1327104 | tf_op jit(solution)/shard_map/reduce_scatter | solution.py:1063
  347.6 48.3 %copy-start.6 = (s32[4]{0:T(128)S(1)}, s32[4]{0:T(128)}, u32[]{:S(2)}) copy-start(s32[4]{0:T(128)} %pad_add_fusion.place_ref) | copy-start | bytes 52
  395.9 1.1 copy-start
  397.0 1.1 copy-start.1
  398.0 1.1 copy-start.2
  399.1 1.0 copy-start.3
  400.1 0.9 copy-start.4
  401.0 0.8 copy-start.5
  401.8 4.0 copy-start.7
Sparse Core Ops, SparseCore 0:
  9.7 77.1 all-gather.3
  88.5 50.3 all-gather.5
  198.0 53.7 reduce-scatter.2
  253.3 39.8 all-gather.7
  295.9 31.7 reduce-scatter.4
